TPU v7x, 32 devices: a whole 2x2x4 slice. The times are simulated.
32 devices in a mesh: line: 4 (over y, core), block: 8 (over z, x).
Axes of the slice: x: 2, y: 2, z: 4, core: 2. Of those that a mesh axis runs over, the one named last changes fastest.
Arguments:
- residual: float32 [6, 32, 15, 1024], P(None, 'line', None, 'block'), may hold values from -6 to 6
- adjoint: float32 [6, 32, 15, 1024], P(None, 'line', None, 'block'), may hold values from -6 to 6
- i_factors: float32 [8, 2, 6, 32, 8], P('block', None, None, 'line'), as said below
- k_factors: float32 [4, 2, 6, 1024, 128], P('line', None, None, 'block'), as said below
- couplings: float32 [4, 8, 4, 3, 6], P('line', 'block')
- receptor_cell: int32 [4, 8, 8, 2048], P('line', 'block'), may hold values from 0 to 15359
- send_count: int32 [4, 8, 8], P('line', 'block'), may hold values from 512 to 2048, as said below
- donor_cell: int32 [4, 8, 8, 2048], P('line', 'block'), may hold values from 0 to 13310, as said below
- donor_weight: float32 [4, 8, 3, 8, 2048], P('line', 'block'), may hold values from 0 to 1
Outputs:
- update: float32 [6, 32, 15, 1024], P(None, 'line', None, 'block')
Inputs may be any that keep to these rules, and one draw needn't show every extreme that they name: The first send_count slots of each device for each donor owner are live. In each group along block one donor owner receives exactly 2048 live slots from every source device of the group; every other owner receives at most 1280 live slots from each source, and some source sends exactly that many to some owner. `donor_cell`: numbered within the owner's block; its base cell has i < 7, j < 14 and k < 127 in the block, so that all eight donor cells lie in the block. `receptor_cell`: numbered within the sending device's block; entries of slots that are not live are arbitrary. `i_factors`: each segment matrix is lower triangular with a diagonal between 0.8 and 1.2. `k_factors`: each segment matrix is lower triangular with a diagonal between 0.8 and 1.2.
All inputs are finite; a program needn't handle non-finite values.
Results may differ from a plain program's by a relative error of at most 0.00022.
Values sent between devices are 32-bit elements; how exact they have to be, the bound alone decides.
No kernel may reach another device: no remote copies, remote signals or barrier semaphores. Data moves between devices by JAX's collectives and lax.ppermute only.
A program may use at most 320 MiB of HBM per device.

v0:
```python
import jax
import jax.numpy as jnp
from jax import lax
from jax.sharding import PartitionSpec as P


def carried_in(array, axis, combine, identity, reverse):
    peers, index = (lax.axis_size(axis), lax.axis_index(axis))
    everything = jax.tree.map(lambda part: lax.all_gather(part, axis), array)
    start = jax.tree.map(
        lambda part, zero: jnp.broadcast_to(jnp.asarray(zero, part.dtype), part.shape),
        array,
        identity,
    )

    def step(k, before):
        at = peers - 1 - k if reverse else k
        reached = at > index if reverse else at < index
        new = combine(before, jax.tree.map(lambda part: part[at], everything))
        return jax.tree.map(lambda a, b: jnp.where(reached, a, b), new, before)

    return lax.fori_loop(0, peers, step, start)


def coupling_matrix(triple):
    zeros_part = jnp.zeros_like(triple[0])
    upper_row = jnp.stack([triple[0], triple[1]], axis=-1)
    lower_row = jnp.stack([triple[2], zeros_part], axis=-1)
    return jnp.stack([upper_row, lower_row], axis=-2)


def compose(earlier, later):
    first_map, first_vec = earlier
    next_map, next_vec = later
    joined_map = jnp.einsum("fab,fbc->fac", next_map, first_map, precision=lax.Precision.HIGHEST)
    joined_vec = (
        jnp.einsum("fab,fbl->fal", next_map, first_vec, precision=lax.Precision.HIGHEST) + next_vec
    )
    return (joined_map, joined_vec)


def unit_pair(transfer, end_state):
    return (
        jnp.broadcast_to(jnp.eye(2, dtype=jnp.float32), transfer.shape),
        jnp.zeros_like(end_state),
    )


def line_state(transfer, end_state, upward):
    identity = unit_pair(transfer, end_state)
    if upward:
        return carried_in((transfer, end_state), "line", compose, identity, True)[1]
    return carried_in((transfer, end_state), "line", compose, identity, False)[1]


def block_state(transfer, end_state, upward):
    identity = unit_pair(transfer, end_state)
    if upward:
        return carried_in((transfer, end_state), "block", compose, identity, True)[1]
    return carried_in((transfer, end_state), "block", compose, identity, False)[1]


def segment_solve(columns, factor, coupling, last_axis):
    if last_axis:
        homogeneous = jnp.einsum("fpq,flq->flp", factor, columns, precision=lax.Precision.HIGHEST)
        end_state = jnp.stack([homogeneous[:, :, -1], homogeneous[:, :, -2]], axis=1)
    else:
        homogeneous = jnp.einsum("fpq,fql->fpl", factor, columns, precision=lax.Precision.HIGHEST)
        end_state = jnp.stack([homogeneous[:, -1], homogeneous[:, -2]], axis=1)
    influence = jnp.einsum(
        "fpa,fab->fpb", factor[:, :, 0:2], coupling, precision=lax.Precision.HIGHEST
    )
    transfer = -jnp.stack([influence[:, -1], influence[:, -2]], axis=1)
    return (homogeneous, influence, end_state, transfer)


def sweep_i(grid_field, i_factors, couplings):
    fields, cells_i = (grid_field.shape[0], grid_field.shape[1])
    columns = grid_field.reshape(fields, cells_i, -1)
    for upward in (False, True):
        direction = 1 if upward else 0
        oriented = jnp.flip(columns, 1) if upward else columns
        homogeneous, influence, end_state, transfer = segment_solve(
            oriented, i_factors[0, direction], coupling_matrix(couplings[0, 0, direction]), False
        )
        incoming = line_state(transfer, end_state, upward)
        solved = homogeneous - jnp.einsum(
            "fpa,fal->fpl", influence, incoming, precision=lax.Precision.HIGHEST
        )
        columns = jnp.flip(solved, 1) if upward else solved
    return columns.reshape(grid_field.shape)


def sweep_k(grid_field, k_factors, couplings):
    fields, cells_k = (grid_field.shape[0], grid_field.shape[3])
    columns = grid_field.reshape(fields, -1, cells_k)
    for upward in (False, True):
        direction = 3 if upward else 2
        oriented = jnp.flip(columns, 2) if upward else columns
        homogeneous, influence, end_state, transfer = segment_solve(
            oriented, k_factors[0, direction - 2], coupling_matrix(couplings[0, 0, direction]), True
        )
        incoming = block_state(transfer, end_state, upward)
        solved = homogeneous - jnp.einsum(
            "fpa,fal->flp", influence, incoming, precision=lax.Precision.HIGHEST
        )
        columns = jnp.flip(solved, 2) if upward else solved
    return columns.reshape(grid_field.shape)


def spread_donors(right_side, incoming, donor_cell, donor_weight, cells_j, cells_k):
    fields = right_side.shape[0]
    base_cell = donor_cell.reshape(-1)
    fractions = donor_weight.reshape(3, -1)
    values = incoming.reshape(fields, -1)
    index_list = []
    weight_list = []
    for corner in range(8):
        step_i = corner // 4
        step_j = corner // 2 % 2
        step_k = corner % 2
        along_i = fractions[0] if step_i else 1.0 - fractions[0]
        along_j = fractions[1] if step_j else 1.0 - fractions[1]
        along_k = fractions[2] if step_k else 1.0 - fractions[2]
        weight_list.append(along_i * along_j * along_k)
        index_list.append(base_cell + step_i * cells_j * cells_k + step_j * cells_k + step_k)
    targets = jnp.concatenate(index_list)
    weights = jnp.concatenate(weight_list)
    spread = jnp.tile(values, (1, 8)) * weights[None, :]
    return right_side.at[:, targets].add(spread)


def per_device(
    residual,
    adjoint,
    i_factors,
    k_factors,
    couplings,
    receptor_cell,
    send_count,
    donor_cell,
    donor_weight,
):
    fields, cells_i, cells_j, cells_k = adjoint.shape
    owners, capacity = (receptor_cell.shape[2], receptor_cell.shape[3])
    flat_adjoint = adjoint.reshape(fields, -1)
    receptor_index = receptor_cell.reshape(-1)
    outgoing = jnp.take(flat_adjoint, receptor_index, axis=1).reshape(fields, owners, capacity)
    counts = send_count.reshape(owners)
    active_slot = jnp.arange(capacity, dtype=jnp.int32)[None, :] < counts[:, None]
    outgoing = jnp.where(active_slot[None], outgoing, 0.0)
    incoming = lax.all_to_all(outgoing, "block", split_axis=1, concat_axis=1, tiled=True)
    combined = spread_donors(
        residual.reshape(fields, -1),
        incoming,
        donor_cell[0, 0],
        donor_weight[0, 0],
        cells_j,
        cells_k,
    )
    right_side = combined.reshape(residual.shape)
    after_i = sweep_i(right_side, i_factors, couplings)
    return sweep_k(after_i, k_factors, couplings)


def solution(mesh):
    return jax.shard_map(
        per_device,
        mesh=mesh,
        in_specs=(
            P(None, "line", None, "block"),
            P(None, "line", None, "block"),
            P("block", None, None, "line", None),
            P("line", None, None, "block", None),
            P("line", "block", None, None, None),
            P("line", "block", None, None),
            P("line", "block", None),
            P("line", "block", None, None),
            P("line", "block", None, None, None),
        ),
        out_specs=P(None, "line", None, "block"),
        check_vma=False,
    )
```

profile of v0, /device:TPU:0, one launch (start us, length us, event | category | flops | bytes accessed | tf_op | source)
XLA Modules:
  0.0 1004.7 jit_solution(11574020361360782889)
XLA Ops:
  0.0 0.9 copy.165
  0.9 0.9 iota_compare_fusion
  1.9 5.4 copy.132
  7.4 57.7 %gather_fusion = f32[16384,6]{1,0:T(8,128)} fusion(f32[6,15360]{0,1:T(8,128)} %bitcast.205, s32[16384]{0:T(1024)S(1)} %broadcast_clamp_fusion), kind=kCustom, calls=%fused_computation | custom fusion | bytes 851968 | tf_op jit(solution)/shard_map/jit(_take)/gather | solution.py:148
  65.0 5.3 copy.133
  70.3 0.9 select_select_fusion
  71.3 7.3 all-to-all-start
  80.2 4.6 copy.131
  85.4 5.2 all_gather.40
  91.2 5.2 all_gather.43
  96.5 0.7 fusion.24
  97.5 26.7 %all_gather.46 = f32[8,6,2,2]{1,3,2,0:T(2,128)S(1)} all-gather(f32[1,6,2,2]{1,3,2,0:T(2,128)S(1)} %maximum_negate_fusion.2), channel_id=1, replica_groups=mesh['line'=4,'block'=8] {'block'}, dimensions={0}, use_global_device_ids=true | all-gather | bytes 864 | tf_op jit(solution)/shard_map/all_gather | solution.py:9
  124.3 0.7 fusion.22
  125.3 26.1 %all_gather.49 = f32[8,6,2,2]{1,3,2,0:T(2,128)S(1)} all-gather(f32[1,6,2,2]{1,3,2,0:T(2,128)S(1)} %maximum_negate_fusion.3), channel_id=1, replica_groups=mesh['line'=4,'block'=8] {'block'}, dimensions={0}, use_global_device_ids=true | all-gather | bytes 864 | tf_op jit(solution)/shard_map/all_gather | solution.py:9
  151.5 5.3 copy.134
  156.8 44.1 %bitcast_multiply_fusion = f32[6,131072]{0,1:T(8,128)} fusion(f32[131072]{0:T(1024)S(1)} %multiply_dynamic-update-slice_fusion, f32[6,16384]{0,1:T(8,128)} %copy.134), kind=kLoop, calls=%fused_computation.32 | loop fusion | flops 786432 | bytes 4063232 | tf_op jit(solution)/shard_map/mul | solution.py:129
  200.9 704.8 %scatter_custom_fusion = f32[6,15360]{0,1:T(8,128)} fusion(f32[6,15360]{0,1:T(8,128)} %bitcast.203, s32[131072]{0:T(1024)S(1)} %bitcast.232, f32[6,131072]{0,1:T(8,128)} %bitcast_multiply_fusion), kind=kCustom, calls=%fused_computation.30 | custom fusion | flops 786432 | bytes 67477504 | tf_op jit(solution)/shard_map/scatter-add | solution.py:130
  905.8 5.0 copy.135
  911.4 6.4 all-gather
  917.8 2.5 while.60
  920.3 0.6 convolution_subtract_fusion.1
  921.8 6.6 all-gather.1
  928.4 2.5 while.61
  931.8 0.8 fusion.30
  933.2 30.8 %all-gather.2 = f32[48,2,120]{2,1,0:T(2,128)S(1)} all-gather(f32[6,2,120]{2,1,0:T(2,128)S(1)} %pad_maximum_fusion.2), channel_id=4, replica_groups=mesh['line'=4,'block'=8] {'block'}, dimensions={0}, use_global_device_ids=true | all-gather | bytes 51840 | tf_op jit(solution)/shard_map/all_gather | solution.py:9
  963.9 2.5 while.62
  966.4 0.8 convolution_subtract_fusion.3
  967.8 0.8 fusion.31
  969.1 30.8 %all-gather.3 = f32[48,2,120]{2,1,0:T(2,128)S(1)} all-gather(f32[6,2,120]{2,1,0:T(2,128)S(1)} %pad_maximum_fusion.3), channel_id=5, replica_groups=mesh['line'=4,'block'=8] {'block'}, dimensions={0}, use_global_device_ids=true | all-gather | bytes 51840 | tf_op jit(solution)/shard_map/all_gather | solution.py:9
  999.9 2.5 while.63
  1002.4 0.8 convolution_subtract_fusion.2
  1003.9 0.9 copy.152
  (199 shorter events, 17.4 us)
Async XLA Ops:
  7.3 71.3 %copy-start.2 = (s32[1,1,8,2048]{3,2,1,0:T(8,128)S(1)}, s32[1,1,8,2048]{3,2,1,0:T(8,128)}, u32[]{:S(2)}) copy-start(s32[1,1,8,2048]{3,2,1,0:T(8,128)} %param.24) | copy-start | bytes 196612
  7.3 71.4 %copy-start.4 = (f32[1,1,3,8,2048]{4,3,2,1,0:T(8,128)S(1)}, f32[1,1,3,8,2048]{4,3,2,1,0:T(8,128)}, u32[]{:S(2)}) copy-start(f32[1,1,3,8,2048]{4,3,2,1,0:T(8,128)} %param.25) | copy-start | bytes 589828
  65.0 15.1 %copy-start.1 = (f32[6,8,15,128]{3,1,2,0:T(8,128)S(1)}, f32[6,8,15,128]{3,1,2,0:T(8,128)}, u32[]{:S(2)}) copy-start(f32[6,8,15,128]{3,1,2,0:T(8,128)} %param.17) | copy-start | bytes 1105924
  70.3 14.5 %copy-start.5 = (f32[1,1,4,3,6]{4,2,3,1,0:T(4,128)S(1)}, f32[1,1,4,3,6]{4,2,3,1,0:T(4,128)}, u32[]{:S(2)}) copy-start(f32[1,1,4,3,6]{4,2,3,1,0:T(4,128)} %param.21) | copy-start | bytes 868
  70.3 14.6 %copy-start.3 = (f32[1,2,6,8,8]{4,3,2,1,0:T(8,128)S(1)}, f32[1,2,6,8,8]{4,3,2,1,0:T(8,128)}, u32[]{:S(2)}) copy-start(f32[1,2,6,8,8]{4,3,2,1,0:T(8,128)} %param.19) | copy-start | bytes 9220
  70.3 26.1 %copy-start = (f32[1,2,6,128,128]{4,3,2,1,0:T(8,128)S(1)}, f32[1,2,6,128,128]{4,3,2,1,0:T(8,128)}, u32[]{:S(2)}) copy-start(f32[1,2,6,128,128]{4,3,2,1,0:T(8,128)} %param.20) | copy-start | bytes 2359300
  71.3 80.2 %all-to-all-start = ((f32[6,8,2048]{2,0,1:T(8,128)}), f32[6,8,2048]{2,0,1:T(8,128)S(1)}, u32[]{:S(2)}, u32[]{:S(2)}) async-start(f32[6,8,2048]{2,0,1:T(8,128)} %select_select_fusion), calls=%async_computation | async-start | bytes 1048576 | tf_op jit(solution)/shard_map/all_to_all | solution.py:152
where the time goes:
time: 1010 us; the launch traced here: 1000 us
  other arithmetic  752 us (74%)
  blocking collectives  138 us (14%)
  local copies, waits for them, and re-layouts  92.9 us (9%)
  matrix products  13.6 us (1%)
    scatter-add x1, other arithmetic, spread_donors(): return right_side.at[:, targets].add(spread)  705 us
    all_gather x8, blocking collectives, carried_in(): everything = jax.tree.map(lambda part: lax.all_gather(part, axis), array)  138 us
    gather x2, local copies, waits for them, and re-layouts, per_device(): jnp.take(flat_adjoint, receptor_index, axis=1)  62.9 us
    mul x1, other arithmetic, spread_donors(): spread = jnp.tile(values, (1, 8)) * weights[None, :]  44.1 us
  transfers between devices with their start and end apart: 1, of which 0 were waited for; matrix products, arithmetic and copies ran while one was open for 1% of the time, Pallas kernels for 0%

commit v1 on v0

v1 whole, which is shorter than its diff:
```python
import functools

import jax
import jax.numpy as jnp
from jax import lax
from jax.experimental import pallas as pl
from jax.experimental.pallas import tpu as pltpu
from jax.sharding import PartitionSpec as P

LANES = 128
HIGHEST = lax.Precision.HIGHEST
F32 = jnp.float32
BF16 = jnp.bfloat16


def split(x):
    high = x.astype(BF16)
    return high, (x - high.astype(F32)).astype(BF16)


def dot_nt(a, b, precision=None):
    return lax.dot_general(
        a, b, (((1,), (1,)), ((), ())), precision=precision, preferred_element_type=F32
    )


def dot_nn(a, b, precision=None):
    return lax.dot_general(
        a, b, (((1,), (0,)), ((), ())), precision=precision, preferred_element_type=F32
    )


def dot_tn(a, b, precision=None):
    return lax.dot_general(
        a, b, (((0,), (0,)), ((), ())), precision=precision, preferred_element_type=F32
    )


def split_cell(cell, cells_i, cells_j):
    row = lax.shift_right_logical(cell, 7)
    k = lax.bitwise_and(cell, LANES - 1)
    i = jnp.zeros_like(row)
    for m in range(1, cells_i):
        i = i + (row >= m * cells_j).astype(jnp.int32)
    return i, row - i * cells_j, k


def col(x, c):
    return jnp.broadcast_to(x[:, c : c + 1], x.shape)


def gather_kernel(count_ref, cell_ref, field_ref, out_ref, high_ref, low_ref, *, chunk):
    fields, cells_i, cells_j, _ = field_ref.shape
    owners, capacity = cell_ref.shape
    rows_j = 16
    half_i = cells_i // 2
    rows = half_i * rows_j
    for f in range(fields):
        for i in range(cells_i):
            part = jnp.concatenate(
                [field_ref[f, i], jnp.zeros((rows_j - cells_j, LANES), F32)], axis=0
            )
            high, low = split(part)
            at = (f * half_i + i // 2) * rows_j
            lane = (i % 2) * LANES
            high_ref[at : at + rows_j, lane : lane + LANES] = high
            low_ref[at : at + rows_j, lane : lane + LANES] = low
    out_ref[...] = jnp.zeros(out_ref.shape, F32)
    per = chunk // LANES
    slot_rows = capacity // LANES

    def owner_body(d, carry):
        count = count_ref[d]

        def chunk_body(c, carry):
            start = pl.multiple_of(c * chunk, chunk)
            cell = cell_ref[pl.ds(d, 1), pl.ds(start, chunk)]
            i, j, k = split_cell(cell, cells_i, cells_j)
            slot = start + lax.broadcasted_iota(jnp.int32, cell.shape, 1)
            row = lax.shift_right_logical(i, 1) * rows_j + j
            row = jnp.where(slot < count, row, -1)
            column = lax.bitwise_and(i, 1) * LANES + k
            hot = lax.broadcasted_iota(jnp.int32, (2 * LANES, chunk), 0) == column
            hot = jnp.where(hot, 1.0, 0.0).astype(BF16)
            found = dot_nn(high_ref[...], hot) + dot_nn(low_ref[...], hot)
            pick = lax.broadcasted_iota(jnp.int32, (rows, chunk), 0) == row
            for f in range(fields):
                value = jnp.where(pick, found[f * rows : (f + 1) * rows], 0.0)
                value = jnp.sum(value, axis=0, keepdims=True)
                for q in range(per):
                    out_ref[d, pl.ds(f * slot_rows + c * per + q, 1), :] = value[
                        :, q * LANES : (q + 1) * LANES
                    ]
            return carry

        return lax.fori_loop(0, lax.div(count + (chunk - 1), chunk), chunk_body, carry)

    lax.fori_loop(0, owners, owner_body, 0)


def gather(count, cell, field, chunk=512):
    fields, cells_i, _, _ = field.shape
    owners, capacity = cell.shape
    table = (fields * cells_i // 2 * 16, 2 * LANES)
    return pl.pallas_call(
        functools.partial(gather_kernel, chunk=chunk),
        out_shape=jax.ShapeDtypeStruct((owners, fields * capacity // LANES, LANES), F32),
        in_specs=[
            pl.BlockSpec(memory_space=pltpu.SMEM),
            pl.BlockSpec(memory_space=pltpu.VMEM),
            pl.BlockSpec(memory_space=pltpu.VMEM),
        ],
        out_specs=pl.BlockSpec(memory_space=pltpu.VMEM),
        scratch_shapes=[pltpu.VMEM(table, BF16), pltpu.VMEM(table, BF16)],
        name="gather",
    )(count, cell, field)


def prepare_kernel(
    couple_ref, i_ref, k_ref, i_out, k_tile, k_map, k_rows, k_carry, f_ref, *, cells_i
):
    fields, length = k_ref.shape[1], k_ref.shape[2]
    lower, upper, edge = i_ref[0], i_ref[1], i_ref[2]
    lane = lax.broadcasted_iota(jnp.int32, (8, LANES), 1)

    def edges(matrix, at):
        e0, e1, e2 = col(edge, at), col(edge, at + 1), col(edge, at + 2)
        table = []
        for p in range(cells_i):
            first, second = col(matrix, p * cells_i), col(matrix, p * cells_i + 1)
            table.append((first * e0 + second * e2, first * e1))
        return table

    low_edge = edges(lower, 0)
    up_edge = edges(upper, 3)
    through = []
    for p in range(cells_i):
        total = [jnp.zeros((8, LANES), F32), jnp.zeros((8, LANES), F32)]
        for q in range(p + 1):
            factor = col(upper, p * cells_i + q)
            for a in range(2):
                total[a] = total[a] + factor * low_edge[cells_i - 1 - q][a]
        through.append(total)
    last, prior = cells_i - 1, cells_i - 2
    entries = []
    for table in (through, up_edge):
        for p in range(cells_i):
            entries += [table[p][0], table[p][1]]
    entries += [-low_edge[last][0], -low_edge[last][1], -low_edge[prior][0], -low_edge[prior][1]]
    entries += [-up_edge[last][0], -up_edge[last][1], -up_edge[prior][0], -up_edge[prior][1]]
    entries += [through[last][0], through[last][1], through[prior][0], through[prior][1]]
    tile = jnp.zeros((8, LANES), F32)
    for at, entry in enumerate(entries):
        tile = jnp.where(lane == at, entry, tile)
    i_out[...] = tile

    row8 = lax.broadcasted_iota(jnp.int32, (8, LANES), 0)
    row_n = lax.broadcasted_iota(jnp.int32, (length, length), 0)
    lane_n = lax.broadcasted_iota(jnp.int32, (length, length), 1)
    turn = jnp.where(row_n + lane_n == length - 1, 1.0, 0.0).astype(F32)

    def edge_rows(direction, f):
        e0 = couple_ref[direction, 0, f]
        e1 = couple_ref[direction, 1, f]
        e2 = couple_ref[direction, 2, f]
        first = jnp.where((row8 == 0) & (lane == 0), e0, 0.0)
        first = jnp.where((row8 == 0) & (lane == 1), e2, first)
        return jnp.where((row8 == 1) & (lane == 0), e1, first)

    f_ref[...] = jnp.zeros(f_ref.shape, F32)
    k_carry[...] = jnp.zeros(k_carry.shape, F32)
    for f in range(fields):
        low, up = k_ref[0, f], k_ref[1, f]
        whole = dot_nn(up, dot_nn(turn, low, HIGHEST), HIGHEST)
        whole = dot_nn(turn, whole, HIGHEST)
        k_map[f] = whole
        k_rows[f, 0:1, :] = low[length - 1 : length]
        k_rows[f, 1:2, :] = low[length - 2 : length - 1]
        k_rows[f, 2:4, :] = whole[0:2]
        k_rows[f, 4:8, :] = jnp.zeros((4, length), F32)
        low_rows = dot_nt(edge_rows(2, f), low, HIGHEST)
        flipped = dot_nn(low_rows, turn, HIGHEST)
        across = dot_nt(flipped, up, HIGHEST)
        up_rows = dot_nt(edge_rows(3, f), up, HIGHEST)
        both = jnp.concatenate([across[0:2], up_rows[0:2], jnp.zeros((4, length), F32)], axis=0)
        both = dot_nn(both, turn, HIGHEST)
        for a in range(4):
            k_carry[a, f : f + 1, :] = both[a : a + 1]
        for a in range(2):
            f_ref[a, f : f + 1, :] = low_rows[a : a + 1]
    end = length - 1
    entries = [
        -col(f_ref[0], end),
        -col(f_ref[1], end),
        -col(f_ref[0], end - 1),
        -col(f_ref[1], end - 1),
        -col(k_carry[2], 0),
        -col(k_carry[3], 0),
        -col(k_carry[2], 1),
        -col(k_carry[3], 1),
        col(k_carry[0], 0),
        col(k_carry[1], 0),
        col(k_carry[0], 1),
        col(k_carry[1], 1),
    ]
    tile = jnp.zeros((8, LANES), F32)
    for at, entry in enumerate(entries):
        tile = jnp.where(lane == at, entry, tile)
    k_tile[...] = tile


def prepare(couplings, i_tiles, k_factors, cells_i):
    fields, length = k_factors.shape[1], k_factors.shape[2]
    return pl.pallas_call(
        functools.partial(prepare_kernel, cells_i=cells_i),
        out_shape=(
            jax.ShapeDtypeStruct((8, LANES), F32),
            jax.ShapeDtypeStruct((8, LANES), F32),
            jax.ShapeDtypeStruct((fields, length, length), F32),
            jax.ShapeDtypeStruct((fields, 8, length), F32),
            jax.ShapeDtypeStruct((4, 8, length), F32),
        ),
        in_specs=[
            pl.BlockSpec(memory_space=pltpu.SMEM),
            pl.BlockSpec(memory_space=pltpu.VMEM),
            pl.BlockSpec(memory_space=pltpu.VMEM),
        ],
        out_specs=(pl.BlockSpec(memory_space=pltpu.VMEM),) * 5,
        scratch_shapes=[pltpu.VMEM((2, 8, length), F32)],
        name="prepare",
    )(couplings, i_tiles, k_factors)


def mat2(a, b):
    return [
        a[0] * b[0] + a[1] * b[2],
        a[0] * b[1] + a[1] * b[3],
        a[2] * b[0] + a[3] * b[2],
        a[2] * b[1] + a[3] * b[3],
    ]


def downstream_map(tiles, base, mine):
    peers = len(tiles)
    total = [jnp.zeros((8, LANES), F32)] * 4
    for m in range(1, peers):
        entry = [col(tiles[m], base + c) for c in range(12)]
        step = mat2(mat2(entry[4:8], total), entry[0:4])
        total = [
            jnp.where(m > mine, new - back, old) for new, back, old in zip(step, entry[8:12], total)
        ]
    return total


def scatter_kernel(*refs, peers, chunk, base):
    mine_ref, solve_ref, got_ref, cell_ref, weight_ref, residual_ref = refs[:6]
    tile_refs = refs[6 : 6 + peers]
    start_ref = refs[6 + peers]
    send_refs = refs[7 + peers : 7 + 2 * peers]
    total_ref = refs[7 + 2 * peers]
    fields, cells_i, cells_j, _ = residual_ref.shape
    sources, capacity = cell_ref.shape
    rows_j = 16
    per = chunk // LANES
    slot_rows = capacity // LANES
    total_ref[...] = jnp.zeros(total_ref.shape, F32)

    def source_body(b, carry):
        def chunk_body(c, carry):
            start = pl.multiple_of(c * chunk, chunk)
            cell = cell_ref[pl.ds(b, 1), pl.ds(start, chunk)]
            x = weight_ref[0, pl.ds(b, 1), pl.ds(start, chunk)]
            y = weight_ref[1, pl.ds(b, 1), pl.ds(start, chunk)]
            z = weight_ref[2, pl.ds(b, 1), pl.ds(start, chunk)]
            i, j, k = split_cell(cell, cells_i, cells_j)

            def hat(size, at, t):
                place = lax.broadcasted_iota(jnp.int32, (size, chunk), 0)
                return jnp.where(place == at, 1.0 - t, jnp.where(place == at + 1, t, 0.0))

            along_i = hat(8, i, x)
            along_j = hat(rows_j, j, y)
            k_high, k_low = split(hat(LANES, k, z))
            along_k = jnp.concatenate([k_high, k_low], axis=0)
            highs = []
            lows = []
            for f in range(fields):
                value = jnp.concatenate(
                    [
                        got_ref[b, pl.ds(f * slot_rows + c * per + q, 1), :]
                        for q in range(per)
                    ],
                    axis=1,
                )
                scaled = along_i * value
                for p in range(cells_i):
                    high, low = split(scaled[p : p + 1] * along_j)
                    highs.append(high)
                    lows.append(low)
            high = jnp.concatenate(highs, axis=0)
            low = jnp.concatenate(lows, axis=0)
            total_ref[...] += dot_nt(high, along_k) + dot_nt(low, along_k)
            return carry

        return lax.fori_loop(0, capacity // chunk, chunk_body, carry)

    lax.fori_loop(0, sources, source_body, 0)

    mine = mine_ref[0]
    tiles = [ref[...] for ref in tile_refs]
    onward = downstream_map(tiles, base, mine)
    turned = mat2([col(tiles[0], base + 4 + c) for c in range(4)], onward)
    pad = jnp.zeros((rows_j - cells_j, LANES), F32)
    for f in range(fields):
        data = []
        for i in range(cells_i):
            at = (f * cells_i + i) * rows_j
            spread = total_ref[at : at + rows_j]
            spread = spread[:, :LANES] + spread[:, LANES:]
            data.append(spread + jnp.concatenate([residual_ref[f, i], pad], axis=0))

        def solve(direction, columns):
            result = []
            for p in range(cells_i):
                value = solve_ref[direction, f, p * cells_i] * columns[0]
                for q in range(1, p + 1):
                    value = value + solve_ref[direction, f, p * cells_i + q] * columns[q]
                result.append(value)
            return result

        first = solve(0, data)
        second = solve(1, first[::-1])
        e0, e1 = first[-1], first[-2]
        g0, g1 = second[-1], second[-2]
        m = [jnp.broadcast_to(entry[f : f + 1], (rows_j, LANES)) for entry in turned]
        h0 = g0 + m[0] * e0 + m[1] * e1
        h1 = g1 + m[2] * e0 + m[3] * e1
        for i in range(cells_i):
            at = (f * cells_i + i) * rows_j
            start_ref[at : at + rows_j] = second[cells_i - 1 - i]
        for shift in range(peers):
            ahead = mine + shift < peers
            at = f * rows_j
            send_refs[shift][at : at + rows_j] = jnp.where(ahead, e0, h0)
            at = (fields + f) * rows_j
            send_refs[shift][at : at + rows_j] = jnp.where(ahead, e1, h1)


def scatter(mine, solve_tiles, got, cell, weight, residual, tiles, base, chunk=512):
    fields, cells_i, _, _ = residual.shape
    peers = len(tiles)
    rows = fields * cells_i * 16
    vmem = pl.BlockSpec(memory_space=pltpu.VMEM)
    smem = pl.BlockSpec(memory_space=pltpu.SMEM)
    return pl.pallas_call(
        functools.partial(scatter_kernel, peers=peers, chunk=chunk, base=base),
        out_shape=(jax.ShapeDtypeStruct((rows, LANES), F32),)
        + (jax.ShapeDtypeStruct((2 * fields * 16, LANES), F32),) * peers,
        in_specs=[smem, smem, vmem, vmem, vmem, vmem] + [vmem] * peers,
        out_specs=(vmem,) * (1 + peers),
        scratch_shapes=[pltpu.VMEM((rows, 2 * LANES), F32)],
        name="scatter",
    )(mine, solve_tiles, got, cell, weight, residual, *tiles)


def middle_kernel(*refs, peers, base, fields, cells_i):
    mine_ref, own_ref, start_ref, map_ref, rows_ref, k_tile_ref = refs[:6]
    tile_refs = refs[6 : 6 + peers]
    got_refs = refs[6 + peers : 6 + 2 * peers]
    out_ref, send_ref, field_ref, end_ref = refs[6 + 2 * peers :]
    rows_j = 16
    mine = mine_ref[0]
    tiles = [ref[...] for ref in tile_refs]
    onward = downstream_map(tiles, base, mine)
    forward = [[col(tile, base + c) for c in range(4)] for tile in tiles]
    backward = [[col(tile, base + 4 + c) for c in range(4)] for tile in tiles]
    end_ref[...] = jnp.zeros(end_ref.shape, F32)
    rows = cells_i * rows_j
    for f in range(fields):

        def wide(entry):
            return jnp.broadcast_to(entry[f : f + 1], (rows_j, LANES))

        def advance(matrix, state, add):
            m = [wide(entry) for entry in matrix]
            return [
                m[0] * state[0] + m[1] * state[1] + add[0],
                m[2] * state[0] + m[3] * state[1] + add[1],
            ]

        got = []
        for shift in range(peers):
            low = got_refs[shift][f * rows_j : (f + 1) * rows_j]
            high = got_refs[shift][(fields + f) * rows_j : (fields + f + 1) * rows_j]
            got.append((low, high))
        zero = jnp.zeros((rows_j, LANES), F32)
        before = [zero, zero]
        for shift in range(peers - 1, 0, -1):
            new = advance(forward[shift], before, got[shift])
            before = [jnp.where(shift <= mine, n, o) for n, o in zip(new, before)]
        after = [zero, zero]
        for shift in range(1, peers):
            new = advance(backward[shift], after, got[shift])
            after = [jnp.where(shift > mine, n, o) for n, o in zip(new, after)]
        onto = advance(forward[0], before, got[0])
        after = advance(onward, onto, after)
        for p in range(cells_i):
            at = (f * cells_i + cells_i - 1 - p) * rows_j
            value = start_ref[at : at + rows_j]
            value = value - own_ref[f, 2 * p] * before[0] - own_ref[f, 2 * p + 1] * before[1]
            shift = 2 * cells_i
            value = value - own_ref[f, shift + 2 * p] * after[0]
            value = value - own_ref[f, shift + 2 * p + 1] * after[1]
            field_ref[at : at + rows_j] = value
        block = field_ref[f * rows : (f + 1) * rows]
        out_ref[f * rows : (f + 1) * rows] = dot_nt(block, map_ref[f], HIGHEST)
        ends = dot_nt(rows_ref[f], block, HIGHEST)
        for a in range(4):
            end_ref[a * 8 + f : a * 8 + f + 1, :] = ends[a : a + 1]
    end_ref[32:40] = k_tile_ref[...]
    for d in range(send_ref.shape[0]):
        send_ref[d] = end_ref[...]


def middle(mine, own, start, k_map, k_rows, k_tile, tiles, got, base, owners, fields, cells_i):
    peers = len(tiles)
    vmem = pl.BlockSpec(memory_space=pltpu.VMEM)
    smem = pl.BlockSpec(memory_space=pltpu.SMEM)
    return pl.pallas_call(
        functools.partial(middle_kernel, peers=peers, base=base, fields=fields, cells_i=cells_i),
        out_shape=(
            jax.ShapeDtypeStruct(start.shape, F32),
            jax.ShapeDtypeStruct((owners, 40, LANES), F32),
        ),
        in_specs=[smem, smem] + [vmem] * (4 + 2 * peers),
        out_specs=(vmem, vmem),
        scratch_shapes=[pltpu.VMEM(start.shape, F32), pltpu.VMEM((40, LANES), F32)],
        name="middle",
    )(mine, own, start, k_map, k_rows, k_tile, *tiles, *got)


def finish_kernel(mine_ref, start_ref, got_ref, carry_ref, out_ref):
    fields, cells_i, cells_j, _ = out_ref.shape
    rows_j = 16
    rows = cells_i * rows_j
    blocks = got_ref.shape[0]
    mine = mine_ref[0]
    zero = jnp.zeros((8, LANES), F32)
    entry = [[col(got_ref[m, 32:40], c) for c in range(12)] for m in range(blocks)]
    part = [[got_ref[m, 8 * a : 8 * a + 8] for a in range(4)] for m in range(blocks)]
    states = []
    state = [zero, zero]
    for m in range(blocks):
        states.append(state)
        p = entry[m]
        state = [
            p[0] * state[0] + p[1] * state[1] + part[m][0],
            p[2] * state[0] + p[3] * state[1] + part[m][1],
        ]
    before = [zero, zero]
    after = [zero, zero]
    state = [zero, zero]
    for m in range(blocks - 1, -1, -1):
        here = m == mine
        before = [jnp.where(here, n, o) for n, o in zip(states[m], before)]
        after = [jnp.where(here, n, o) for n, o in zip(state, after)]
        q, b = entry[m][4:8], entry[m][8:12]
        old = states[m]
        state = [
            q[0] * state[0] + q[1] * state[1] + part[m][2] - b[0] * old[0] - b[1] * old[1],
            q[2] * state[0] + q[3] * state[1] + part[m][3] - b[2] * old[0] - b[3] * old[1],
        ]
    for f in range(fields):
        carried = jnp.concatenate(
            [x[f : f + 1] for x in (before[0], before[1], after[0], after[1])]
            + [jnp.zeros((4, LANES), F32)],
            axis=0,
        )
        response = jnp.concatenate(
            [carry_ref[a, f : f + 1, :] for a in range(4)] + [jnp.zeros((4, LANES), F32)], axis=0
        )
        change = dot_tn(carried, response, HIGHEST)
        value = start_ref[f * rows : (f + 1) * rows] - change
        for i in range(cells_i):
            out_ref[f, i] = value[i * rows_j : i * rows_j + cells_j]


def finish(mine, start, got, carry, shape):
    vmem = pl.BlockSpec(memory_space=pltpu.VMEM)
    smem = pl.BlockSpec(memory_space=pltpu.SMEM)
    return pl.pallas_call(
        finish_kernel,
        out_shape=jax.ShapeDtypeStruct(shape, F32),
        in_specs=[smem, vmem, vmem, vmem],
        out_specs=vmem,
        name="finish",
    )(mine, start, got, carry)


def per_device(
    residual,
    adjoint,
    i_factors,
    k_factors,
    couplings,
    receptor_cell,
    send_count,
    donor_cell,
    donor_weight,
):
    fields, cells_i, cells_j, cells_k = adjoint.shape
    owners = receptor_cell.shape[2]
    peers = lax.axis_size("line")
    line = lax.axis_index("line").astype(jnp.int32).reshape(1)
    block = lax.axis_index("block").astype(jnp.int32).reshape(1)
    base = 4 * cells_i

    outgoing = gather(send_count.reshape(owners), receptor_cell[0, 0], adjoint)
    incoming = lax.all_to_all(outgoing, "block", split_axis=0, concat_axis=0, tiled=True)

    square = i_factors[0].reshape(2, fields, cells_i * cells_i)
    square = jnp.pad(square, ((0, 0), (0, 8 - fields), (0, LANES - cells_i * cells_i)))
    edge = couplings[0, 0, 0:2].reshape(6, fields).T
    edge = jnp.pad(edge, ((0, 8 - fields), (0, LANES - 6)))
    i_tiles = jnp.concatenate([square, edge[None]], axis=0)
    own, k_tile, k_map, k_rows, k_carry = prepare(couplings[0, 0], i_tiles, k_factors[0], cells_i)

    def shifted(value, shift):
        return lax.ppermute(value, "line", [(s, (s + shift) % peers) for s in range(peers)])

    tiles = [own] + [shifted(own, m) for m in range(1, peers)]
    start, *ends = scatter(
        line, i_tiles, incoming, donor_cell[0, 0], donor_weight[0, 0], residual, tiles, base
    )
    got = [ends[0]] + [shifted(ends[m], m) for m in range(1, peers)]
    start, message = middle(
        line, own, start, k_map, k_rows, k_tile, tiles, got, base, owners, fields, cells_i
    )
    message = lax.all_to_all(message, "block", split_axis=0, concat_axis=0, tiled=True)
    return finish(block, start, message, k_carry, residual.shape)


def solution(mesh):
    return jax.shard_map(
        per_device,
        mesh=mesh,
        in_specs=(
            P(None, "line", None, "block"),
            P(None, "line", None, "block"),
            P("block", None, None, "line", None),
            P("line", None, None, "block", None),
            P("line", "block", None, None, None),
            P("line", "block", None, None),
            P("line", "block", None),
            P("line", "block", None, None),
            P("line", "block", None, None, None),
        ),
        out_specs=P(None, "line", None, "block"),
        check_vma=False,
    )
```

time: 1010 us -> 90.5 us (0.09)
  other arithmetic: 752 us -> 0.6 us
  blocking collectives: 138 us -> 0 us
  local copies, waits for them, and re-layouts: 92.9 us -> 8.72 us
  Pallas kernels: 0 us -> 47.5 us
  waiting for transfers between devices: 0.01 us -> 14.7 us
  matrix products: 13.6 us -> 0 us
  starting transfers between devices: 7.28 us -> 18.5 us
    scatter-add x1 -> x0, other arithmetic: 705 us -> none  [spread_donors(): return right_side.at[:, targets].add(spread)]
    all_gather x8 -> x0, blocking collectives: 138 us -> none  [carried_in(): everything = jax.tree.map(lambda part: lax.all_gather(part, axis), array)]
    gather x2 -> x0, local copies, waits for them, and re-layouts: 62.9 us -> none  [per_device(): jnp.take(flat_adjoint, receptor_index, axis=1)]
    pallas_call x0 -> x5, Pallas kernels: none -> 47.5 us  [the longest x1 22.8 us: scatter(): pl.pallas_call(functools.partial(scatter_kernel, peers=peers, chunk=chunk...]
    mul x1 -> x0, other arithmetic: 44.1 us -> none  [spread_donors(): spread = jnp.tile(values, (1, 8)) * weights[None, :]]
    dot_general x36 -> x0, matrix products: 13.6 us -> none  [the longest x24 6.59 us: compose(): jnp.einsum('fab,fbl->fal', next_map, first_vec, precision=lax.Precision.H...]
    another operation x14 -> x3, local copies, waits for them, and re-layouts: 10.8 us -> 0.26 us  [the longest x2 0.18 us: per_device(): edge = couplings[0, 0, 0:2].reshape(6, fields).T]
  transfers between devices with their start and end apart: 1 -> 8, of which waited for: 0 -> 5; matrix products, arithmetic and copies ran while one was open for 1% -> 3% of each run, Pallas kernels for 0% -> 9%
where the time goes in v1:
time: 90.5 us; the launch traced here: 90 us
  Pallas kernels  47.5 us (52%)
  starting transfers between devices  18.5 us (20%)
  waiting for transfers between devices  14.7 us (16%)
  local copies, waits for them, and re-layouts  8.72 us (10%)
    pallas_call x1, Pallas kernels, scatter(): pl.pallas_call(functools.partial(scatter_kernel, peers=peers, chunk=chunk...  22.8 us
    pallas_call x1, Pallas kernels, gather(): pl.pallas_call(functools.partial(gather_kernel, chunk=chunk), out_shape=j...  10.1 us
    all_to_all x1, waiting for transfers between devices, per_device(): lax.all_to_all(message, 'block', split_axis=0, concat_axis=0, tiled=True)  8.64 us
    pallas_call x1, Pallas kernels, prepare(): pl.pallas_call(functools.partial(prepare_kernel, cells_i=cells_i), out_sh...  8.4 us
    all_to_all x1, starting transfers between devices, per_device(): lax.all_to_all(outgoing, 'block', split_axis=0, concat_axis=0, tiled=True)  7.62 us
    ppermute x6, waiting for transfers between devices, shifted(): lax.ppermute(value, 'line', [(s, (s + shift) % peers) for s in range(peer...  6.02 us
    all_to_all x1, starting transfers between devices, per_device(): lax.all_to_all(message, 'block', split_axis=0, concat_axis=0, tiled=True)  6 us
    unnamed x24, local copies, waits for them, and re-layouts  5.33 us
  transfers between devices with their start and end apart: 8, of which 5 were waited for; matrix products, arithmetic and copies ran while one was open for 3% of the time, Pallas kernels for 9%

profile of v1, /device:TPU:0, one launch (start us, length us, event | category | flops | bytes accessed | tf_op | source)
XLA Modules:
  0.0 90.0 jit_solution(9727300327206654809)
XLA Ops:
  0.0 1.8 %copy.21.field_ref = f32[6,8,15,128]{3,2,1,0:T(8,128)} copy(f32[6,8,15,128]{3,1,2,0:T(8,128)} %param.10) | data formatting | bytes 737280 | tf_op args[1]
  1.8 10.1 %gather.1 = f32[8,96,128]{2,1,0:T(8,128)} custom-call(s32[8]{0:T(128)} %bitcast.21, s32[8,2048]{1,0:T(8,128)} %bitcast.17, f32[6,8,15,128]{3,2,1,0:T(8,128)} %copy.21.field_ref), custom_call_target="tpu_custom_call" | custom-call | tf_op jit(solution)/shard_map/gather/pallas_call | solution.py:105
  11.9 7.6 %all-to-all-start = ((f32[8,96,128]{2,1,0:T(8,128)}), f32[8,96,128]{2,1,0:T(8,128)S(1)}, u32[]{:S(2)}, u32[]{:S(2)}) async-start(f32[8,96,128]{2,1,0:T(8,128)} %gather.1), calls=%async_computation | async-start | bytes 786432 | tf_op jit(solution)/shard_map/all_to_all | solution.py:519
  19.5 0.7 slice-done
  20.2 0.1 copy.25
  20.3 0.1 reshape.13
  20.4 0.1 reshape.12
  20.5 0.6 copy-done.10
  21.1 0.6 copy.20.couple_ref
  21.7 0.6 select_maximum_fusion.i_ref.refs_1_
  22.3 8.4 %prepare.1 = (f32[8,128]{1,0:T(8,128)}, f32[8,128]{1,0:T(8,128)}, f32[6,128,128]{2,1,0:T(8,128)}, f32[6,8,128]{2,1,0:T(8,128)}, f32[4,8,128]{2,1,0:T(8,128)}) custom-call(f32[4,3,6]{2,1,0:T(4,128)} %copy.20.couple_ref, f32[3,8,128]{2,1,0:T(8,128)} %select_maximum_fusion.i_ref.refs_1_, f32[2,6,128,128]{3,2,1,0:T(8,128)} %bitcast.15), custom_call_target="tpu_custom_call" | custom-call | tf_op jit(solution)/shard_map/prepare/pallas_call | solution.py:214
  30.7 0.1 collective-permute-start.2
  30.7 2.5 %collective-permute-start.1 = (f32[8,128]{1,0:T(8,128)}, f32[8,128]{1,0:T(8,128)S(1)}, u32[]{:S(2)}, u32[]{:S(2)}) collective-permute-start(f32[8,128]{1,0:T(8,128)} %get-tuple-element.17.refs_6_.refs_1_), channel_id=1, source_target_pairs={{0,16},{8,24},{16,0},{24,8},{1,17},{9,25},{17,1},{25,9},{2,18},{10... | collective-permute-start | bytes 12296 | tf_op jit(solution)/shard_map/ppermute | solution.py:529
  33.2 0.2 collective-permute-start
  33.5 0.8 copy.22.refs_5_
  34.3 0.8 collective-permute-done.1.refs_8_
  35.1 1.4 %collective-permute-done.refs_7_ = f32[8,128]{1,0:T(8,128)S(1)} collective-permute-done((f32[8,128]{1,0:T(8,128)}, f32[8,128]{1,0:T(8,128)S(1)}, u32[]{:S(2)}, u32[]{:S(2)}) %collective-permute-start) | collective-permute-done | bytes 4128 | tf_op jit(solution)/shard_map/ppermute | solution.py:529
  36.5 0.6 copy-done.9
  37.1 0.2 copy-done
  37.2 22.8 %scatter.1 = (f32[768,128]{1,0:T(8,128)}, f32[192,128]{1,0:T(8,128)}, f32[192,128]{1,0:T(8,128)}, f32[192,128]{1,0:T(8,128)}, f32[192,128]{1,0:T(8,128)}) custom-call(s32[1]{0:T(128)} %bitcast.1.refs_0_, f32[3,8,128]{2,1,0:T(8,128)} %select_maximum_fusion.i_ref.refs_1_, f32[8,96,128]{2,1,0:T(8,128)} %copy-done, s32[8,2048]{1,0:T(8,128)} %bitcast.18, ...), custom_call_target="tpu_custom_call" | custom-call | tf_op jit(solution)/shard_map/scatter/pallas_call | solution.py:355
  60.0 0.7 collective-permute-start.4
  60.7 1.4 %collective-permute-start.5 = (f32[192,128]{1,0:T(8,128)}, f32[192,128]{1,0:T(8,128)S(1)}, u32[]{:S(2)}, u32[]{:S(2)}) collective-permute-start(f32[192,128]{1,0:T(8,128)} %get-tuple-element.25), channel_id=1, source_target_pairs={{0,24},{8,0},{16,8},{24,16},{1,25},{9,1},{17,9},{25,17},{2,26},{10... | collective-permute-start | bytes 294920 | tf_op jit(solution)/shard_map/ppermute | solution.py:529
  62.1 2.6 %collective-permute-done.3.refs_11_ = f32[192,128]{1,0:T(8,128)S(1)} collective-permute-done((f32[192,128]{1,0:T(8,128)}, f32[192,128]{1,0:T(8,128)S(1)}, u32[]{:S(2)}, u32[]{:S(2)}) %collective-permute-start.3) | collective-permute-done | bytes 98336 | tf_op jit(solution)/shard_map/ppermute | solution.py:529
  64.7 1.2 %collective-permute-done.4.refs_12_ = f32[192,128]{1,0:T(8,128)S(1)} collective-permute-done((f32[192,128]{1,0:T(8,128)}, f32[192,128]{1,0:T(8,128)S(1)}, u32[]{:S(2)}, u32[]{:S(2)}) %collective-permute-start.4) | collective-permute-done | bytes 98336 | tf_op jit(solution)/shard_map/ppermute | solution.py:529
  65.9 0.6 copy-done.4
  66.6 0.1 copy-done.5
  66.6 3.6 %middle.1 = (f32[768,128]{1,0:T(8,128)}, f32[8,40,128]{2,1,0:T(8,128)}) custom-call(s32[1]{0:T(128)} %bitcast.1.refs_0_, f32[8,128]{1,0:T(8,128)} %get-tuple-element.17.refs_6_.refs_1_, f32[768,128]{1,0:T(8,128)} %get-tuple-element.18.refs_2_, f32[6,128,128]{2,1,0:T(8,128)} %get-tuple-element.19.refs_3_, f32[6,8,128]{2,1,0:T(8,128)} %get-tuple-element.20.refs_4_, ...), custom_call_target="tpu_custom_call" | custom-call | tf_op jit(solution)/shard_map/middle/pallas_call | solution.py:429
  70.3 6.0 %all-to-all-start.1 = ((f32[8,40,128]{2,1,0:T(8,128)}), f32[8,40,128]{2,1,0:T(8,128)S(1)}, u32[]{:S(2)}, u32[]{:S(2)}) async-start(f32[8,40,128]{2,1,0:T(8,128)} %get-tuple-element.27), calls=%async_computation.1 | async-start | bytes 327680 | tf_op jit(solution)/shard_map/all_to_all | solution.py:539
  76.2 8.6 %all-to-all-done.1.got_ref = f32[8,40,128]{2,1,0:T(8,128)S(1)} async-done(((f32[8,40,128]{2,1,0:T(8,128)}), f32[8,40,128]{2,1,0:T(8,128)S(1)}, u32[]{:S(2)}, u32[]{:S(2)}) %all-to-all-start.1) | async-done | bytes 163872 | tf_op jit(solution)/shard_map/all_to_all | solution.py:539
  84.9 0.7 copy-done.1
  85.6 2.6 %finish.1 = f32[6,8,15,128]{3,2,1,0:T(8,128)} custom-call(s32[1]{0:T(128)} %bitcast.mine_ref, f32[768,128]{1,0:T(8,128)} %get-tuple-element.26.start_ref, f32[8,40,128]{2,1,0:T(8,128)} %copy-done.1, f32[4,8,128]{2,1,0:T(8,128)} %get-tuple-element.28.carry_ref), custom_call_target="tpu_custom_call" | custom-call | tf_op jit(solution)/shard_map/finish/pallas_call | solution.py:491
  88.2 1.9 %copy.23 = f32[6,8,15,128]{3,1,2,0:T(8,128)} copy(f32[6,8,15,128]{3,2,1,0:T(8,128)} %finish.1) | data formatting | bytes 737280 | tf_op jit(solution)/shard_map/finish/pallas_call | solution.py:491
  (22 shorter events, 0.0 us)
Async XLA Ops:
  11.9 8.5 %copy-start.6 = (f32[1,2,6,8,8]{4,3,2,1,0:T(8,128)S(1)}, f32[1,2,6,8,8]{4,3,2,1,0:T(8,128)}, u32[]{:S(2)}) copy-start(f32[1,2,6,8,8]{4,3,2,1,0:T(8,128)} %param.11) | copy-start | bytes 9220
  11.9 24.6 %all-to-all-start = ((f32[8,96,128]{2,1,0:T(8,128)}), f32[8,96,128]{2,1,0:T(8,128)S(1)}, u32[]{:S(2)}, u32[]{:S(2)}) async-start(f32[8,96,128]{2,1,0:T(8,128)} %gather.1), calls=%async_computation | async-start | bytes 786432 | tf_op jit(solution)/shard_map/all_to_all | solution.py:519
  19.5 0.7 slice-start
  20.4 0.7 copy-start.10
  22.3 11.2 %copy-start.2 = (f32[6,8,15,128]{3,1,2,0:T(8,128)S(1)}, f32[6,8,15,128]{3,1,2,0:T(8,128)}, u32[]{:S(2)}) copy-start(f32[6,8,15,128]{3,1,2,0:T(8,128)} %param.9) | copy-start | bytes 1105924
  30.7 3.6 %collective-permute-start.2 = (f32[8,128]{1,0:T(8,128)}, f32[8,128]{1,0:T(8,128)S(1)}, u32[]{:S(2)}, u32[]{:S(2)}) collective-permute-start(f32[8,128]{1,0:T(8,128)} %get-tuple-element.17.refs_6_.refs_1_), channel_id=1, source_target_pairs={{0,24},{8,0},{16,8},{24,16},{1,25},{9,1},{17,9},{25,17},{2,26},{10... | collective-permute-start | bytes 12296 | tf_op jit(solution)/shard_map/ppermute | solution.py:529
  30.7 4.3 %collective-permute-start.1 = (f32[8,128]{1,0:T(8,128)}, f32[8,128]{1,0:T(8,128)S(1)}, u32[]{:S(2)}, u32[]{:S(2)}) collective-permute-start(f32[8,128]{1,0:T(8,128)} %get-tuple-element.17.refs_6_.refs_1_), channel_id=1, source_target_pairs={{0,16},{8,24},{16,0},{24,8},{1,17},{9,25},{17,1},{25,9},{2,18},{10... | collective-permute-start | bytes 12296 | tf_op jit(solution)/shard_map/ppermute | solution.py:529
  33.2 3.2 %collective-permute-start = (f32[8,128]{1,0:T(8,128)}, f32[8,128]{1,0:T(8,128)S(1)}, u32[]{:S(2)}, u32[]{:S(2)}) collective-permute-start(f32[8,128]{1,0:T(8,128)} %get-tuple-element.17.refs_6_.refs_1_), channel_id=1, source_target_pairs={{0,8},{8,16},{16,24},{24,0},{1,9},{9,17},{17,25},{25,1},{2,10},{10... | collective-permute-start | bytes 12296 | tf_op jit(solution)/shard_map/ppermute | solution.py:529
  34.3 2.2 %copy-start.7 = (f32[8,128]{1,0:T(8,128)}, f32[8,128]{1,0:T(8,128)S(1)}, u32[]{:S(2)}) copy-start(f32[8,128]{1,0:T(8,128)S(1)} %collective-permute-done.2.refs_9_) | copy-start | bytes 12292
  35.1 1.4 %copy-start.8 = (f32[8,128]{1,0:T(8,128)}, f32[8,128]{1,0:T(8,128)S(1)}, u32[]{:S(2)}) copy-start(f32[8,128]{1,0:T(8,128)S(1)} %collective-permute-done.1.refs_8_) | copy-start | bytes 12292
  36.5 0.6 copy-start.9
  36.5 0.7 copy-start
  60.0 4.7 %collective-permute-start.3 = (f32[192,128]{1,0:T(8,128)}, f32[192,128]{1,0:T(8,128)S(1)}, u32[]{:S(2)}, u32[]{:S(2)}) collective-permute-start(f32[192,128]{1,0:T(8,128)} %get-tuple-element.23), channel_id=1, source_target_pairs={{0,8},{8,16},{16,24},{24,0},{1,9},{9,17},{17,25},{25,1},{2,10},{10... | collective-permute-start | bytes 294920 | tf_op jit(solution)/shard_map/ppermute | solution.py:529
  60.0 5.9 %collective-permute-start.4 = (f32[192,128]{1,0:T(8,128)}, f32[192,128]{1,0:T(8,128)S(1)}, u32[]{:S(2)}, u32[]{:S(2)}) collective-permute-start(f32[192,128]{1,0:T(8,128)} %get-tuple-element.24), channel_id=1, source_target_pairs={{0,16},{8,24},{16,0},{24,8},{1,17},{9,25},{17,1},{25,9},{2,18},{10... | collective-permute-start | bytes 294920 | tf_op jit(solution)/shard_map/ppermute | solution.py:529
  60.7 5.3 %collective-permute-start.5 = (f32[192,128]{1,0:T(8,128)}, f32[192,128]{1,0:T(8,128)S(1)}, u32[]{:S(2)}, u32[]{:S(2)}) collective-permute-start(f32[192,128]{1,0:T(8,128)} %get-tuple-element.25), channel_id=1, source_target_pairs={{0,24},{8,0},{16,8},{24,16},{1,25},{9,1},{17,9},{25,17},{2,26},{10... | collective-permute-start | bytes 294920 | tf_op jit(solution)/shard_map/ppermute | solution.py:529
  64.7 1.3 %copy-start.3 = (f32[192,128]{1,0:T(8,128)}, f32[192,128]{1,0:T(8,128)S(1)}, u32[]{:S(2)}) copy-start(f32[192,128]{1,0:T(8,128)S(1)} %collective-permute-done.3.refs_11_) | copy-start | bytes 294916
  65.9 0.6 copy-start.4
  65.9 0.7 copy-start.5
  70.3 14.6 %all-to-all-start.1 = ((f32[8,40,128]{2,1,0:T(8,128)}), f32[8,40,128]{2,1,0:T(8,128)S(1)}, u32[]{:S(2)}, u32[]{:S(2)}) async-start(f32[8,40,128]{2,1,0:T(8,128)} %get-tuple-element.27), calls=%async_computation.1 | async-start | bytes 327680 | tf_op jit(solution)/shard_map/all_to_all | solution.py:539
  84.9 0.7 copy-start.1

commit v2 on v1

--- a/solution.py
+++ b/solution.py
@@ -34,6 +34,39 @@
     return lax.dot_general(
         a, b, (((0,), (0,)), ((), ())), precision=precision, preferred_element_type=F32
     )
+
+
+def dot3(dot, a, b, axis_a, axis_b):
+    a_high, a_low = split(a)
+    b_high, b_low = split(b)
+    left = jnp.concatenate([a_high, a_high, a_low], axis=axis_a)
+    right = jnp.concatenate([b_high, b_low, b_high], axis=axis_b)
+    return dot(left, right)
+
+
+def product_nt(a, b):
+    return dot3(dot_nt, a, b, 1, 1)
+
+
+def product_nn(a, b):
+    return dot3(dot_nn, a, b, 1, 0)
+
+
+def turn_lanes(x, turn):
+    return dot_nn(jnp.concatenate(split(x), axis=1), jnp.concatenate([turn, turn], axis=0))
+
+
+def turn_rows(x, turn):
+    return dot_nn(jnp.concatenate([turn, turn], axis=1), jnp.concatenate(split(x), axis=0))
+
+
+def rows_of(value, count, dtype):
+    return jnp.broadcast_to(value, (count, value.shape[1])).astype(dtype)
+
+
+def places(size, width):
+    place = lax.broadcasted_iota(jnp.int32, (size, width), 0)
+    return place.astype(F32).astype(BF16)
 
 
 def split_cell(cell, cells_i, cells_j):
@@ -49,23 +82,24 @@
     return jnp.broadcast_to(x[:, c : c + 1], x.shape)
 
 
-def gather_kernel(count_ref, cell_ref, field_ref, out_ref, high_ref, low_ref, *, chunk):
-    fields, cells_i, cells_j, _ = field_ref.shape
+def gather_kernel(
+    count_ref, cell_ref, field_ref, out_ref, high_ref, low_ref, place_ref, *, chunk
+):
+    fields, cells_j, cells_i, _ = field_ref.shape
     owners, capacity = cell_ref.shape
     rows_j = 16
     half_i = cells_i // 2
     rows = half_i * rows_j
+    pad = jnp.zeros((rows_j - cells_j, LANES), F32)
     for f in range(fields):
         for i in range(cells_i):
-            part = jnp.concatenate(
-                [field_ref[f, i], jnp.zeros((rows_j - cells_j, LANES), F32)], axis=0
-            )
-            high, low = split(part)
+            high, low = split(jnp.concatenate([field_ref[f, :, i, :], pad], axis=0))
             at = (f * half_i + i // 2) * rows_j
             lane = (i % 2) * LANES
             high_ref[at : at + rows_j, lane : lane + LANES] = high
             low_ref[at : at + rows_j, lane : lane + LANES] = low
     out_ref[...] = jnp.zeros(out_ref.shape, F32)
+    place_ref[...] = places(2 * LANES, LANES)
     per = chunk // LANES
     slot_rows = capacity // LANES
 
@@ -79,9 +113,14 @@
             slot = start + lax.broadcasted_iota(jnp.int32, cell.shape, 1)
             row = lax.shift_right_logical(i, 1) * rows_j + j
             row = jnp.where(slot < count, row, -1)
-            column = lax.bitwise_and(i, 1) * LANES + k
-            hot = lax.broadcasted_iota(jnp.int32, (2 * LANES, chunk), 0) == column
-            hot = jnp.where(hot, 1.0, 0.0).astype(BF16)
+            column = (lax.bitwise_and(i, 1) * LANES + k).astype(F32)
+            column = rows_of(column, 16, BF16)
+            place = place_ref[...]
+            hot = []
+            for r in range(2 * LANES // 16):
+                here = jnp.concatenate([place[16 * r : 16 * r + 16]] * per, axis=1)
+                hot.append(jnp.where(here == column, jnp.asarray(1, BF16), jnp.asarray(0, BF16)))
+            hot = jnp.concatenate(hot, axis=0)
             found = dot_nn(high_ref[...], hot) + dot_nn(low_ref[...], hot)
             pick = lax.broadcasted_iota(jnp.int32, (rows, chunk), 0) == row
             for f in range(fields):
@@ -99,7 +138,7 @@
 
 
 def gather(count, cell, field, chunk=512):
-    fields, cells_i, _, _ = field.shape
+    fields, _, cells_i, _ = field.shape
     owners, capacity = cell.shape
     table = (fields * cells_i // 2 * 16, 2 * LANES)
     return pl.pallas_call(
@@ -111,17 +150,25 @@
             pl.BlockSpec(memory_space=pltpu.VMEM),
         ],
         out_specs=pl.BlockSpec(memory_space=pltpu.VMEM),
-        scratch_shapes=[pltpu.VMEM(table, BF16), pltpu.VMEM(table, BF16)],
+        scratch_shapes=[
+            pltpu.VMEM(table, BF16),
+            pltpu.VMEM(table, BF16),
+            pltpu.VMEM((2 * LANES, LANES), BF16),
+        ],
         name="gather",
     )(count, cell, field)
 
 
-def prepare_kernel(
-    couple_ref, i_ref, k_ref, i_out, k_tile, k_map, k_rows, k_carry, f_ref, *, cells_i
-):
-    fields, length = k_ref.shape[1], k_ref.shape[2]
+def lay_out(entries):
+    lane = lax.broadcasted_iota(jnp.int32, (8, LANES), 1)
+    tile = jnp.zeros((8, LANES), F32)
+    for at, entry in enumerate(entries):
+        tile = jnp.where(lane == at, entry, tile)
+    return tile
+
+
+def prepare_i_kernel(i_ref, i_out, *, cells_i):
     lower, upper, edge = i_ref[0], i_ref[1], i_ref[2]
-    lane = lax.broadcasted_iota(jnp.int32, (8, LANES), 1)
 
     def edges(matrix, at):
         e0, e1, e2 = col(edge, at), col(edge, at + 1), col(edge, at + 2)
@@ -149,20 +196,31 @@
     entries += [-low_edge[last][0], -low_edge[last][1], -low_edge[prior][0], -low_edge[prior][1]]
     entries += [-up_edge[last][0], -up_edge[last][1], -up_edge[prior][0], -up_edge[prior][1]]
     entries += [through[last][0], through[last][1], through[prior][0], through[prior][1]]
-    tile = jnp.zeros((8, LANES), F32)
-    for at, entry in enumerate(entries):
-        tile = jnp.where(lane == at, entry, tile)
-    i_out[...] = tile
-
+    i_out[...] = lay_out(entries)
+
+
+def prepare_i(i_tiles, cells_i):
+    return pl.pallas_call(
+        functools.partial(prepare_i_kernel, cells_i=cells_i),
+        out_shape=jax.ShapeDtypeStruct((8, LANES), F32),
+        in_specs=[pl.BlockSpec(memory_space=pltpu.VMEM)],
+        out_specs=pl.BlockSpec(memory_space=pltpu.VMEM),
+        name="prepare_i",
+    )(i_tiles)
+
+
+def prepare_k_kernel(couple_ref, k_ref, k_tile, k_map, k_rows, k_carry, f_ref):
+    fields, length = k_ref.shape[1], k_ref.shape[2]
+    lane = lax.broadcasted_iota(jnp.int32, (8, LANES), 1)
     row8 = lax.broadcasted_iota(jnp.int32, (8, LANES), 0)
     row_n = lax.broadcasted_iota(jnp.int32, (length, length), 0)
     lane_n = lax.broadcasted_iota(jnp.int32, (length, length), 1)
-    turn = jnp.where(row_n + lane_n == length - 1, 1.0, 0.0).astype(F32)
+    turn = jnp.where(row_n + lane_n == length - 1, 1.0, 0.0).astype(BF16)
 
     def edge_rows(direction, f):
-        e0 = couple_ref[direction, 0, f]
-        e1 = couple_ref[direction, 1, f]
-        e2 = couple_ref[direction, 2, f]
+        e0 = couple_ref[0, direction, f]
+        e1 = couple_ref[1, direction, f]
+        e2 = couple_ref[2, direction, f]
         first = jnp.where((row8 == 0) & (lane == 0), e0, 0.0)
         first = jnp.where((row8 == 0) & (lane == 1), e2, first)
         return jnp.where((row8 == 1) & (lane == 0), e1, first)
@@ -171,50 +229,50 @@
     k_carry[...] = jnp.zeros(k_carry.shape, F32)
     for f in range(fields):
         low, up = k_ref[0, f], k_ref[1, f]
-        whole = dot_nn(up, dot_nn(turn, low, HIGHEST), HIGHEST)
-        whole = dot_nn(turn, whole, HIGHEST)
+        whole = turn_rows(product_nn(up, turn_rows(low, turn)), turn)
         k_map[f] = whole
-        k_rows[f, 0:1, :] = low[length - 1 : length]
-        k_rows[f, 1:2, :] = low[length - 2 : length - 1]
-        k_rows[f, 2:4, :] = whole[0:2]
-        k_rows[f, 4:8, :] = jnp.zeros((4, length), F32)
-        low_rows = dot_nt(edge_rows(2, f), low, HIGHEST)
-        flipped = dot_nn(low_rows, turn, HIGHEST)
-        across = dot_nt(flipped, up, HIGHEST)
-        up_rows = dot_nt(edge_rows(3, f), up, HIGHEST)
+        low_rows = product_nt(edge_rows(2, f), low)
+        across = product_nt(turn_lanes(low_rows, turn), up)
+        up_rows = product_nt(edge_rows(3, f), up)
         both = jnp.concatenate([across[0:2], up_rows[0:2], jnp.zeros((4, length), F32)], axis=0)
-        both = dot_nn(both, turn, HIGHEST)
+        both = turn_lanes(both, turn)
+        k_rows[f] = jnp.concatenate(
+            [
+                low[length - 1 : length],
+                low[length - 2 : length - 1],
+                whole[0:2],
+                jnp.zeros((4, length), F32),
+            ],
+            axis=0,
+        )
         for a in range(4):
             k_carry[a, f : f + 1, :] = both[a : a + 1]
         for a in range(2):
             f_ref[a, f : f + 1, :] = low_rows[a : a + 1]
     end = length - 1
-    entries = [
-        -col(f_ref[0], end),
-        -col(f_ref[1], end),
-        -col(f_ref[0], end - 1),
-        -col(f_ref[1], end - 1),
-        -col(k_carry[2], 0),
-        -col(k_carry[3], 0),
-        -col(k_carry[2], 1),
-        -col(k_carry[3], 1),
-        col(k_carry[0], 0),
-        col(k_carry[1], 0),
-        col(k_carry[0], 1),
-        col(k_carry[1], 1),
-    ]
-    tile = jnp.zeros((8, LANES), F32)
-    for at, entry in enumerate(entries):
-        tile = jnp.where(lane == at, entry, tile)
-    k_tile[...] = tile
-
-
-def prepare(couplings, i_tiles, k_factors, cells_i):
+    k_tile[...] = lay_out(
+        [
+            -col(f_ref[0], end),
+            -col(f_ref[1], end),
+            -col(f_ref[0], end - 1),
+            -col(f_ref[1], end - 1),
+            -col(k_carry[2], 0),
+            -col(k_carry[3], 0),
+            -col(k_carry[2], 1),
+            -col(k_carry[3], 1),
+            col(k_carry[0], 0),
+            col(k_carry[1], 0),
+            col(k_carry[0], 1),
+            col(k_carry[1], 1),
+        ]
+    )
+
+
+def prepare_k(couplings, k_factors):
     fields, length = k_factors.shape[1], k_factors.shape[2]
     return pl.pallas_call(
-        functools.partial(prepare_kernel, cells_i=cells_i),
+        prepare_k_kernel,
         out_shape=(
-            jax.ShapeDtypeStruct((8, LANES), F32),
             jax.ShapeDtypeStruct((8, LANES), F32),
             jax.ShapeDtypeStruct((fields, length, length), F32),
             jax.ShapeDtypeStruct((fields, 8, length), F32),
@@ -223,12 +281,11 @@
         in_specs=[
             pl.BlockSpec(memory_space=pltpu.SMEM),
             pl.BlockSpec(memory_space=pltpu.VMEM),
-            pl.BlockSpec(memory_space=pltpu.VMEM),
         ],
-        out_specs=(pl.BlockSpec(memory_space=pltpu.VMEM),) * 5,
+        out_specs=(pl.BlockSpec(memory_space=pltpu.VMEM),) * 4,
         scratch_shapes=[pltpu.VMEM((2, 8, length), F32)],
-        name="prepare",
-    )(couplings, i_tiles, k_factors)
+        name="prepare_k",
+    )(couplings, k_factors)
 
 
 def mat2(a, b):
@@ -257,13 +314,14 @@
     tile_refs = refs[6 : 6 + peers]
     start_ref = refs[6 + peers]
     send_refs = refs[7 + peers : 7 + 2 * peers]
-    total_ref = refs[7 + 2 * peers]
-    fields, cells_i, cells_j, _ = residual_ref.shape
+    total_ref, place_ref, fold_ref = refs[7 + 2 * peers :]
+    fields, cells_j, cells_i, _ = residual_ref.shape
     sources, capacity = cell_ref.shape
     rows_j = 16
     per = chunk // LANES
     slot_rows = capacity // LANES
     total_ref[...] = jnp.zeros(total_ref.shape, F32)
+    place_ref[...] = places(LANES, LANES)
 
     def source_body(b, carry):
         def chunk_body(c, carry):
@@ -278,12 +336,22 @@
                 place = lax.broadcasted_iota(jnp.int32, (size, chunk), 0)
                 return jnp.where(place == at, 1.0 - t, jnp.where(place == at + 1, t, 0.0))
 
-            along_i = hat(8, i, x)
+            along_i = hat(cells_i, i, x)
             along_j = hat(rows_j, j, y)
-            k_high, k_low = split(hat(LANES, k, z))
-            along_k = jnp.concatenate([k_high, k_low], axis=0)
-            highs = []
-            lows = []
+            first = rows_of(k.astype(F32), 16, BF16)
+            second = rows_of((k + 1).astype(F32), 16, BF16)
+            far = split(rows_of(z, 16, F32))
+            near = split(rows_of(1.0 - z, 16, F32))
+            zero = jnp.zeros((16, chunk), BF16)
+            place = place_ref[...]
+            along_k = []
+            for part in range(2):
+                for r in range(LANES // 16):
+                    here = jnp.concatenate([place[16 * r : 16 * r + 16]] * per, axis=1)
+                    weight = jnp.where(here == second, far[part], zero)
+                    along_k.append(jnp.where(here == first, near[part], weight))
+            along_k = jnp.concatenate(along_k, axis=0)
+            blocks = []
             for f in range(fields):
                 value = jnp.concatenate(
                     [
@@ -292,20 +360,19 @@
                     ],
                     axis=1,
                 )
-                scaled = along_i * value
-                for p in range(cells_i):
-                    high, low = split(scaled[p : p + 1] * along_j)
-                    highs.append(high)
-                    lows.append(low)
-            high = jnp.concatenate(highs, axis=0)
-            low = jnp.concatenate(lows, axis=0)
-            total_ref[...] += dot_nt(high, along_k) + dot_nt(low, along_k)
+                scaled = along_j * value
+                blocks += [along_i * scaled[q : q + 1] for q in range(cells_j)]
+            high, low = split(jnp.concatenate(blocks, axis=0))
+            total_ref[...] += dot_nt(
+                jnp.concatenate([high, low], axis=1), jnp.concatenate([along_k, along_k], axis=1)
+            )
             return carry
 
         return lax.fori_loop(0, capacity // chunk, chunk_body, carry)
 
     lax.fori_loop(0, sources, source_body, 0)
 
+    fold_ref[...] = total_ref[:, :LANES] + total_ref[:, LANES:]
     mine = mine_ref[0]
     tiles = [ref[...] for ref in tile_refs]
     onward = downstream_map(tiles, base, mine)
@@ -314,10 +381,8 @@
     for f in range(fields):
         data = []
         for i in range(cells_i):
-            at = (f * cells_i + i) * rows_j
-            spread = total_ref[at : at + rows_j]
-            spread = spread[:, :LANES] + spread[:, LANES:]
-            data.append(spread + jnp.concatenate([residual_ref[f, i], pad], axis=0))
+            at = pl.ds(f * cells_i * cells_j + i, cells_j, stride=cells_i)
+            data.append(jnp.concatenate([fold_ref[at, :] + residual_ref[f, :, i, :], pad], axis=0))
 
         def solve(direction, columns):
             result = []
@@ -346,8 +411,8 @@
             send_refs[shift][at : at + rows_j] = jnp.where(ahead, e1, h1)
 
 
-def scatter(mine, solve_tiles, got, cell, weight, residual, tiles, base, chunk=512):
-    fields, cells_i, _, _ = residual.shape
+def scatter(mine, solve_tiles, got, cell, weight, residual, tiles, base, chunk=1024):
+    fields, cells_j, cells_i, _ = residual.shape
     peers = len(tiles)
     rows = fields * cells_i * 16
     vmem = pl.BlockSpec(memory_space=pltpu.VMEM)
@@ -358,7 +423,11 @@
         + (jax.ShapeDtypeStruct((2 * fields * 16, LANES), F32),) * peers,
         in_specs=[smem, smem, vmem, vmem, vmem, vmem] + [vmem] * peers,
         out_specs=(vmem,) * (1 + peers),
-        scratch_shapes=[pltpu.VMEM((rows, 2 * LANES), F32)],
+        scratch_shapes=[
+            pltpu.VMEM((fields * cells_i * cells_j, 2 * LANES), F32),
+            pltpu.VMEM((LANES, LANES), BF16),
+            pltpu.VMEM((fields * cells_i * cells_j, LANES), F32),
+        ],
         name="scatter",
     )(mine, solve_tiles, got, cell, weight, residual, *tiles)
 
@@ -413,11 +482,11 @@
             value = value - own_ref[f, shift + 2 * p + 1] * after[1]
             field_ref[at : at + rows_j] = value
         block = field_ref[f * rows : (f + 1) * rows]
-        out_ref[f * rows : (f + 1) * rows] = dot_nt(block, map_ref[f], HIGHEST)
-        ends = dot_nt(rows_ref[f], block, HIGHEST)
+        out_ref[f * rows : (f + 1) * rows] = product_nt(block, map_ref[f])
+        ends = product_nt(rows_ref[f], block)
         for a in range(4):
-            end_ref[a * 8 + f : a * 8 + f + 1, :] = ends[a : a + 1]
-    end_ref[32:40] = k_tile_ref[...]
+            end_ref[a * fields + f : a * fields + f + 1, :] = ends[a : a + 1]
+    end_ref[4 * fields : 4 * fields + 8] = k_tile_ref[...]
     for d in range(send_ref.shape[0]):
         send_ref[d] = end_ref[...]
 
@@ -430,24 +499,24 @@
         functools.partial(middle_kernel, peers=peers, base=base, fields=fields, cells_i=cells_i),
         out_shape=(
             jax.ShapeDtypeStruct(start.shape, F32),
-            jax.ShapeDtypeStruct((owners, 40, LANES), F32),
+            jax.ShapeDtypeStruct((owners, 4 * fields + 8, LANES), F32),
         ),
         in_specs=[smem, smem] + [vmem] * (4 + 2 * peers),
         out_specs=(vmem, vmem),
-        scratch_shapes=[pltpu.VMEM(start.shape, F32), pltpu.VMEM((40, LANES), F32)],
+        scratch_shapes=[pltpu.VMEM(start.shape, F32), pltpu.VMEM((4 * fields + 8, LANES), F32)],
         name="middle",
     )(mine, own, start, k_map, k_rows, k_tile, *tiles, *got)
 
 
 def finish_kernel(mine_ref, start_ref, got_ref, carry_ref, out_ref):
-    fields, cells_i, cells_j, _ = out_ref.shape
+    fields, cells_j, cells_i, _ = out_ref.shape
     rows_j = 16
     rows = cells_i * rows_j
     blocks = got_ref.shape[0]
     mine = mine_ref[0]
     zero = jnp.zeros((8, LANES), F32)
-    entry = [[col(got_ref[m, 32:40], c) for c in range(12)] for m in range(blocks)]
-    part = [[got_ref[m, 8 * a : 8 * a + 8] for a in range(4)] for m in range(blocks)]
+    entry = [[col(got_ref[m, 4 * fields : 4 * fields + 8], c) for c in range(12)] for m in range(blocks)]
+    part = [[got_ref[m, fields * a : fields * a + 8] for a in range(4)] for m in range(blocks)]
     states = []
     state = [zero, zero]
     for m in range(blocks):
@@ -479,10 +548,10 @@
         response = jnp.concatenate(
             [carry_ref[a, f : f + 1, :] for a in range(4)] + [jnp.zeros((4, LANES), F32)], axis=0
         )
-        change = dot_tn(carried, response, HIGHEST)
+        change = dot3(dot_tn, carried, response, 0, 0)
         value = start_ref[f * rows : (f + 1) * rows] - change
         for i in range(cells_i):
-            out_ref[f, i] = value[i * rows_j : i * rows_j + cells_j]
+            out_ref[f, :, i, :] = value[i * rows_j : i * rows_j + cells_j]
 
 
 def finish(mine, start, got, carry, shape):
@@ -515,6 +584,7 @@
     block = lax.axis_index("block").astype(jnp.int32).reshape(1)
     base = 4 * cells_i
 
+    adjoint, residual = (x.transpose(0, 2, 1, 3) for x in (adjoint, residual))
     outgoing = gather(send_count.reshape(owners), receptor_cell[0, 0], adjoint)
     incoming = lax.all_to_all(outgoing, "block", split_axis=0, concat_axis=0, tiled=True)
 
@@ -523,7 +593,7 @@
     edge = couplings[0, 0, 0:2].reshape(6, fields).T
     edge = jnp.pad(edge, ((0, 8 - fields), (0, LANES - 6)))
     i_tiles = jnp.concatenate([square, edge[None]], axis=0)
-    own, k_tile, k_map, k_rows, k_carry = prepare(couplings[0, 0], i_tiles, k_factors[0], cells_i)
+    own = prepare_i(i_tiles, cells_i)
 
     def shifted(value, shift):
         return lax.ppermute(value, "line", [(s, (s + shift) % peers) for s in range(peers)])
@@ -533,11 +603,14 @@
         line, i_tiles, incoming, donor_cell[0, 0], donor_weight[0, 0], residual, tiles, base
     )
     got = [ends[0]] + [shifted(ends[m], m) for m in range(1, peers)]
+    couple = couplings[0, 0].transpose(1, 0, 2)
+    factors, _ = lax.optimization_barrier((k_factors[0], ends[0]))
+    k_tile, k_map, k_rows, k_carry = prepare_k(couple, factors)
     start, message = middle(
         line, own, start, k_map, k_rows, k_tile, tiles, got, base, owners, fields, cells_i
     )
     message = lax.all_to_all(message, "block", split_axis=0, concat_axis=0, tiled=True)
-    return finish(block, start, message, k_carry, residual.shape)
+    return finish(block, start, message, k_carry, residual.shape).transpose(0, 2, 1, 3)
 
 
 def solution(mesh):

time: 90.5 us -> 75.9 us (0.84)
  local copies, waits for them, and re-layouts: 8.72 us -> 3 us
  Pallas kernels: 47.5 us -> 42.6 us
  starting transfers between devices: 18.5 us -> 15.8 us
  waiting for transfers between devices: 14.7 us -> 13.2 us
    pallas_call x1, Pallas kernels: 22.8 us -> 18.9 us  [scatter(): pl.pallas_call(functools.partial(scatter_kernel, peers=peers, chunk=chunk...]
    unnamed x24 -> x18, local copies, waits for them, and re-layouts: 5.33 us -> 2.05 us
    ppermute x6, waiting for transfers between devices: 6.02 us -> 3.02 us  [shifted(): lax.ppermute(value, 'line', [(s, (s + shift) % peers) for s in range(peer...]
    all_to_all x1, waiting for transfers between devices: 0.01 us -> 2.87 us  [per_device(): lax.all_to_all(outgoing, 'block', split_axis=0, concat_axis=0, tiled=True)]
    all_to_all x1, starting transfers between devices: 6 us -> 3.68 us  [per_device(): lax.all_to_all(message, 'block', split_axis=0, concat_axis=0, tiled=True)]
    pallas_call x1 -> x0, local copies, waits for them, and re-layouts: 1.85 us -> none  [finish(): pl.pallas_call(finish_kernel, out_shape=jax.ShapeDtypeStruct(shape, F32),...]
    all_to_all x1, waiting for transfers between devices: 8.64 us -> 7.34 us  [per_device(): lax.all_to_all(message, 'block', split_axis=0, concat_axis=0, tiled=True)]
    pallas_call x1 -> x2, Pallas kernels: 8.4 us -> 7.22 us  [the longest x1 5.73 us: prepare_k(): pl.pallas_call(prepare_k_kernel, out_shape=(jax.ShapeDtypeStruct((8, LANE...]
  transfers between devices with their start and end apart: 8 -> 8, of which waited for: 5 -> 4; matrix products, arithmetic and copies ran while one was open for 3% -> 1% of each run, Pallas kernels for 9% -> 10%
where the time goes in v2:
time: 75.9 us; the launch traced here: 75.3 us
  Pallas kernels  42.6 us (56%)
  starting transfers between devices  15.8 us (21%)
  waiting for transfers between devices  13.2 us (17%)
  local copies, waits for them, and re-layouts  3 us (4%)
    pallas_call x1, Pallas kernels, scatter(): pl.pallas_call(functools.partial(scatter_kernel, peers=peers, chunk=chunk...  18.9 us
    pallas_call x1, Pallas kernels, gather(): pl.pallas_call(functools.partial(gather_kernel, chunk=chunk), out_shape=j...  11.2 us
    all_to_all x1, waiting for transfers between devices, per_device(): lax.all_to_all(message, 'block', split_axis=0, concat_axis=0, tiled=True)  7.34 us
    all_to_all x1, starting transfers between devices, per_device(): lax.all_to_all(outgoing, 'block', split_axis=0, concat_axis=0, tiled=True)  6.49 us
    pallas_call x1, Pallas kernels, prepare_k(): pl.pallas_call(prepare_k_kernel, out_shape=(jax.ShapeDtypeStruct((8, LANE...  5.73 us
    ppermute x6, starting transfers between devices, shifted(): lax.ppermute(value, 'line', [(s, (s + shift) % peers) for s in range(peer...  5.64 us
    all_to_all x1, starting transfers between devices, per_device(): lax.all_to_all(message, 'block', split_axis=0, concat_axis=0, tiled=True)  3.68 us
    ppermute x6, waiting for transfers between devices, shifted(): lax.ppermute(value, 'line', [(s, (s + shift) % peers) for s in range(peer...  3.02 us
  transfers between devices with their start and end apart: 8, of which 4 were waited for; matrix products, arithmetic and copies ran while one was open for 1% of the time, Pallas kernels for 10%

profile of v2, /device:TPU:0, one launch (start us, length us, event | category | flops | bytes accessed | tf_op | source)
XLA Modules:
  0.0 75.3 jit_solution(4441576493689036797)
XLA Ops:
  0.0 11.2 %gather.1 = f32[8,96,128]{2,1,0:T(8,128)} custom-call(s32[8]{0:T(128)} %bitcast.28, s32[8,2048]{1,0:T(8,128)} %bitcast.24, f32[6,15,8,128]{3,2,1,0:T(8,128)} %bitcast.21), custom_call_target="tpu_custom_call" | custom-call | tf_op jit(solution)/shard_map/gather/pallas_call | solution.py:144
  11.2 6.5 %all-to-all-start = ((f32[8,96,128]{2,1,0:T(8,128)}), f32[8,96,128]{2,1,0:T(8,128)S(1)}, u32[]{:S(2)}, u32[]{:S(2)}) async-start(f32[8,96,128]{2,1,0:T(8,128)} %gather.1), calls=%async_computation | async-start | bytes 786432 | tf_op jit(solution)/shard_map/all_to_all | solution.py:589
  17.7 0.7 slice-done
  18.4 0.1 copy.17
  18.5 0.1 reshape.13
  18.6 0.1 reshape.12
  18.7 0.6 select_maximum_fusion.i_ref.refs_1_
  19.3 1.5 %prepare_i.1.refs_6_.refs_1_ = f32[8,128]{1,0:T(8,128)} custom-call(f32[3,8,128]{2,1,0:T(8,128)} %select_maximum_fusion.i_ref.refs_1_), custom_call_target="tpu_custom_call" | custom-call | tf_op jit(solution)/shard_map/prepare_i/pallas_call | solution.py:203
  20.7 0.6 collective-permute-start.2
  21.3 1.9 %collective-permute-start.1 = (f32[8,128]{1,0:T(8,128)}, f32[8,128]{1,0:T(8,128)S(1)}, u32[]{:S(2)}, u32[]{:S(2)}) collective-permute-start(f32[8,128]{1,0:T(8,128)} %prepare_i.1.refs_6_.refs_1_), channel_id=1, source_target_pairs={{0,16},{8,24},{16,0},{24,8},{1,17},{9,25},{17,1},{25,9},{2,18},{10... | collective-permute-start | bytes 12296 | tf_op jit(solution)/shard_map/ppermute | solution.py:599
  23.2 0.2 collective-permute-start
  23.4 0.0 collective-permute-done.2.refs_9_
  23.4 1.7 %collective-permute-done.1.refs_8_ = f32[8,128]{1,0:T(8,128)S(1)} collective-permute-done((f32[8,128]{1,0:T(8,128)}, f32[8,128]{1,0:T(8,128)S(1)}, u32[]{:S(2)}, u32[]{:S(2)}) %collective-permute-start.1) | collective-permute-done | bytes 4128 | tf_op jit(solution)/shard_map/ppermute | solution.py:599
  25.1 1.3 %collective-permute-done.refs_7_ = f32[8,128]{1,0:T(8,128)S(1)} collective-permute-done((f32[8,128]{1,0:T(8,128)}, f32[8,128]{1,0:T(8,128)S(1)}, u32[]{:S(2)}, u32[]{:S(2)}) %collective-permute-start) | collective-permute-done | bytes 4128 | tf_op jit(solution)/shard_map/ppermute | solution.py:599
  26.4 2.9 %all-to-all-done.refs_2_ = f32[8,96,128]{2,1,0:T(8,128)S(1)} async-done(((f32[8,96,128]{2,1,0:T(8,128)}), f32[8,96,128]{2,1,0:T(8,128)S(1)}, u32[]{:S(2)}, u32[]{:S(2)}) %all-to-all-start) | async-done | bytes 393248 | tf_op jit(solution)/shard_map/all_to_all | solution.py:589
  29.3 0.7 copy-done
  30.0 18.9 %scatter.1 = (f32[768,128]{1,0:T(8,128)}, f32[192,128]{1,0:T(8,128)}, f32[192,128]{1,0:T(8,128)}, f32[192,128]{1,0:T(8,128)}, f32[192,128]{1,0:T(8,128)}) custom-call(s32[1]{0:T(128)} %bitcast.1.refs_0_, f32[3,8,128]{2,1,0:T(8,128)} %select_maximum_fusion.i_ref.refs_1_, f32[8,96,128]{2,1,0:T(8,128)} %copy-done, s32[8,2048]{1,0:T(8,128)} %bitcast.25, ...), custom_call_target="tpu_custom_call" | custom-call | tf_op jit(solution)/shard_map/scatter/pallas_call | solution.py:420
  49.0 0.0 collective-permute-start.3
  49.0 1.5 %collective-permute-start.4 = (f32[192,128]{1,0:T(8,128)}, f32[192,128]{1,0:T(8,128)S(1)}, u32[]{:S(2)}, u32[]{:S(2)}) collective-permute-start(f32[192,128]{1,0:T(8,128)} %get-tuple-element.24), channel_id=1, source_target_pairs={{0,16},{8,24},{16,0},{24,8},{1,17},{9,25},{17,1},{25,9},{2,18},{10... | collective-permute-start | bytes 294920 | tf_op jit(solution)/shard_map/ppermute | solution.py:599
  50.5 1.4 %collective-permute-start.5 = (f32[192,128]{1,0:T(8,128)}, f32[192,128]{1,0:T(8,128)S(1)}, u32[]{:S(2)}, u32[]{:S(2)}) collective-permute-start(f32[192,128]{1,0:T(8,128)} %get-tuple-element.25), channel_id=1, source_target_pairs={{0,24},{8,0},{16,8},{24,16},{1,25},{9,1},{17,9},{25,17},{2,26},{10... | collective-permute-start | bytes 294920 | tf_op jit(solution)/shard_map/ppermute | solution.py:599
  51.9 5.7 %prepare_k.1 = (f32[8,128]{1,0:T(8,128)}, f32[6,128,128]{2,1,0:T(8,128)}, f32[6,8,128]{2,1,0:T(8,128)}, f32[4,8,128]{2,1,0:T(8,128)}) custom-call(f32[3,4,6]{2,1,0:T(4,128)} %bitcast.27, f32[2,6,128,128]{3,2,1,0:T(8,128)} %bitcast.20), custom_call_target="tpu_custom_call" | custom-call | tf_op jit(solution)/shard_map/prepare_k/pallas_call | solution.py:273
  57.7 0.0 collective-permute-done.3.refs_11_
  57.7 0.0 collective-permute-done.4.refs_12_
  57.7 0.0 collective-permute-done.5.refs_13_
  57.7 0.6 copy-done.2
  58.3 0.0 copy-done.3
  58.3 0.0 copy-done.4
  58.4 2.8 %middle.1 = (f32[768,128]{1,0:T(8,128)}, f32[8,32,128]{2,1,0:T(8,128)}) custom-call(s32[1]{0:T(128)} %bitcast.1.refs_0_, f32[8,128]{1,0:T(8,128)} %prepare_i.1.refs_6_.refs_1_, f32[768,128]{1,0:T(8,128)} %get-tuple-element.17.refs_2_, f32[6,128,128]{2,1,0:T(8,128)} %get-tuple-element.20.refs_3_, f32[6,8,128]{2,1,0:T(8,128)} %get-tuple-element.21.refs_4_, ...), custom_call_target="tpu_custom_call" | custom-call | tf_op jit(solution)/shard_map/middle/pallas_call | solution.py:498
  61.2 3.7 %all-to-all-start.1 = ((f32[8,32,128]{2,1,0:T(8,128)}), f32[8,32,128]{2,1,0:T(8,128)S(1)}, u32[]{:S(2)}, u32[]{:S(2)}) async-start(f32[8,32,128]{2,1,0:T(8,128)} %get-tuple-element.27), calls=%async_computation.1 | async-start | bytes 262144 | tf_op jit(solution)/shard_map/all_to_all | solution.py:612
  64.9 7.3 %all-to-all-done.1.got_ref = f32[8,32,128]{2,1,0:T(8,128)S(1)} async-done(((f32[8,32,128]{2,1,0:T(8,128)}), f32[8,32,128]{2,1,0:T(8,128)S(1)}, u32[]{:S(2)}, u32[]{:S(2)}) %all-to-all-start.1) | async-done | bytes 131104 | tf_op jit(solution)/shard_map/all_to_all | solution.py:612
  72.2 0.6 copy-done.1
  72.9 2.4 %finish.1 = f32[6,15,8,128]{3,2,1,0:T(8,128)} custom-call(s32[1]{0:T(128)} %bitcast.mine_ref, f32[768,128]{1,0:T(8,128)} %get-tuple-element.26.start_ref, f32[8,32,128]{2,1,0:T(8,128)} %copy-done.1, f32[4,8,128]{2,1,0:T(8,128)} %get-tuple-element.28.carry_ref), custom_call_target="tpu_custom_call" | custom-call | tf_op jit(solution)/shard_map/finish/pallas_call | solution.py:560
  (15 shorter events, 0.0 us)
Async XLA Ops:
  11.2 7.4 %copy-start.5 = (f32[1,2,6,8,8]{4,3,2,1,0:T(8,128)S(1)}, f32[1,2,6,8,8]{4,3,2,1,0:T(8,128)}, u32[]{:S(2)}) copy-start(f32[1,2,6,8,8]{4,3,2,1,0:T(8,128)} %param.11) | copy-start | bytes 9220
  11.2 18.1 %all-to-all-start = ((f32[8,96,128]{2,1,0:T(8,128)}), f32[8,96,128]{2,1,0:T(8,128)S(1)}, u32[]{:S(2)}, u32[]{:S(2)}) async-start(f32[8,96,128]{2,1,0:T(8,128)} %gather.1), calls=%async_computation | async-start | bytes 786432 | tf_op jit(solution)/shard_map/all_to_all | solution.py:589
  17.7 0.7 slice-start
  20.7 2.7 %collective-permute-start.2 = (f32[8,128]{1,0:T(8,128)}, f32[8,128]{1,0:T(8,128)S(1)}, u32[]{:S(2)}, u32[]{:S(2)}) collective-permute-start(f32[8,128]{1,0:T(8,128)} %prepare_i.1.refs_6_.refs_1_), channel_id=1, source_target_pairs={{0,24},{8,0},{16,8},{24,16},{1,25},{9,1},{17,9},{25,17},{2,26},{10... | collective-permute-start | bytes 12296 | tf_op jit(solution)/shard_map/ppermute | solution.py:599
  21.3 3.8 %collective-permute-start.1 = (f32[8,128]{1,0:T(8,128)}, f32[8,128]{1,0:T(8,128)S(1)}, u32[]{:S(2)}, u32[]{:S(2)}) collective-permute-start(f32[8,128]{1,0:T(8,128)} %prepare_i.1.refs_6_.refs_1_), channel_id=1, source_target_pairs={{0,16},{8,24},{16,0},{24,8},{1,17},{9,25},{17,1},{25,9},{2,18},{10... | collective-permute-start | bytes 12296 | tf_op jit(solution)/shard_map/ppermute | solution.py:599
  23.2 3.2 %collective-permute-start = (f32[8,128]{1,0:T(8,128)}, f32[8,128]{1,0:T(8,128)S(1)}, u32[]{:S(2)}, u32[]{:S(2)}) collective-permute-start(f32[8,128]{1,0:T(8,128)} %prepare_i.1.refs_6_.refs_1_), channel_id=1, source_target_pairs={{0,8},{8,16},{16,24},{24,0},{1,9},{9,17},{17,25},{25,1},{2,10},{10... | collective-permute-start | bytes 12296 | tf_op jit(solution)/shard_map/ppermute | solution.py:599
  23.4 5.9 %copy-start.6 = (f32[8,128]{1,0:T(8,128)}, f32[8,128]{1,0:T(8,128)S(1)}, u32[]{:S(2)}) copy-start(f32[8,128]{1,0:T(8,128)S(1)} %collective-permute-done.2.refs_9_) | copy-start | bytes 12292
  25.1 4.2 %copy-start.7 = (f32[8,128]{1,0:T(8,128)}, f32[8,128]{1,0:T(8,128)S(1)}, u32[]{:S(2)}) copy-start(f32[8,128]{1,0:T(8,128)S(1)} %collective-permute-done.1.refs_8_) | copy-start | bytes 12292
  26.4 2.9 %copy-start.8 = (f32[8,128]{1,0:T(8,128)}, f32[8,128]{1,0:T(8,128)S(1)}, u32[]{:S(2)}) copy-start(f32[8,128]{1,0:T(8,128)S(1)} %collective-permute-done.refs_7_) | copy-start | bytes 12292
  29.3 0.7 copy-start
  49.0 8.7 %collective-permute-start.3 = (f32[192,128]{1,0:T(8,128)}, f32[192,128]{1,0:T(8,128)S(1)}, u32[]{:S(2)}, u32[]{:S(2)}) collective-permute-start(f32[192,128]{1,0:T(8,128)} %get-tuple-element.23), channel_id=1, source_target_pairs={{0,8},{8,16},{16,24},{24,0},{1,9},{9,17},{17,25},{25,1},{2,10},{10... | collective-permute-start | bytes 294920 | tf_op jit(solution)/shard_map/ppermute | solution.py:599
  49.0 8.7 %collective-permute-start.4 = (f32[192,128]{1,0:T(8,128)}, f32[192,128]{1,0:T(8,128)S(1)}, u32[]{:S(2)}, u32[]{:S(2)}) collective-permute-start(f32[192,128]{1,0:T(8,128)} %get-tuple-element.24), channel_id=1, source_target_pairs={{0,16},{8,24},{16,0},{24,8},{1,17},{9,25},{17,1},{25,9},{2,18},{10... | collective-permute-start | bytes 294920 | tf_op jit(solution)/shard_map/ppermute | solution.py:599
  50.5 7.2 %collective-permute-start.5 = (f32[192,128]{1,0:T(8,128)}, f32[192,128]{1,0:T(8,128)S(1)}, u32[]{:S(2)}, u32[]{:S(2)}) collective-permute-start(f32[192,128]{1,0:T(8,128)} %get-tuple-element.25), channel_id=1, source_target_pairs={{0,24},{8,0},{16,8},{24,16},{1,25},{9,1},{17,9},{25,17},{2,26},{10... | collective-permute-start | bytes 294920 | tf_op jit(solution)/shard_map/ppermute | solution.py:599
  57.7 0.6 copy-start.2
  57.7 0.7 copy-start.3
  57.7 0.7 copy-start.4
  61.2 11.0 %all-to-all-start.1 = ((f32[8,32,128]{2,1,0:T(8,128)}), f32[8,32,128]{2,1,0:T(8,128)S(1)}, u32[]{:S(2)}, u32[]{:S(2)}) async-start(f32[8,32,128]{2,1,0:T(8,128)} %get-tuple-element.27), calls=%async_computation.1 | async-start | bytes 262144 | tf_op jit(solution)/shard_map/all_to_all | solution.py:612
  72.2 0.7 copy-start.1

commit v3 on v2

--- a/solution.py
+++ b/solution.py
@@ -78,12 +78,16 @@
     return i, row - i * cells_j, k
 
 
+def near(x):
+    return pltpu.with_memory_space_constraint(x, pltpu.VMEM)
+
+
 def col(x, c):
     return jnp.broadcast_to(x[:, c : c + 1], x.shape)
 
 
 def gather_kernel(
-    count_ref, cell_ref, field_ref, out_ref, high_ref, low_ref, place_ref, *, chunk
+    mine_ref, count_ref, cell_ref, field_ref, out_ref, own_ref, high_ref, low_ref, place_ref, *, chunk
 ):
     fields, cells_j, cells_i, _ = field_ref.shape
     owners, capacity = cell_ref.shape
@@ -135,28 +139,33 @@
         return lax.fori_loop(0, lax.div(count + (chunk - 1), chunk), chunk_body, carry)
 
     lax.fori_loop(0, owners, owner_body, 0)
-
-
-def gather(count, cell, field, chunk=512):
+    own_ref[...] = out_ref[mine_ref[0]]
+
+
+def gather(mine, count, cell, field, chunk=512):
     fields, _, cells_i, _ = field.shape
     owners, capacity = cell.shape
     table = (fields * cells_i // 2 * 16, 2 * LANES)
     return pl.pallas_call(
         functools.partial(gather_kernel, chunk=chunk),
-        out_shape=jax.ShapeDtypeStruct((owners, fields * capacity // LANES, LANES), F32),
+        out_shape=(
+            pltpu.VMEM((owners, fields * capacity // LANES, LANES), F32),
+            pltpu.VMEM((fields * capacity // LANES, LANES), F32),
+        ),
         in_specs=[
+            pl.BlockSpec(memory_space=pltpu.SMEM),
             pl.BlockSpec(memory_space=pltpu.SMEM),
             pl.BlockSpec(memory_space=pltpu.VMEM),
             pl.BlockSpec(memory_space=pltpu.VMEM),
         ],
-        out_specs=pl.BlockSpec(memory_space=pltpu.VMEM),
+        out_specs=(pl.BlockSpec(memory_space=pltpu.VMEM),) * 2,
         scratch_shapes=[
             pltpu.VMEM(table, BF16),
             pltpu.VMEM(table, BF16),
             pltpu.VMEM((2 * LANES, LANES), BF16),
         ],
         name="gather",
-    )(count, cell, field)
+    )(mine, count, cell, field)
 
 
 def lay_out(entries):
@@ -202,7 +211,7 @@
 def prepare_i(i_tiles, cells_i):
     return pl.pallas_call(
         functools.partial(prepare_i_kernel, cells_i=cells_i),
-        out_shape=jax.ShapeDtypeStruct((8, LANES), F32),
+        out_shape=pltpu.VMEM((8, LANES), F32),
         in_specs=[pl.BlockSpec(memory_space=pltpu.VMEM)],
         out_specs=pl.BlockSpec(memory_space=pltpu.VMEM),
         name="prepare_i",
@@ -273,10 +282,10 @@
     return pl.pallas_call(
         prepare_k_kernel,
         out_shape=(
-            jax.ShapeDtypeStruct((8, LANES), F32),
-            jax.ShapeDtypeStruct((fields, length, length), F32),
-            jax.ShapeDtypeStruct((fields, 8, length), F32),
-            jax.ShapeDtypeStruct((4, 8, length), F32),
+            pltpu.VMEM((8, LANES), F32),
+            pltpu.VMEM((fields, length, length), F32),
+            pltpu.VMEM((fields, 8, length), F32),
+            pltpu.VMEM((4, 8, length), F32),
         ),
         in_specs=[
             pl.BlockSpec(memory_space=pltpu.SMEM),
@@ -309,68 +318,122 @@
     return total
 
 
+def spread_slots(total_ref, place_ref, value_of, cell_ref, weight_ref, b, c, sizes, chunk):
+    fields, cells_j, cells_i = sizes
+    rows_j = 16
+    per = chunk // LANES
+    start = pl.multiple_of(c * chunk, chunk)
+    cell = cell_ref[pl.ds(b, 1), pl.ds(start, chunk)]
+    x = weight_ref[0, pl.ds(b, 1), pl.ds(start, chunk)]
+    y = weight_ref[1, pl.ds(b, 1), pl.ds(start, chunk)]
+    z = weight_ref[2, pl.ds(b, 1), pl.ds(start, chunk)]
+    i, j, k = split_cell(cell, cells_i, cells_j)
+
+    def hat(size, at, t):
+        place = lax.broadcasted_iota(jnp.int32, (size, chunk), 0)
+        return jnp.where(place == at, 1.0 - t, jnp.where(place == at + 1, t, 0.0))
+
+    along_i = hat(cells_i, i, x)
+    along_j = hat(rows_j, j, y)
+    first = rows_of(k.astype(F32), 16, BF16)
+    second = rows_of((k + 1).astype(F32), 16, BF16)
+    far = split(rows_of(z, 16, F32))
+    close = split(rows_of(1.0 - z, 16, F32))
+    zero = jnp.zeros((16, chunk), BF16)
+    place = place_ref[...]
+    along_k = []
+    for part in range(2):
+        for r in range(LANES // 16):
+            here = jnp.concatenate([place[16 * r : 16 * r + 16]] * per, axis=1)
+            weight = jnp.where(here == second, far[part], zero)
+            along_k.append(jnp.where(here == first, close[part], weight))
+    along_k = jnp.concatenate(along_k, axis=0)
+    blocks = []
+    for f in range(fields):
+        value = jnp.concatenate([value_of(f, c * per + q) for q in range(per)], axis=1)
+        scaled = along_j * value
+        blocks += [along_i * scaled[q : q + 1] for q in range(cells_j)]
+    high, low = split(jnp.concatenate(blocks, axis=0))
+    total_ref[...] += dot_nt(
+        jnp.concatenate([high, low], axis=1), jnp.concatenate([along_k, along_k], axis=1)
+    )
+
+
+def scatter_own_kernel(
+    mine_ref, got_ref, cell_ref, weight_ref, total_ref, place_ref, *, sizes, chunk
+):
+    capacity = cell_ref.shape[1]
+    slot_rows = capacity // LANES
+    total_ref[...] = jnp.zeros(total_ref.shape, F32)
+    place_ref[...] = places(LANES, LANES)
+    mine = mine_ref[0]
+
+    def chunk_body(c, carry):
+        spread_slots(
+            total_ref,
+            place_ref,
+            lambda f, q: got_ref[pl.ds(f * slot_rows + q, 1), :],
+            cell_ref,
+            weight_ref,
+            mine,
+            c,
+            sizes,
+            chunk,
+        )
+        return carry
+
+    lax.fori_loop(0, capacity // chunk, chunk_body, 0)
+
+
+def scatter_own(mine, got, cell, weight, sizes, chunk=2048):
+    vmem = pl.BlockSpec(memory_space=pltpu.VMEM)
+    smem = pl.BlockSpec(memory_space=pltpu.SMEM)
+    fields, cells_j, cells_i = sizes
+    return pl.pallas_call(
+        functools.partial(scatter_own_kernel, sizes=sizes, chunk=chunk),
+        out_shape=pltpu.VMEM((fields * cells_i * cells_j, 2 * LANES), F32),
+        in_specs=[smem, vmem, vmem, vmem],
+        out_specs=vmem,
+        scratch_shapes=[pltpu.VMEM((LANES, LANES), BF16)],
+        name="scatter_own",
+    )(mine, near(got), cell, weight)
+
+
 def scatter_kernel(*refs, peers, chunk, base):
-    mine_ref, solve_ref, got_ref, cell_ref, weight_ref, residual_ref = refs[:6]
-    tile_refs = refs[6 : 6 + peers]
-    start_ref = refs[6 + peers]
-    send_refs = refs[7 + peers : 7 + 2 * peers]
-    total_ref, place_ref, fold_ref = refs[7 + 2 * peers :]
+    mine_ref, block_ref, solve_ref, begun_ref, got_ref, cell_ref, weight_ref, residual_ref = refs[:8]
+    refs = refs[8:]
+    tile_refs = refs[:peers]
+    start_ref = refs[peers]
+    send_refs = refs[1 + peers : 1 + 2 * peers]
+    total_ref, place_ref, fold_ref = refs[1 + 2 * peers :]
     fields, cells_j, cells_i, _ = residual_ref.shape
     sources, capacity = cell_ref.shape
     rows_j = 16
-    per = chunk // LANES
     slot_rows = capacity // LANES
-    total_ref[...] = jnp.zeros(total_ref.shape, F32)
+    total_ref[...] = begun_ref[...]
     place_ref[...] = places(LANES, LANES)
-
-    def source_body(b, carry):
+    own = block_ref[0]
+
+    def source_body(at, carry):
+        b = at + (at >= own).astype(jnp.int32)
+
         def chunk_body(c, carry):
-            start = pl.multiple_of(c * chunk, chunk)
-            cell = cell_ref[pl.ds(b, 1), pl.ds(start, chunk)]
-            x = weight_ref[0, pl.ds(b, 1), pl.ds(start, chunk)]
-            y = weight_ref[1, pl.ds(b, 1), pl.ds(start, chunk)]
-            z = weight_ref[2, pl.ds(b, 1), pl.ds(start, chunk)]
-            i, j, k = split_cell(cell, cells_i, cells_j)
-
-            def hat(size, at, t):
-                place = lax.broadcasted_iota(jnp.int32, (size, chunk), 0)
-                return jnp.where(place == at, 1.0 - t, jnp.where(place == at + 1, t, 0.0))
-
-            along_i = hat(cells_i, i, x)
-            along_j = hat(rows_j, j, y)
-            first = rows_of(k.astype(F32), 16, BF16)
-            second = rows_of((k + 1).astype(F32), 16, BF16)
-            far = split(rows_of(z, 16, F32))
-            near = split(rows_of(1.0 - z, 16, F32))
-            zero = jnp.zeros((16, chunk), BF16)
-            place = place_ref[...]
-            along_k = []
-            for part in range(2):
-                for r in range(LANES // 16):
-                    here = jnp.concatenate([place[16 * r : 16 * r + 16]] * per, axis=1)
-                    weight = jnp.where(here == second, far[part], zero)
-                    along_k.append(jnp.where(here == first, near[part], weight))
-            along_k = jnp.concatenate(along_k, axis=0)
-            blocks = []
-            for f in range(fields):
-                value = jnp.concatenate(
-                    [
-                        got_ref[b, pl.ds(f * slot_rows + c * per + q, 1), :]
-                        for q in range(per)
-                    ],
-                    axis=1,
-                )
-                scaled = along_j * value
-                blocks += [along_i * scaled[q : q + 1] for q in range(cells_j)]
-            high, low = split(jnp.concatenate(blocks, axis=0))
-            total_ref[...] += dot_nt(
-                jnp.concatenate([high, low], axis=1), jnp.concatenate([along_k, along_k], axis=1)
+            spread_slots(
+                total_ref,
+                place_ref,
+                lambda f, q: got_ref[b, pl.ds(f * slot_rows + q, 1), :],
+                cell_ref,
+                weight_ref,
+                b,
+                c,
+                (fields, cells_j, cells_i),
+                chunk,
             )
             return carry
 
         return lax.fori_loop(0, capacity // chunk, chunk_body, carry)
 
-    lax.fori_loop(0, sources, source_body, 0)
+    lax.fori_loop(0, sources - 1, source_body, 0)
 
     fold_ref[...] = total_ref[:, :LANES] + total_ref[:, LANES:]
     mine = mine_ref[0]
@@ -411,7 +474,7 @@
             send_refs[shift][at : at + rows_j] = jnp.where(ahead, e1, h1)
 
 
-def scatter(mine, solve_tiles, got, cell, weight, residual, tiles, base, chunk=1024):
+def scatter(mine, block, solve_tiles, begun, got, cell, weight, residual, tiles, base, chunk=2048):
     fields, cells_j, cells_i, _ = residual.shape
     peers = len(tiles)
     rows = fields * cells_i * 16
@@ -419,9 +482,9 @@
     smem = pl.BlockSpec(memory_space=pltpu.SMEM)
     return pl.pallas_call(
         functools.partial(scatter_kernel, peers=peers, chunk=chunk, base=base),
-        out_shape=(jax.ShapeDtypeStruct((rows, LANES), F32),)
-        + (jax.ShapeDtypeStruct((2 * fields * 16, LANES), F32),) * peers,
-        in_specs=[smem, smem, vmem, vmem, vmem, vmem] + [vmem] * peers,
+        out_shape=(pltpu.VMEM((rows, LANES), F32),)
+        + (pltpu.VMEM((2 * fields * 16, LANES), F32),) * peers,
+        in_specs=[smem, smem, smem] + [vmem] * (5 + peers),
         out_specs=(vmem,) * (1 + peers),
         scratch_shapes=[
             pltpu.VMEM((fields * cells_i * cells_j, 2 * LANES), F32),
@@ -429,14 +492,14 @@
             pltpu.VMEM((fields * cells_i * cells_j, LANES), F32),
         ],
         name="scatter",
-    )(mine, solve_tiles, got, cell, weight, residual, *tiles)
+    )(mine, block, solve_tiles, near(begun), near(got), cell, weight, residual, *map(near, tiles))
 
 
 def middle_kernel(*refs, peers, base, fields, cells_i):
-    mine_ref, own_ref, start_ref, map_ref, rows_ref, k_tile_ref = refs[:6]
-    tile_refs = refs[6 : 6 + peers]
-    got_refs = refs[6 + peers : 6 + 2 * peers]
-    out_ref, send_ref, field_ref, end_ref = refs[6 + 2 * peers :]
+    mine_ref, own_ref, start_ref, rows_ref, k_tile_ref = refs[:5]
+    tile_refs = refs[5 : 5 + peers]
+    got_refs = refs[5 + peers : 5 + 2 * peers]
+    field_ref, send_ref, end_ref = refs[5 + 2 * peers :]
     rows_j = 16
     mine = mine_ref[0]
     tiles = [ref[...] for ref in tile_refs]
@@ -482,7 +545,6 @@
             value = value - own_ref[f, shift + 2 * p + 1] * after[1]
             field_ref[at : at + rows_j] = value
         block = field_ref[f * rows : (f + 1) * rows]
-        out_ref[f * rows : (f + 1) * rows] = product_nt(block, map_ref[f])
         ends = product_nt(rows_ref[f], block)
         for a in range(4):
             end_ref[a * fields + f : a * fields + f + 1, :] = ends[a : a + 1]
@@ -491,21 +553,40 @@
         send_ref[d] = end_ref[...]
 
 
-def middle(mine, own, start, k_map, k_rows, k_tile, tiles, got, base, owners, fields, cells_i):
+def middle(mine, own, start, k_rows, k_tile, tiles, got, base, owners, fields, cells_i):
     peers = len(tiles)
     vmem = pl.BlockSpec(memory_space=pltpu.VMEM)
     smem = pl.BlockSpec(memory_space=pltpu.SMEM)
     return pl.pallas_call(
         functools.partial(middle_kernel, peers=peers, base=base, fields=fields, cells_i=cells_i),
         out_shape=(
-            jax.ShapeDtypeStruct(start.shape, F32),
-            jax.ShapeDtypeStruct((owners, 4 * fields + 8, LANES), F32),
+            pltpu.VMEM(start.shape, F32),
+            pltpu.VMEM((owners, 4 * fields + 8, LANES), F32),
         ),
-        in_specs=[smem, smem] + [vmem] * (4 + 2 * peers),
+        in_specs=[smem, smem] + [vmem] * (3 + 2 * peers),
         out_specs=(vmem, vmem),
-        scratch_shapes=[pltpu.VMEM(start.shape, F32), pltpu.VMEM((4 * fields + 8, LANES), F32)],
+        scratch_shapes=[pltpu.VMEM((4 * fields + 8, LANES), F32)],
         name="middle",
-    )(mine, own, start, k_map, k_rows, k_tile, *tiles, *got)
+    )(mine, own, *map(near, (start, k_rows, k_tile, *tiles, *got)))
+
+
+def apply_k_kernel(field_ref, map_ref, out_ref):
+    fields = map_ref.shape[0]
+    rows = field_ref.shape[0] // fields
+    for f in range(fields):
+        at = slice(f * rows, (f + 1) * rows)
+        out_ref[at] = product_nt(field_ref[at], map_ref[f])
+
+
+def apply_k(field, k_map):
+    vmem = pl.BlockSpec(memory_space=pltpu.VMEM)
+    return pl.pallas_call(
+        apply_k_kernel,
+        out_shape=pltpu.VMEM(field.shape, F32),
+        in_specs=[vmem, vmem],
+        out_specs=vmem,
+        name="apply_k",
+    )(near(field), near(k_map))
 
 
 def finish_kernel(mine_ref, start_ref, got_ref, carry_ref, out_ref):
@@ -563,7 +644,7 @@
         in_specs=[smem, vmem, vmem, vmem],
         out_specs=vmem,
         name="finish",
-    )(mine, start, got, carry)
+    )(mine, near(start), near(got), near(carry))
 
 
 def per_device(
@@ -585,7 +666,7 @@
     base = 4 * cells_i
 
     adjoint, residual = (x.transpose(0, 2, 1, 3) for x in (adjoint, residual))
-    outgoing = gather(send_count.reshape(owners), receptor_cell[0, 0], adjoint)
+    outgoing, kept = gather(block, send_count.reshape(owners), receptor_cell[0, 0], adjoint)
     incoming = lax.all_to_all(outgoing, "block", split_axis=0, concat_axis=0, tiled=True)
 
     square = i_factors[0].reshape(2, fields, cells_i * cells_i)
@@ -599,17 +680,30 @@
         return lax.ppermute(value, "line", [(s, (s + shift) % peers) for s in range(peers)])
 
     tiles = [own] + [shifted(own, m) for m in range(1, peers)]
+    begun = scatter_own(
+        block, kept, donor_cell[0, 0], donor_weight[0, 0], (fields, cells_j, cells_i)
+    )
     start, *ends = scatter(
-        line, i_tiles, incoming, donor_cell[0, 0], donor_weight[0, 0], residual, tiles, base
+        line,
+        block,
+        i_tiles,
+        begun,
+        incoming,
+        donor_cell[0, 0],
+        donor_weight[0, 0],
+        residual,
+        tiles,
+        base,
     )
     got = [ends[0]] + [shifted(ends[m], m) for m in range(1, peers)]
     couple = couplings[0, 0].transpose(1, 0, 2)
     factors, _ = lax.optimization_barrier((k_factors[0], ends[0]))
     k_tile, k_map, k_rows, k_carry = prepare_k(couple, factors)
     start, message = middle(
-        line, own, start, k_map, k_rows, k_tile, tiles, got, base, owners, fields, cells_i
+        line, own, start, k_rows, k_tile, tiles, got, base, owners, fields, cells_i
     )
     message = lax.all_to_all(message, "block", split_axis=0, concat_axis=0, tiled=True)
+    start = apply_k(start, k_map)
     return finish(block, start, message, k_carry, residual.shape).transpose(0, 2, 1, 3)
 
 

time: 75.9 us -> 67.1 us (0.88)
  Pallas kernels: 42.6 us -> 37 us
  local copies, waits for them, and re-layouts: 3 us -> 0.95 us
  waiting for transfers between devices: 13.2 us -> 11.6 us
  starting transfers between devices: 15.8 us -> 16.7 us
    pallas_call x1, Pallas kernels: 18.9 us -> 14.2 us  [scatter(): pl.pallas_call(functools.partial(scatter_kernel, peers=peers, chunk=chunk...]
    ppermute x6, waiting for transfers between devices: 3.02 us -> 0.21 us  [shifted(): lax.ppermute(value, 'line', [(s, (s + shift) % peers) for s in range(peer...]
    unnamed x18 -> x2, local copies, waits for them, and re-layouts: 2.05 us -> 0.01 us
    pallas_call x2 -> x4, Pallas kernels: 16.9 us -> 18.6 us  [the longest x1 10.4 us: gather(): pl.pallas_call(functools.partial(gather_kernel, chunk=chunk), out_shape=(...]
    all_to_all x1, waiting for transfers between devices: 2.87 us -> 4.48 us  [per_device(): lax.all_to_all(outgoing, 'block', split_axis=0, concat_axis=0, tiled=True)]
    pallas_call x1, Pallas kernels: 2.42 us -> 1.36 us  [finish(): pl.pallas_call(finish_kernel, out_shape=jax.ShapeDtypeStruct(shape, F32),...]
    all_to_all x1, starting transfers between devices: 6.49 us -> 7.41 us  [per_device(): lax.all_to_all(outgoing, 'block', split_axis=0, concat_axis=0, tiled=True)]
    pallas_call x1, Pallas kernels: 2.84 us -> 1.93 us  [middle(): pl.pallas_call(functools.partial(middle_kernel, peers=peers, base=base, f...]
  transfers between devices with their start and end apart: 8 -> 8, of which waited for: 4 -> 3; matrix products, arithmetic and copies ran while one was open for 1% -> 1% of each run, Pallas kernels for 10% -> 14%
where the time goes in v3:
time: 67.1 us; the launch traced here: 67 us
  Pallas kernels  37 us (55%)
  starting transfers between devices  16.7 us (25%)
  waiting for transfers between devices  11.6 us (17%)
  local copies, waits for them, and re-layouts  0.95 us (1%)
    pallas_call x1, Pallas kernels, scatter(): pl.pallas_call(functools.partial(scatter_kernel, peers=peers, chunk=chunk...  14.2 us
    pallas_call x1, Pallas kernels, gather(): pl.pallas_call(functools.partial(gather_kernel, chunk=chunk), out_shape=(...  10.4 us
    all_to_all x1, starting transfers between devices, per_device(): lax.all_to_all(outgoing, 'block', split_axis=0, concat_axis=0, tiled=True)  7.41 us
    all_to_all x1, waiting for transfers between devices, per_device(): lax.all_to_all(message, 'block', split_axis=0, concat_axis=0, tiled=True)  6.95 us
    ppermute x6, starting transfers between devices, shifted(): lax.ppermute(value, 'line', [(s, (s + shift) % peers) for s in range(peer...  5.62 us
    pallas_call x1, Pallas kernels, prepare_k(): pl.pallas_call(prepare_k_kernel, out_shape=(pltpu.VMEM((8, LANES), F32),...  5.12 us
    all_to_all x1, waiting for transfers between devices, per_device(): lax.all_to_all(outgoing, 'block', split_axis=0, concat_axis=0, tiled=True)  4.48 us
    all_to_all x1, starting transfers between devices, per_device(): lax.all_to_all(message, 'block', split_axis=0, concat_axis=0, tiled=True)  3.64 us
  transfers between devices with their start and end apart: 8, of which 3 were waited for; matrix products, arithmetic and copies ran while one was open for 1% of the time, Pallas kernels for 14%

profile of v3, /device:TPU:0, one launch (start us, length us, event | category | flops | bytes accessed | tf_op | source)
XLA Modules:
  0.0 67.0 jit_solution(9941931533741149987)
XLA Ops:
  0.0 10.4 %gather.1 = (f32[8,96,128]{2,1,0:T(8,128)}, f32[96,128]{1,0:T(8,128)S(1)}) custom-call(s32[1]{0:T(128)} %bitcast.mine_ref.refs_1_, s32[8]{0:T(128)} %bitcast.30, s32[8,2048]{1,0:T(8,128)} %bitcast.27, f32[6,15,8,128]{3,2,1,0:T(8,128)} %bitcast.23), custom_call_target="tpu_custom_call" | custom-call | tf_op jit(solution)/shard_map/gather/pallas_call | solution.py:149
  10.4 0.0 copy-start
  10.4 7.4 %all-to-all-start = ((f32[8,96,128]{2,1,0:T(8,128)}), f32[8,96,128]{2,1,0:T(8,128)S(1)}, u32[]{:S(2)}, u32[]{:S(2)}) async-start(f32[8,96,128]{2,1,0:T(8,128)} %get-tuple-element.20), calls=%async_computation | async-start | bytes 786432 | tf_op jit(solution)/shard_map/all_to_all | solution.py:670
  17.8 0.0 slice-start
  17.8 0.7 %slice-done = f32[1,1,2,3,6]{4,2,3,1,0:T(2,128)S(1)} async-done(((f32[1,1,4,3,6]{4,2,3,1,0:T(4,128)}), f32[1,1,2,3,6]{4,2,3,1,0:T(2,128)S(1)}, s32[]{:S(2)}) %slice-start) | async-done | bytes 168 | tf_op jit(solution)/shard_map/slice | solution.py:674
  18.5 0.1 copy.17
  18.6 0.1 reshape.13
  18.7 0.0 copy-done
  18.7 0.1 reshape.12
  18.8 0.6 select_maximum_fusion.i_ref.refs_2_
  19.4 0.9 %prepare_i.1.refs_8_.refs_1_.refs_5_ = f32[8,128]{1,0:T(8,128)S(1)} custom-call(f32[3,8,128]{2,1,0:T(8,128)} %select_maximum_fusion.i_ref.refs_2_), custom_call_target="tpu_custom_call" | custom-call | tf_op jit(solution)/shard_map/prepare_i/pallas_call | solution.py:212
  20.3 1.5 %collective-permute-start.2 = (f32[8,128]{1,0:T(8,128)S(1)}, f32[8,128]{1,0:T(8,128)S(1)}, u32[]{:S(2)}, u32[]{:S(2)}) collective-permute-start(f32[8,128]{1,0:T(8,128)S(1)} %prepare_i.1.refs_8_.refs_1_.refs_5_), channel_id=1, source_target_pairs={{0,24},{8,0},{16,8},{24,16},{1,25},{9,1},{17,9},{25,17},{2,26},{10... | collective-permute-start | bytes 12296 | tf_op jit(solution)/shard_map/ppermute | solution.py:680
  21.8 0.5 collective-permute-start.1
  22.3 0.2 collective-permute-start
  22.5 2.7 %scatter_own.1.refs_3_ = f32[720,256]{1,0:T(8,128)S(1)} custom-call(s32[1]{0:T(128)} %bitcast.mine_ref.refs_1_, f32[96,128]{1,0:T(8,128)S(1)} %get-tuple-element.19.got_ref, s32[8,2048]{1,0:T(8,128)} %bitcast.25, f32[3,8,2048]{2,1,0:T(8,128)} %bitcast.21), custom_call_target="tpu_custom_call" | custom-call | tf_op jit(solution)/shard_map/scatter_own/pallas_call | solution.py:392
  25.2 0.0 collective-permute-done.2.refs_11_.refs_8_
  25.2 0.2 collective-permute-done.1.refs_10_.refs_7_
  25.4 0.0 collective-permute-done.refs_9_.refs_6_
  25.4 4.5 %all-to-all-done.refs_4_ = f32[8,96,128]{2,1,0:T(8,128)S(1)} async-done(((f32[8,96,128]{2,1,0:T(8,128)}), f32[8,96,128]{2,1,0:T(8,128)S(1)}, u32[]{:S(2)}, u32[]{:S(2)}) %all-to-all-start) | async-done | bytes 393248 | tf_op jit(solution)/shard_map/all_to_all | solution.py:670
  29.9 14.2 %scatter.1 = (f32[768,128]{1,0:T(8,128)S(1)}, f32[192,128]{1,0:T(8,128)S(1)}, f32[192,128]{1,0:T(8,128)S(1)}, f32[192,128]{1,0:T(8,128)S(1)}, f32[192,128]{1,0:T(8,128)S(1)}) custom-call(s32[1]{0:T(128)} %bitcast.1.refs_0_, s32[1]{0:T(128)} %bitcast.mine_ref.refs_1_, f32[3,8,128]{2,1,0:T(8,128)} %select_maximum_fusion.i_ref.refs_2_, ...), custom_call_target="tpu_custom_call" | custom-call | tf_op jit(solution)/shard_map/scatter/pallas_call | solution.py:483
  44.1 0.1 collective-permute-start.3
  44.2 2.0 %collective-permute-start.4 = (f32[192,128]{1,0:T(8,128)S(1)}, f32[192,128]{1,0:T(8,128)S(1)}, u32[]{:S(2)}, u32[]{:S(2)}) collective-permute-start(f32[192,128]{1,0:T(8,128)S(1)} %get-tuple-element.27), channel_id=1, source_target_pairs={{0,16},{8,24},{16,0},{24,8},{1,17},{9,25},{17,1},{25,9},{2,18},{10... | collective-permute-start | bytes 294920 | tf_op jit(solution)/shard_map/ppermute | solution.py:680
  46.2 1.4 %collective-permute-start.5 = (f32[192,128]{1,0:T(8,128)S(1)}, f32[192,128]{1,0:T(8,128)S(1)}, u32[]{:S(2)}, u32[]{:S(2)}) collective-permute-start(f32[192,128]{1,0:T(8,128)S(1)} %get-tuple-element.28), channel_id=1, source_target_pairs={{0,24},{8,0},{16,8},{24,16},{1,25},{9,1},{17,9},{25,17},{2,26},{10... | collective-permute-start | bytes 294920 | tf_op jit(solution)/shard_map/ppermute | solution.py:680
  47.6 5.1 %prepare_k.1 = (f32[8,128]{1,0:T(8,128)S(1)}, f32[6,128,128]{2,1,0:T(8,128)S(1)}, f32[6,8,128]{2,1,0:T(8,128)S(1)}, f32[4,8,128]{2,1,0:T(8,128)S(1)}) custom-call(f32[3,4,6]{2,1,0:T(4,128)} %bitcast.29, f32[2,6,128,128]{3,2,1,0:T(8,128)} %bitcast.20), custom_call_target="tpu_custom_call" | custom-call | tf_op jit(solution)/shard_map/prepare_k/pallas_call | solution.py:282
  52.7 0.0 collective-permute-done.3.refs_10_
  52.7 0.0 collective-permute-done.4.refs_11_
  52.7 0.0 collective-permute-done.5.refs_12_
  52.7 1.9 %middle.1 = (f32[768,128]{1,0:T(8,128)S(1)}, f32[8,32,128]{2,1,0:T(8,128)}) custom-call(s32[1]{0:T(128)} %bitcast.1.refs_0_, f32[8,128]{1,0:T(8,128)S(1)} %prepare_i.1.refs_8_.refs_1_.refs_5_, f32[768,128]{1,0:T(8,128)S(1)} %get-tuple-element.21.refs_2_, f32[6,8,128]{2,1,0:T(8,128)S(1)} %get-tuple-element.24.refs_3_, ...), custom_call_target="tpu_custom_call" | custom-call | tf_op jit(solution)/shard_map/middle/pallas_call | solution.py:560
  54.7 3.6 %all-to-all-start.1 = ((f32[8,32,128]{2,1,0:T(8,128)}), f32[8,32,128]{2,1,0:T(8,128)S(1)}, u32[]{:S(2)}, u32[]{:S(2)}) async-start(f32[8,32,128]{2,1,0:T(8,128)} %get-tuple-element.31), calls=%async_computation.1 | async-start | bytes 262144 | tf_op jit(solution)/shard_map/all_to_all | solution.py:705
  58.3 0.4 apply_k.1.start_ref
  58.7 7.0 %all-to-all-done.1.got_ref = f32[8,32,128]{2,1,0:T(8,128)S(1)} async-done(((f32[8,32,128]{2,1,0:T(8,128)}), f32[8,32,128]{2,1,0:T(8,128)S(1)}, u32[]{:S(2)}, u32[]{:S(2)}) %all-to-all-start.1) | async-done | bytes 131104 | tf_op jit(solution)/shard_map/all_to_all | solution.py:705
  65.6 1.4 %finish.1 = f32[6,15,8,128]{3,2,1,0:T(8,128)} custom-call(s32[1]{0:T(128)} %bitcast.mine_ref.refs_1_, f32[768,128]{1,0:T(8,128)S(1)} %apply_k.1.start_ref, f32[8,32,128]{2,1,0:T(8,128)S(1)} %all-to-all-done.1.got_ref, f32[4,8,128]{2,1,0:T(8,128)S(1)} %get-tuple-element.32.carry_ref), custom_call_target="tpu_custom_call" | custom-call | tf_op jit(solution)/shard_map/finish/pallas_call | solution.py:641
  (1 shorter events, 0.0 us)
Async XLA Ops:
  10.4 8.3 %copy-start = (f32[1,2,6,8,8]{4,3,2,1,0:T(8,128)S(1)}, f32[1,2,6,8,8]{4,3,2,1,0:T(8,128)}, u32[]{:S(2)}) copy-start(f32[1,2,6,8,8]{4,3,2,1,0:T(8,128)} %param.11) | copy-start | bytes 9220
  10.4 19.5 %all-to-all-start = ((f32[8,96,128]{2,1,0:T(8,128)}), f32[8,96,128]{2,1,0:T(8,128)S(1)}, u32[]{:S(2)}, u32[]{:S(2)}) async-start(f32[8,96,128]{2,1,0:T(8,128)} %get-tuple-element.20), calls=%async_computation | async-start | bytes 786432 | tf_op jit(solution)/shard_map/all_to_all | solution.py:670
  17.8 0.7 %slice-start = ((f32[1,1,4,3,6]{4,2,3,1,0:T(4,128)}), f32[1,1,2,3,6]{4,2,3,1,0:T(2,128)S(1)}, s32[]{:S(2)}) async-start(f32[1,1,4,3,6]{4,2,3,1,0:T(4,128)} %param.13), calls=%async_computation.2 | async-start | bytes 6144 | tf_op jit(solution)/shard_map/slice | solution.py:674
  20.3 4.9 %collective-permute-start.2 = (f32[8,128]{1,0:T(8,128)S(1)}, f32[8,128]{1,0:T(8,128)S(1)}, u32[]{:S(2)}, u32[]{:S(2)}) collective-permute-start(f32[8,128]{1,0:T(8,128)S(1)} %prepare_i.1.refs_8_.refs_1_.refs_5_), channel_id=1, source_target_pairs={{0,24},{8,0},{16,8},{24,16},{1,25},{9,1},{17,9},{25,17},{2,26},{10... | collective-permute-start | bytes 12296 | tf_op jit(solution)/shard_map/ppermute | solution.py:680
  21.8 3.6 %collective-permute-start.1 = (f32[8,128]{1,0:T(8,128)S(1)}, f32[8,128]{1,0:T(8,128)S(1)}, u32[]{:S(2)}, u32[]{:S(2)}) collective-permute-start(f32[8,128]{1,0:T(8,128)S(1)} %prepare_i.1.refs_8_.refs_1_.refs_5_), channel_id=1, source_target_pairs={{0,16},{8,24},{16,0},{24,8},{1,17},{9,25},{17,1},{25,9},{2,18},{10... | collective-permute-start | bytes 12296 | tf_op jit(solution)/shard_map/ppermute | solution.py:680
  22.3 3.1 %collective-permute-start = (f32[8,128]{1,0:T(8,128)S(1)}, f32[8,128]{1,0:T(8,128)S(1)}, u32[]{:S(2)}, u32[]{:S(2)}) collective-permute-start(f32[8,128]{1,0:T(8,128)S(1)} %prepare_i.1.refs_8_.refs_1_.refs_5_), channel_id=1, source_target_pairs={{0,8},{8,16},{16,24},{24,0},{1,9},{9,17},{17,25},{25,1},{2,10},{10... | collective-permute-start | bytes 12296 | tf_op jit(solution)/shard_map/ppermute | solution.py:680
  44.1 8.6 %collective-permute-start.3 = (f32[192,128]{1,0:T(8,128)S(1)}, f32[192,128]{1,0:T(8,128)S(1)}, u32[]{:S(2)}, u32[]{:S(2)}) collective-permute-start(f32[192,128]{1,0:T(8,128)S(1)} %get-tuple-element.26), channel_id=1, source_target_pairs={{0,8},{8,16},{16,24},{24,0},{1,9},{9,17},{17,25},{25,1},{2,10},{10... | collective-permute-start | bytes 294920 | tf_op jit(solution)/shard_map/ppermute | solution.py:680
  44.2 8.5 %collective-permute-start.4 = (f32[192,128]{1,0:T(8,128)S(1)}, f32[192,128]{1,0:T(8,128)S(1)}, u32[]{:S(2)}, u32[]{:S(2)}) collective-permute-start(f32[192,128]{1,0:T(8,128)S(1)} %get-tuple-element.27), channel_id=1, source_target_pairs={{0,16},{8,24},{16,0},{24,8},{1,17},{9,25},{17,1},{25,9},{2,18},{10... | collective-permute-start | bytes 294920 | tf_op jit(solution)/shard_map/ppermute | solution.py:680
  46.2 6.5 %collective-permute-start.5 = (f32[192,128]{1,0:T(8,128)S(1)}, f32[192,128]{1,0:T(8,128)S(1)}, u32[]{:S(2)}, u32[]{:S(2)}) collective-permute-start(f32[192,128]{1,0:T(8,128)S(1)} %get-tuple-element.28), channel_id=1, source_target_pairs={{0,24},{8,0},{16,8},{24,16},{1,25},{9,1},{17,9},{25,17},{2,26},{10... | collective-permute-start | bytes 294920 | tf_op jit(solution)/shard_map/ppermute | solution.py:680
  54.7 11.0 %all-to-all-start.1 = ((f32[8,32,128]{2,1,0:T(8,128)}), f32[8,32,128]{2,1,0:T(8,128)S(1)}, u32[]{:S(2)}, u32[]{:S(2)}) async-start(f32[8,32,128]{2,1,0:T(8,128)} %get-tuple-element.31), calls=%async_computation.1 | async-start | bytes 262144 | tf_op jit(solution)/shard_map/all_to_all | solution.py:705

commit v4 on v3

--- a/solution.py
+++ b/solution.py
@@ -8,9 +8,9 @@
 from jax.sharding import PartitionSpec as P
 
 LANES = 128
-HIGHEST = lax.Precision.HIGHEST
 F32 = jnp.float32
 BF16 = jnp.bfloat16
+PARAMS = pltpu.CompilerParams(vmem_limit_bytes=32 * 1024 * 1024)
 
 
 def split(x):
@@ -82,90 +82,152 @@
     return pltpu.with_memory_space_constraint(x, pltpu.VMEM)
 
 
+def far(x):
+    return pltpu.with_memory_space_constraint(x, pltpu.HBM)
+
+
 def col(x, c):
     return jnp.broadcast_to(x[:, c : c + 1], x.shape)
 
 
+def gather_slots(cell_ref, tables, place, d, c, count, sizes, chunk, put):
+    high_ref, low_ref = tables
+    fields, cells_j, cells_i = sizes
+    rows_j = 16
+    rows = cells_i // 2 * rows_j
+    per = chunk // LANES
+    start = pl.multiple_of(c * chunk, chunk)
+    cell = cell_ref[pl.ds(d, 1), pl.ds(start, chunk)]
+    i, j, k = split_cell(cell, cells_i, cells_j)
+    slot = start + lax.broadcasted_iota(jnp.int32, cell.shape, 1)
+    row = lax.shift_right_logical(i, 1) * rows_j + j
+    row = jnp.where(slot < count, row, -1)
+    column = (lax.bitwise_and(i, 1) * LANES + k).astype(F32)
+    column = rows_of(column, 16, BF16)
+    hot = []
+    for r in range(2 * LANES // 16):
+        here = jnp.concatenate([place[16 * r : 16 * r + 16]] * per, axis=1)
+        hot.append(jnp.where(here == column, jnp.asarray(1, BF16), jnp.asarray(0, BF16)))
+    hot = jnp.concatenate(hot, axis=0)
+    found = dot_nn(high_ref[...], hot) + dot_nn(low_ref[...], hot)
+    pick = lax.broadcasted_iota(jnp.int32, (rows, chunk), 0) == row
+    for f in range(fields):
+        value = jnp.where(pick, found[f * rows : (f + 1) * rows], 0.0)
+        value = jnp.sum(value, axis=0, keepdims=True)
+        for q in range(per):
+            put(f, c * per + q, value[:, q * LANES : (q + 1) * LANES])
+
+
 def gather_kernel(
-    mine_ref, count_ref, cell_ref, field_ref, out_ref, own_ref, high_ref, low_ref, place_ref, *, chunk
+    mine_ref,
+    count_ref,
+    cell_hbm,
+    field_hbm,
+    out_hbm,
+    high_ref,
+    low_ref,
+    cell_ref,
+    field_ref,
+    out_ref,
+    place_ref,
+    cell_sem,
+    field_sem,
+    out_sem,
+    *,
+    chunk,
 ):
     fields, cells_j, cells_i, _ = field_ref.shape
     owners, capacity = cell_ref.shape
     rows_j = 16
     half_i = cells_i // 2
-    rows = half_i * rows_j
+    slot_rows = capacity // LANES
+    loads = [
+        pltpu.make_async_copy(field_hbm.at[f], field_ref.at[f], field_sem.at[f])
+        for f in range(fields)
+    ]
+    cell_load = pltpu.make_async_copy(cell_hbm, cell_ref, cell_sem)
+    for load in loads:
+        load.start()
+    cell_load.start()
+    out_ref[...] = jnp.zeros(out_ref.shape, F32)
+    place_ref[...] = places(2 * LANES, LANES)
     pad = jnp.zeros((rows_j - cells_j, LANES), F32)
     for f in range(fields):
+        loads[f].wait()
         for i in range(cells_i):
             high, low = split(jnp.concatenate([field_ref[f, :, i, :], pad], axis=0))
             at = (f * half_i + i // 2) * rows_j
             lane = (i % 2) * LANES
             high_ref[at : at + rows_j, lane : lane + LANES] = high
             low_ref[at : at + rows_j, lane : lane + LANES] = low
-    out_ref[...] = jnp.zeros(out_ref.shape, F32)
-    place_ref[...] = places(2 * LANES, LANES)
-    per = chunk // LANES
-    slot_rows = capacity // LANES
+    cell_load.wait()
+    mine = mine_ref[0]
+
+    def send(d):
+        return pltpu.make_async_copy(out_ref.at[d], out_hbm.at[d], out_sem.at[d])
 
     def owner_body(d, carry):
-        count = count_ref[d]
+        count = jnp.where(d == mine, 0, count_ref[d])
+
+        def put(f, row, value):
+            out_ref[d, pl.ds(f * slot_rows + row, 1), :] = value
 
         def chunk_body(c, carry):
-            start = pl.multiple_of(c * chunk, chunk)
-            cell = cell_ref[pl.ds(d, 1), pl.ds(start, chunk)]
-            i, j, k = split_cell(cell, cells_i, cells_j)
-            slot = start + lax.broadcasted_iota(jnp.int32, cell.shape, 1)
-            row = lax.shift_right_logical(i, 1) * rows_j + j
-            row = jnp.where(slot < count, row, -1)
-            column = (lax.bitwise_and(i, 1) * LANES + k).astype(F32)
-            column = rows_of(column, 16, BF16)
-            place = place_ref[...]
-            hot = []
-            for r in range(2 * LANES // 16):
-                here = jnp.concatenate([place[16 * r : 16 * r + 16]] * per, axis=1)
-                hot.append(jnp.where(here == column, jnp.asarray(1, BF16), jnp.asarray(0, BF16)))
-            hot = jnp.concatenate(hot, axis=0)
-            found = dot_nn(high_ref[...], hot) + dot_nn(low_ref[...], hot)
-            pick = lax.broadcasted_iota(jnp.int32, (rows, chunk), 0) == row
-            for f in range(fields):
-                value = jnp.where(pick, found[f * rows : (f + 1) * rows], 0.0)
-                value = jnp.sum(value, axis=0, keepdims=True)
-                for q in range(per):
-                    out_ref[d, pl.ds(f * slot_rows + c * per + q, 1), :] = value[
-                        :, q * LANES : (q + 1) * LANES
-                    ]
+            gather_slots(
+                cell_ref,
+                (high_ref, low_ref),
+                place_ref[...],
+                d,
+                c,
+                count,
+                (fields, cells_j, cells_i),
+                chunk,
+                put,
+            )
             return carry
 
-        return lax.fori_loop(0, lax.div(count + (chunk - 1), chunk), chunk_body, carry)
+        lax.fori_loop(0, lax.div(count + (chunk - 1), chunk), chunk_body, 0)
+        send(d).start()
+        return carry
 
     lax.fori_loop(0, owners, owner_body, 0)
-    own_ref[...] = out_ref[mine_ref[0]]
+
+    def wait_body(d, carry):
+        send(d).wait()
+        return carry
+
+    lax.fori_loop(0, owners, wait_body, 0)
 
 
 def gather(mine, count, cell, field, chunk=512):
     fields, _, cells_i, _ = field.shape
     owners, capacity = cell.shape
     table = (fields * cells_i // 2 * 16, 2 * LANES)
+    out = (owners, fields * capacity // LANES, LANES)
+    smem = pl.BlockSpec(memory_space=pltpu.SMEM)
+    vmem = pl.BlockSpec(memory_space=pltpu.VMEM)
+    hbm = pl.BlockSpec(memory_space=pltpu.HBM)
     return pl.pallas_call(
         functools.partial(gather_kernel, chunk=chunk),
         out_shape=(
-            pltpu.VMEM((owners, fields * capacity // LANES, LANES), F32),
-            pltpu.VMEM((fields * capacity // LANES, LANES), F32),
-        ),
-        in_specs=[
-            pl.BlockSpec(memory_space=pltpu.SMEM),
-            pl.BlockSpec(memory_space=pltpu.SMEM),
-            pl.BlockSpec(memory_space=pltpu.VMEM),
-            pl.BlockSpec(memory_space=pltpu.VMEM),
-        ],
-        out_specs=(pl.BlockSpec(memory_space=pltpu.VMEM),) * 2,
-        scratch_shapes=[
+            jax.ShapeDtypeStruct(out, F32),
             pltpu.VMEM(table, BF16),
             pltpu.VMEM(table, BF16),
+        ),
+        in_specs=[smem, smem, hbm, hbm],
+        out_specs=(hbm, vmem, vmem),
+        scratch_shapes=[
+            pltpu.VMEM(cell.shape, jnp.int32),
+            pltpu.VMEM(field.shape, F32),
+            pltpu.VMEM(out, F32),
             pltpu.VMEM((2 * LANES, LANES), BF16),
+            pltpu.SemaphoreType.DMA(()),
+            pltpu.SemaphoreType.DMA((fields,)),
+            pltpu.SemaphoreType.DMA((owners,)),
         ],
+        compiler_params=PARAMS,
         name="gather",
-    )(mine, count, cell, field)
+    )(mine, far(count), far(cell), far(field))
 
 
 def lay_out(entries):
@@ -214,8 +276,9 @@
         out_shape=pltpu.VMEM((8, LANES), F32),
         in_specs=[pl.BlockSpec(memory_space=pltpu.VMEM)],
         out_specs=pl.BlockSpec(memory_space=pltpu.VMEM),
+        compiler_params=PARAMS,
         name="prepare_i",
-    )(i_tiles)
+    )(near(i_tiles))
 
 
 def prepare_k_kernel(couple_ref, k_ref, k_tile, k_map, k_rows, k_carry, f_ref):
@@ -293,8 +356,9 @@
         ],
         out_specs=(pl.BlockSpec(memory_space=pltpu.VMEM),) * 4,
         scratch_shapes=[pltpu.VMEM((2, 8, length), F32)],
+        compiler_params=PARAMS,
         name="prepare_k",
-    )(couplings, k_factors)
+    )(couplings, near(k_factors))
 
 
 def mat2(a, b):
@@ -337,15 +401,15 @@
     along_j = hat(rows_j, j, y)
     first = rows_of(k.astype(F32), 16, BF16)
     second = rows_of((k + 1).astype(F32), 16, BF16)
-    far = split(rows_of(z, 16, F32))
+    remote = split(rows_of(z, 16, F32))
     close = split(rows_of(1.0 - z, 16, F32))
     zero = jnp.zeros((16, chunk), BF16)
-    place = place_ref[...]
+    place = place_ref[:LANES]
     along_k = []
     for part in range(2):
         for r in range(LANES // 16):
             here = jnp.concatenate([place[16 * r : 16 * r + 16]] * per, axis=1)
-            weight = jnp.where(here == second, far[part], zero)
+            weight = jnp.where(here == second, remote[part], zero)
             along_k.append(jnp.where(here == first, close[part], weight))
     along_k = jnp.concatenate(along_k, axis=0)
     blocks = []
@@ -360,13 +424,47 @@
 
 
 def scatter_own_kernel(
-    mine_ref, got_ref, cell_ref, weight_ref, total_ref, place_ref, *, sizes, chunk
+    mine_ref,
+    count_ref,
+    high_ref,
+    low_ref,
+    from_ref,
+    cell_ref,
+    weight_ref,
+    total_ref,
+    got_ref,
+    place_ref,
+    *,
+    sizes,
+    chunk,
+    gather_chunk,
 ):
     capacity = cell_ref.shape[1]
     slot_rows = capacity // LANES
     total_ref[...] = jnp.zeros(total_ref.shape, F32)
-    place_ref[...] = places(LANES, LANES)
+    got_ref[...] = jnp.zeros(got_ref.shape, F32)
+    place_ref[...] = places(2 * LANES, LANES)
     mine = mine_ref[0]
+    count = count_ref[mine]
+
+    def put(f, row, value):
+        got_ref[pl.ds(f * slot_rows + row, 1), :] = value
+
+    def find_body(c, carry):
+        gather_slots(
+            from_ref,
+            (high_ref, low_ref),
+            place_ref[...],
+            mine,
+            c,
+            count,
+            sizes,
+            gather_chunk,
+            put,
+        )
+        return carry
+
+    lax.fori_loop(0, lax.div(count + (gather_chunk - 1), gather_chunk), find_body, 0)
 
     def chunk_body(c, carry):
         spread_slots(
@@ -385,18 +483,24 @@
     lax.fori_loop(0, capacity // chunk, chunk_body, 0)
 
 
-def scatter_own(mine, got, cell, weight, sizes, chunk=2048):
+def scatter_own(mine, count, tables, receptor, cell, weight, sizes, chunk=2048, gather_chunk=512):
     vmem = pl.BlockSpec(memory_space=pltpu.VMEM)
     smem = pl.BlockSpec(memory_space=pltpu.SMEM)
     fields, cells_j, cells_i = sizes
     return pl.pallas_call(
-        functools.partial(scatter_own_kernel, sizes=sizes, chunk=chunk),
+        functools.partial(
+            scatter_own_kernel, sizes=sizes, chunk=chunk, gather_chunk=gather_chunk
+        ),
         out_shape=pltpu.VMEM((fields * cells_i * cells_j, 2 * LANES), F32),
-        in_specs=[smem, vmem, vmem, vmem],
+        in_specs=[smem, smem] + [vmem] * 5,
         out_specs=vmem,
-        scratch_shapes=[pltpu.VMEM((LANES, LANES), BF16)],
+        scratch_shapes=[
+            pltpu.VMEM((fields * cell.shape[1] // LANES, LANES), F32),
+            pltpu.VMEM((2 * LANES, LANES), BF16),
+        ],
+        compiler_params=PARAMS,
         name="scatter_own",
-    )(mine, near(got), cell, weight)
+    )(mine, far(count), *map(near, (*tables, receptor, cell, weight)))
 
 
 def scatter_kernel(*refs, peers, chunk, base):
@@ -491,8 +595,9 @@
             pltpu.VMEM((LANES, LANES), BF16),
             pltpu.VMEM((fields * cells_i * cells_j, LANES), F32),
         ],
+        compiler_params=PARAMS,
         name="scatter",
-    )(mine, block, solve_tiles, near(begun), near(got), cell, weight, residual, *map(near, tiles))
+    )(mine, block, solve_tiles, *map(near, (begun, got, cell, weight, residual, *tiles)))
 
 
 def middle_kernel(*refs, peers, base, fields, cells_i):
@@ -566,6 +671,7 @@
         in_specs=[smem, smem] + [vmem] * (3 + 2 * peers),
         out_specs=(vmem, vmem),
         scratch_shapes=[pltpu.VMEM((4 * fields + 8, LANES), F32)],
+        compiler_params=PARAMS,
         name="middle",
     )(mine, own, *map(near, (start, k_rows, k_tile, *tiles, *got)))
 
@@ -585,11 +691,12 @@
         out_shape=pltpu.VMEM(field.shape, F32),
         in_specs=[vmem, vmem],
         out_specs=vmem,
+        compiler_params=PARAMS,
         name="apply_k",
     )(near(field), near(k_map))
 
 
-def finish_kernel(mine_ref, start_ref, got_ref, carry_ref, out_ref):
+def finish_kernel(mine_ref, start_ref, got_ref, carry_ref, out_hbm, out_ref, out_sem):
     fields, cells_j, cells_i, _ = out_ref.shape
     rows_j = 16
     rows = cells_i * rows_j
@@ -633,6 +740,9 @@
         value = start_ref[f * rows : (f + 1) * rows] - change
         for i in range(cells_i):
             out_ref[f, :, i, :] = value[i * rows_j : i * rows_j + cells_j]
+        pltpu.make_async_copy(out_ref.at[f], out_hbm.at[f], out_sem.at[f]).start()
+    for f in range(fields):
+        pltpu.make_async_copy(out_ref.at[f], out_hbm.at[f], out_sem.at[f]).wait()
 
 
 def finish(mine, start, got, carry, shape):
@@ -642,7 +752,9 @@
         finish_kernel,
         out_shape=jax.ShapeDtypeStruct(shape, F32),
         in_specs=[smem, vmem, vmem, vmem],
-        out_specs=vmem,
+        out_specs=pl.BlockSpec(memory_space=pltpu.HBM),
+        scratch_shapes=[pltpu.VMEM(shape, F32), pltpu.SemaphoreType.DMA((shape[0],))],
+        compiler_params=PARAMS,
         name="finish",
     )(mine, near(start), near(got), near(carry))
 
@@ -666,7 +778,8 @@
     base = 4 * cells_i
 
     adjoint, residual = (x.transpose(0, 2, 1, 3) for x in (adjoint, residual))
-    outgoing, kept = gather(block, send_count.reshape(owners), receptor_cell[0, 0], adjoint)
+    counts = send_count.reshape(owners)
+    outgoing, *tables = gather(block, counts, receptor_cell[0, 0], adjoint)
     incoming = lax.all_to_all(outgoing, "block", split_axis=0, concat_axis=0, tiled=True)
 
     square = i_factors[0].reshape(2, fields, cells_i * cells_i)
@@ -681,7 +794,13 @@
 
     tiles = [own] + [shifted(own, m) for m in range(1, peers)]
     begun = scatter_own(
-        block, kept, donor_cell[0, 0], donor_weight[0, 0], (fields, cells_j, cells_i)
+        block,
+        counts,
+        tables,
+        receptor_cell[0, 0],
+        donor_cell[0, 0],
+        donor_weight[0, 0],
+        (fields, cells_j, cells_i),
     )
     start, *ends = scatter(
         line,
@@ -697,8 +816,8 @@
     )
     got = [ends[0]] + [shifted(ends[m], m) for m in range(1, peers)]
     couple = couplings[0, 0].transpose(1, 0, 2)
-    factors, _ = lax.optimization_barrier((k_factors[0], ends[0]))
-    k_tile, k_map, k_rows, k_carry = prepare_k(couple, factors)
+    couple, _ = lax.optimization_barrier((couple, ends[0]))
+    k_tile, k_map, k_rows, k_carry = prepare_k(couple, k_factors[0])
     start, message = middle(
         line, own, start, k_rows, k_tile, tiles, got, base, owners, fields, cells_i
     )

time: 67.1 us -> 65.5 us (0.976)
  waiting for transfers between devices: 11.6 us -> 10.3 us
    pallas_call x1, Pallas kernels: 2.72 us -> 4.19 us  [scatter_own(): pl.pallas_call(functools.partial(scatter_own_kernel, sizes=sizes, chunk=c...]
    all_to_all x1, starting transfers between devices: 7.41 us -> 8.61 us  [per_device(): lax.all_to_all(outgoing, 'block', split_axis=0, concat_axis=0, tiled=True)]
    all_to_all x1, waiting for transfers between devices: 4.48 us -> 3.28 us  [per_device(): lax.all_to_all(outgoing, 'block', split_axis=0, concat_axis=0, tiled=True)]
    ppermute x6, starting transfers between devices: 5.62 us -> 4.86 us  [shifted(): lax.ppermute(value, 'line', [(s, (s + shift) % peers) for s in range(peer...]
    pallas_call x1, Pallas kernels: 0.89 us -> 0.18 us  [prepare_i(): pl.pallas_call(functools.partial(prepare_i_kernel, cells_i=cells_i), out_...]
  transfers between devices with their start and end apart: 8 -> 8, of which waited for: 3 -> 2; matrix products, arithmetic and copies ran while one was open for 1% -> 0% of each run, Pallas kernels for 14% -> 14%
where the time goes in v4:
time: 65.5 us; the launch traced here: 65.1 us
  Pallas kernels  36.6 us (56%)
  starting transfers between devices  17.1 us (26%)
  waiting for transfers between devices  10.3 us (16%)
  local copies, waits for them, and re-layouts  0.97 us (1%)
    pallas_call x1, Pallas kernels, scatter(): pl.pallas_call(functools.partial(scatter_kernel, peers=peers, chunk=chunk...  13.8 us
    pallas_call x1, Pallas kernels, gather(): pl.pallas_call(functools.partial(gather_kernel, chunk=chunk), out_shape=(...  10.1 us
    all_to_all x1, starting transfers between devices, per_device(): lax.all_to_all(outgoing, 'block', split_axis=0, concat_axis=0, tiled=True)  8.61 us
    all_to_all x1, waiting for transfers between devices, per_device(): lax.all_to_all(message, 'block', split_axis=0, concat_axis=0, tiled=True)  6.96 us
    ppermute x6, starting transfers between devices, shifted(): lax.ppermute(value, 'line', [(s, (s + shift) % peers) for s in range(peer...  4.86 us
    pallas_call x1, Pallas kernels, prepare_k(): pl.pallas_call(prepare_k_kernel, out_shape=(pltpu.VMEM((8, LANES), F32),...  4.62 us
    pallas_call x1, Pallas kernels, scatter_own(): pl.pallas_call(functools.partial(scatter_own_kernel, sizes=sizes, chunk=c...  4.19 us
    all_to_all x1, starting transfers between devices, per_device(): lax.all_to_all(message, 'block', split_axis=0, concat_axis=0, tiled=True)  3.65 us
  transfers between devices with their start and end apart: 8, of which 2 were waited for; matrix products, arithmetic and copies ran while one was open for 0% of the time, Pallas kernels for 14%

profile of v4, /device:TPU:0, one launch (start us, length us, event | category | flops | bytes accessed | tf_op | source)
XLA Modules:
  0.0 65.1 jit_solution(9961905295931542770)
XLA Ops:
  0.0 10.1 %gather.1 = (f32[8,96,128]{2,1,0:T(8,128)}, bf16[384,256]{1,0:T(8,128)(2,1)S(1)}, bf16[384,256]{1,0:T(8,128)(2,1)S(1)}) custom-call(s32[1]{0:T(128)} %bitcast.mine_ref.refs_1_, s32[8]{0:T(128)} %bitcast.31, s32[8,2048]{1,0:T(8,128)} %bitcast.26, f32[6,15,8,128]{3,2,1,0:T(8,128)} %bitcast.29), custom_call_target="tpu_custom_call" | custom-call | tf_op jit(solution)/shard_map/gather/pallas_call | solution.py:210
  10.1 0.0 copy-start.6
  10.1 0.0 copy-start
  10.1 8.6 %all-to-all-start = ((f32[8,96,128]{2,1,0:T(8,128)}), f32[8,96,128]{2,1,0:T(8,128)S(1)}, u32[]{:S(2)}, u32[]{:S(2)}) async-start(f32[8,96,128]{2,1,0:T(8,128)} %get-tuple-element.22), calls=%async_computation | async-start | bytes 786432 | tf_op jit(solution)/shard_map/all_to_all | solution.py:783
  18.8 0.7 %slice-done = f32[1,1,2,3,6]{4,2,3,1,0:T(2,128)S(1)} async-done(((f32[1,1,4,3,6]{4,2,3,1,0:T(4,128)}), f32[1,1,2,3,6]{4,2,3,1,0:T(2,128)S(1)}, s32[]{:S(2)}) %slice-start) | async-done | bytes 168 | tf_op jit(solution)/shard_map/slice | solution.py:787
  19.4 0.1 copy.17
  19.5 0.1 reshape.13
  19.6 0.0 copy-done.6
  19.6 0.1 reshape.12
  19.7 0.2 prepare_i.1.refs_8_.refs_1_.refs_5_
  19.9 0.1 collective-permute-start.2
  20.0 0.8 %collective-permute-start.1 = (f32[8,128]{1,0:T(8,128)S(1)}, f32[8,128]{1,0:T(8,128)S(1)}, u32[]{:S(2)}, u32[]{:S(2)}) collective-permute-start(f32[8,128]{1,0:T(8,128)S(1)} %prepare_i.1.refs_8_.refs_1_.refs_5_), channel_id=1, source_target_pairs={{0,16},{8,24},{16,0},{24,8},{1,17},{9,25},{17,1},{25,9},{2,18},{10... | collective-permute-start | bytes 12296 | tf_op jit(solution)/shard_map/ppermute | solution.py:793
  20.8 0.2 collective-permute-start
  20.9 4.2 %scatter_own.1.refs_3_ = f32[720,256]{1,0:T(8,128)S(1)} custom-call(s32[1]{0:T(128)} %bitcast.mine_ref.refs_1_, s32[8]{0:T(128)} %bitcast.32, bf16[384,256]{1,0:T(8,128)(2,1)S(1)} %get-tuple-element.20.high_ref, bf16[384,256]{1,0:T(8,128)(2,1)S(1)} %get-tuple-element.21.low_ref, s32[8,2048]{1,0:T(8,128)S(1)} %bitcast.27, s32[8,2048]{1,0:T(8,128)S(1)} %bitcast.24, ...), custom_call_target="tpu_custom_call" | custom-call | tf_op jit(solution)/shard_map/scatter_own/pallas_call | solution.py:490
  25.1 0.0 collective-permute-done.2.refs_11_.refs_8_
  25.2 0.0 collective-permute-done.1.refs_10_.refs_7_
  25.2 0.0 collective-permute-done.refs_9_.refs_6_
  25.2 3.3 %all-to-all-done.refs_4_ = f32[8,96,128]{2,1,0:T(8,128)S(1)} async-done(((f32[8,96,128]{2,1,0:T(8,128)}), f32[8,96,128]{2,1,0:T(8,128)S(1)}, u32[]{:S(2)}, u32[]{:S(2)}) %all-to-all-start) | async-done | bytes 393248 | tf_op jit(solution)/shard_map/all_to_all | solution.py:783
  28.5 13.8 %scatter.1 = (f32[768,128]{1,0:T(8,128)S(1)}, f32[192,128]{1,0:T(8,128)S(1)}, f32[192,128]{1,0:T(8,128)S(1)}, f32[192,128]{1,0:T(8,128)S(1)}, f32[192,128]{1,0:T(8,128)S(1)}) custom-call(s32[1]{0:T(128)} %bitcast.1.refs_0_, s32[1]{0:T(128)} %bitcast.mine_ref.refs_1_, f32[3,8,128]{2,1,0:T(8,128)S(1)} %select_maximum_fusion.i_ref.refs_2_, ...), custom_call_target="tpu_custom_call" | custom-call | tf_op jit(solution)/shard_map/scatter/pallas_call | solution.py:587
  42.3 0.0 copy-start.5
  42.3 0.1 collective-permute-start.3
  42.3 2.4 %collective-permute-start.4 = (f32[192,128]{1,0:T(8,128)S(1)}, f32[192,128]{1,0:T(8,128)S(1)}, u32[]{:S(2)}, u32[]{:S(2)}) collective-permute-start(f32[192,128]{1,0:T(8,128)S(1)} %get-tuple-element.29), channel_id=1, source_target_pairs={{0,16},{8,24},{16,0},{24,8},{1,17},{9,25},{17,1},{25,9},{2,18},{10... | collective-permute-start | bytes 294920 | tf_op jit(solution)/shard_map/ppermute | solution.py:793
  44.8 1.4 %collective-permute-start.5 = (f32[192,128]{1,0:T(8,128)S(1)}, f32[192,128]{1,0:T(8,128)S(1)}, u32[]{:S(2)}, u32[]{:S(2)}) collective-permute-start(f32[192,128]{1,0:T(8,128)S(1)} %get-tuple-element.30), channel_id=1, source_target_pairs={{0,24},{8,0},{16,8},{24,16},{1,25},{9,1},{17,9},{25,17},{2,26},{10... | collective-permute-start | bytes 294920 | tf_op jit(solution)/shard_map/ppermute | solution.py:793
  46.1 4.6 %prepare_k.1 = (f32[8,128]{1,0:T(8,128)S(1)}, f32[6,128,128]{2,1,0:T(8,128)S(1)}, f32[6,8,128]{2,1,0:T(8,128)S(1)}, f32[4,8,128]{2,1,0:T(8,128)S(1)}) custom-call(f32[3,4,6]{2,1,0:T(4,128)S(1)} %bitcast.28, f32[2,6,128,128]{3,2,1,0:T(8,128)S(1)} %bitcast.22), custom_call_target="tpu_custom_call" | custom-call | tf_op jit(solution)/shard_map/prepare_k/pallas_call | solution.py:345
  50.8 0.0 collective-permute-done.3.refs_10_
  50.8 0.0 collective-permute-done.4.refs_11_
  50.8 0.0 collective-permute-done.5.refs_12_
  50.8 1.9 %middle.1 = (f32[768,128]{1,0:T(8,128)S(1)}, f32[8,32,128]{2,1,0:T(8,128)}) custom-call(s32[1]{0:T(128)} %bitcast.1.refs_0_, f32[8,128]{1,0:T(8,128)S(1)} %prepare_i.1.refs_8_.refs_1_.refs_5_, f32[768,128]{1,0:T(8,128)S(1)} %get-tuple-element.23.refs_2_, f32[6,8,128]{2,1,0:T(8,128)S(1)} %get-tuple-element.26.refs_3_, ...), custom_call_target="tpu_custom_call" | custom-call | tf_op jit(solution)/shard_map/middle/pallas_call | solution.py:665
  52.7 3.7 %all-to-all-start.1 = ((f32[8,32,128]{2,1,0:T(8,128)}), f32[8,32,128]{2,1,0:T(8,128)S(1)}, u32[]{:S(2)}, u32[]{:S(2)}) async-start(f32[8,32,128]{2,1,0:T(8,128)} %get-tuple-element.33), calls=%async_computation.1 | async-start | bytes 262144 | tf_op jit(solution)/shard_map/all_to_all | solution.py:824
  56.4 0.4 apply_k.1.start_ref
  56.8 7.0 %all-to-all-done.1.got_ref = f32[8,32,128]{2,1,0:T(8,128)S(1)} async-done(((f32[8,32,128]{2,1,0:T(8,128)}), f32[8,32,128]{2,1,0:T(8,128)S(1)}, u32[]{:S(2)}, u32[]{:S(2)}) %all-to-all-start.1) | async-done | bytes 131104 | tf_op jit(solution)/shard_map/all_to_all | solution.py:824
  63.7 1.4 %finish.1 = f32[6,15,8,128]{3,2,1,0:T(8,128)} custom-call(s32[1]{0:T(128)} %bitcast.mine_ref.refs_1_, f32[768,128]{1,0:T(8,128)S(1)} %apply_k.1.start_ref, f32[8,32,128]{2,1,0:T(8,128)S(1)} %all-to-all-done.1.got_ref, f32[4,8,128]{2,1,0:T(8,128)S(1)} %get-tuple-element.34.carry_ref), custom_call_target="tpu_custom_call" | custom-call | tf_op jit(solution)/shard_map/finish/pallas_call | solution.py:751
  (13 shorter events, 0.0 us)
Async XLA Ops:
  10.1 9.5 %copy-start.6 = (f32[1,2,6,8,8]{4,3,2,1,0:T(8,128)S(1)}, f32[1,2,6,8,8]{4,3,2,1,0:T(8,128)}, u32[]{:S(2)}) copy-start(f32[1,2,6,8,8]{4,3,2,1,0:T(8,128)} %param.11) | copy-start | bytes 9220
  10.1 10.8 %copy-start = (f32[1,1,3,8,2048]{4,3,2,1,0:T(8,128)S(1)}, f32[1,1,3,8,2048]{4,3,2,1,0:T(8,128)}, u32[]{:S(2)}) copy-start(f32[1,1,3,8,2048]{4,3,2,1,0:T(8,128)} %param.17) | copy-start | bytes 589828
  10.1 18.3 %all-to-all-start = ((f32[8,96,128]{2,1,0:T(8,128)}), f32[8,96,128]{2,1,0:T(8,128)S(1)}, u32[]{:S(2)}, u32[]{:S(2)}) async-start(f32[8,96,128]{2,1,0:T(8,128)} %get-tuple-element.22), calls=%async_computation | async-start | bytes 786432 | tf_op jit(solution)/shard_map/all_to_all | solution.py:783
  18.8 0.7 %slice-start = ((f32[1,1,4,3,6]{4,2,3,1,0:T(4,128)}), f32[1,1,2,3,6]{4,2,3,1,0:T(2,128)S(1)}, s32[]{:S(2)}) async-start(f32[1,1,4,3,6]{4,2,3,1,0:T(4,128)} %param.13), calls=%async_computation.2 | async-start | bytes 6144 | tf_op jit(solution)/shard_map/slice | solution.py:787
  19.5 1.4 %copy-start.3 = (s32[1,1,8,2048]{3,2,1,0:T(8,128)S(1)}, s32[1,1,8,2048]{3,2,1,0:T(8,128)}, u32[]{:S(2)}) copy-start(s32[1,1,8,2048]{3,2,1,0:T(8,128)} %param.16) | copy-start | bytes 196612
  19.5 1.4 %copy-start.4 = (s32[1,1,8,2048]{3,2,1,0:T(8,128)S(1)}, s32[1,1,8,2048]{3,2,1,0:T(8,128)}, u32[]{:S(2)}) copy-start(s32[1,1,8,2048]{3,2,1,0:T(8,128)} %param.14) | copy-start | bytes 196612
  19.9 5.2 %collective-permute-start.2 = (f32[8,128]{1,0:T(8,128)S(1)}, f32[8,128]{1,0:T(8,128)S(1)}, u32[]{:S(2)}, u32[]{:S(2)}) collective-permute-start(f32[8,128]{1,0:T(8,128)S(1)} %prepare_i.1.refs_8_.refs_1_.refs_5_), channel_id=1, source_target_pairs={{0,24},{8,0},{16,8},{24,16},{1,25},{9,1},{17,9},{25,17},{2,26},{10... | collective-permute-start | bytes 12296 | tf_op jit(solution)/shard_map/ppermute | solution.py:793
  20.0 5.2 %collective-permute-start.1 = (f32[8,128]{1,0:T(8,128)S(1)}, f32[8,128]{1,0:T(8,128)S(1)}, u32[]{:S(2)}, u32[]{:S(2)}) collective-permute-start(f32[8,128]{1,0:T(8,128)S(1)} %prepare_i.1.refs_8_.refs_1_.refs_5_), channel_id=1, source_target_pairs={{0,16},{8,24},{16,0},{24,8},{1,17},{9,25},{17,1},{25,9},{2,18},{10... | collective-permute-start | bytes 12296 | tf_op jit(solution)/shard_map/ppermute | solution.py:793
  20.8 4.4 %collective-permute-start = (f32[8,128]{1,0:T(8,128)S(1)}, f32[8,128]{1,0:T(8,128)S(1)}, u32[]{:S(2)}, u32[]{:S(2)}) collective-permute-start(f32[8,128]{1,0:T(8,128)S(1)} %prepare_i.1.refs_8_.refs_1_.refs_5_), channel_id=1, source_target_pairs={{0,8},{8,16},{16,24},{24,0},{1,9},{9,17},{17,25},{25,1},{2,10},{10... | collective-permute-start | bytes 12296 | tf_op jit(solution)/shard_map/ppermute | solution.py:793
  20.9 7.5 %copy-start.2 = (f32[6,8,15,128]{3,1,2,0:T(8,128)S(1)}, f32[6,8,15,128]{3,1,2,0:T(8,128)}, u32[]{:S(2)}) copy-start(f32[6,8,15,128]{3,1,2,0:T(8,128)} %param.9) | copy-start | bytes 1105924
  28.5 17.7 %copy-start.1 = (f32[1,2,6,128,128]{4,3,2,1,0:T(8,128)S(1)}, f32[1,2,6,128,128]{4,3,2,1,0:T(8,128)}, u32[]{:S(2)}) copy-start(f32[1,2,6,128,128]{4,3,2,1,0:T(8,128)} %param.12) | copy-start | bytes 2359300
  42.3 3.9 %copy-start.5 = (f32[1,1,4,3,6]{4,2,3,1,0:T(4,128)S(1)}, f32[1,1,4,3,6]{4,2,3,1,0:T(4,128)}, u32[]{:S(2)}) copy-start(f32[1,1,4,3,6]{4,2,3,1,0:T(4,128)} %param.13) | copy-start | bytes 868
  42.3 8.5 %collective-permute-start.3 = (f32[192,128]{1,0:T(8,128)S(1)}, f32[192,128]{1,0:T(8,128)S(1)}, u32[]{:S(2)}, u32[]{:S(2)}) collective-permute-start(f32[192,128]{1,0:T(8,128)S(1)} %get-tuple-element.28), channel_id=1, source_target_pairs={{0,8},{8,16},{16,24},{24,0},{1,9},{9,17},{17,25},{25,1},{2,10},{10... | collective-permute-start | bytes 294920 | tf_op jit(solution)/shard_map/ppermute | solution.py:793
  42.3 8.5 %collective-permute-start.4 = (f32[192,128]{1,0:T(8,128)S(1)}, f32[192,128]{1,0:T(8,128)S(1)}, u32[]{:S(2)}, u32[]{:S(2)}) collective-permute-start(f32[192,128]{1,0:T(8,128)S(1)} %get-tuple-element.29), channel_id=1, source_target_pairs={{0,16},{8,24},{16,0},{24,8},{1,17},{9,25},{17,1},{25,9},{2,18},{10... | collective-permute-start | bytes 294920 | tf_op jit(solution)/shard_map/ppermute | solution.py:793
  44.8 6.0 %collective-permute-start.5 = (f32[192,128]{1,0:T(8,128)S(1)}, f32[192,128]{1,0:T(8,128)S(1)}, u32[]{:S(2)}, u32[]{:S(2)}) collective-permute-start(f32[192,128]{1,0:T(8,128)S(1)} %get-tuple-element.30), channel_id=1, source_target_pairs={{0,24},{8,0},{16,8},{24,16},{1,25},{9,1},{17,9},{25,17},{2,26},{10... | collective-permute-start | bytes 294920 | tf_op jit(solution)/shard_map/ppermute | solution.py:793
  52.7 11.0 %all-to-all-start.1 = ((f32[8,32,128]{2,1,0:T(8,128)}), f32[8,32,128]{2,1,0:T(8,128)S(1)}, u32[]{:S(2)}, u32[]{:S(2)}) async-start(f32[8,32,128]{2,1,0:T(8,128)} %get-tuple-element.33), calls=%async_computation.1 | async-start | bytes 262144 | tf_op jit(solution)/shard_map/all_to_all | solution.py:824

commit v5 on v4

--- a/solution.py
+++ b/solution.py
@@ -90,29 +90,35 @@
     return jnp.broadcast_to(x[:, c : c + 1], x.shape)
 
 
-def gather_slots(cell_ref, tables, place, d, c, count, sizes, chunk, put):
-    high_ref, low_ref = tables
+def build_hot(hot_ref, lane, cell_ref, place, d, c, chunk, sizes):
+    _, cells_j, cells_i = sizes
+    start = pl.multiple_of(c * chunk, chunk)
+    cell = cell_ref[pl.ds(d, 1), pl.ds(start, chunk)]
+    i, _, k = split_cell(cell, cells_i, cells_j)
+    column = (lax.bitwise_and(i, 1) * LANES + k).astype(F32)
+    column = rows_of(column, 16, BF16)
+    for r in range(2 * LANES // 16):
+        here = jnp.concatenate([place[16 * r : 16 * r + 16]] * (chunk // LANES), axis=1)
+        hot_ref[16 * r : 16 * r + 16, lane : lane + chunk] = jnp.where(
+            here == column, jnp.asarray(1, BF16), jnp.asarray(0, BF16)
+        )
+
+
+def pick_rows(found_ref, lane, cell_ref, d, c, count, chunk, sizes, put):
     fields, cells_j, cells_i = sizes
     rows_j = 16
     rows = cells_i // 2 * rows_j
     per = chunk // LANES
     start = pl.multiple_of(c * chunk, chunk)
     cell = cell_ref[pl.ds(d, 1), pl.ds(start, chunk)]
-    i, j, k = split_cell(cell, cells_i, cells_j)
+    i, j, _ = split_cell(cell, cells_i, cells_j)
     slot = start + lax.broadcasted_iota(jnp.int32, cell.shape, 1)
     row = lax.shift_right_logical(i, 1) * rows_j + j
     row = jnp.where(slot < count, row, -1)
-    column = (lax.bitwise_and(i, 1) * LANES + k).astype(F32)
-    column = rows_of(column, 16, BF16)
-    hot = []
-    for r in range(2 * LANES // 16):
-        here = jnp.concatenate([place[16 * r : 16 * r + 16]] * per, axis=1)
-        hot.append(jnp.where(here == column, jnp.asarray(1, BF16), jnp.asarray(0, BF16)))
-    hot = jnp.concatenate(hot, axis=0)
-    found = dot_nn(high_ref[...], hot) + dot_nn(low_ref[...], hot)
     pick = lax.broadcasted_iota(jnp.int32, (rows, chunk), 0) == row
     for f in range(fields):
-        value = jnp.where(pick, found[f * rows : (f + 1) * rows], 0.0)
+        value = found_ref[f * rows : (f + 1) * rows, lane : lane + chunk]
+        value = jnp.where(pick, value, 0.0)
         value = jnp.sum(value, axis=0, keepdims=True)
         for q in range(per):
             put(f, c * per + q, value[:, q * LANES : (q + 1) * LANES])
@@ -130,27 +136,64 @@
     field_ref,
     out_ref,
     place_ref,
+    hot_ref,
+    found_ref,
+    list_ref,
     cell_sem,
     field_sem,
     out_sem,
     *,
     chunk,
+    group,
 ):
     fields, cells_j, cells_i, _ = field_ref.shape
     owners, capacity = cell_ref.shape
+    sizes = (fields, cells_j, cells_i)
     rows_j = 16
     half_i = cells_i // 2
     slot_rows = capacity // LANES
+    steps = capacity // chunk
     loads = [
         pltpu.make_async_copy(field_hbm.at[f], field_ref.at[f], field_sem.at[f])
         for f in range(fields)
     ]
     cell_load = pltpu.make_async_copy(cell_hbm, cell_ref, cell_sem)
+    cell_load.start()
     for load in loads:
         load.start()
-    cell_load.start()
+    mine = mine_ref[0]
+
+    def send(d):
+        return pltpu.make_async_copy(out_ref.at[d], out_hbm.at[d], out_sem.at[d])
+
     out_ref[...] = jnp.zeros(out_ref.shape, F32)
+    send(mine).start()
     place_ref[...] = places(2 * LANES, LANES)
+
+    def list_owner(d, total):
+        live = jnp.maximum(lax.div(count_ref[d] + (chunk - 1), chunk), 1)
+        live = jnp.where(d == mine, 0, live)
+
+        def list_chunk(c, at):
+            list_ref[at] = d * steps + c
+            return at + 1
+
+        return lax.fori_loop(0, live, list_chunk, total)
+
+    total = lax.fori_loop(0, owners, list_owner, 0)
+    groups = lax.div(total + (group - 1), group)
+
+    def place_of(n):
+        entry = list_ref[jnp.minimum(n, total - 1)]
+        return lax.div(entry, steps), lax.rem(entry, steps)
+
+    def build(n):
+        for g in range(group):
+            d, c = place_of(n * group + g)
+            build_hot(hot_ref, g * chunk, cell_ref, place_ref[...], d, c, chunk, sizes)
+
+    cell_load.wait()
+    build(0)
     pad = jnp.zeros((rows_j - cells_j, LANES), F32)
     for f in range(fields):
         loads[f].wait()
@@ -160,37 +203,46 @@
             lane = (i % 2) * LANES
             high_ref[at : at + rows_j, lane : lane + LANES] = high
             low_ref[at : at + rows_j, lane : lane + LANES] = low
-    cell_load.wait()
-    mine = mine_ref[0]
-
-    def send(d):
-        return pltpu.make_async_copy(out_ref.at[d], out_hbm.at[d], out_sem.at[d])
-
-    def owner_body(d, carry):
-        count = jnp.where(d == mine, 0, count_ref[d])
-
-        def put(f, row, value):
-            out_ref[d, pl.ds(f * slot_rows + row, 1), :] = value
-
-        def chunk_body(c, carry):
-            gather_slots(
-                cell_ref,
-                (high_ref, low_ref),
-                place_ref[...],
-                d,
-                c,
-                count,
-                (fields, cells_j, cells_i),
-                chunk,
-                put,
+
+    def pick(n):
+        for g in range(group):
+            d, c = place_of(n * group + g)
+
+            def put(f, row, value, d=d):
+                out_ref[d, pl.ds(f * slot_rows + row, 1), :] = value
+
+            pick_rows(
+                found_ref, g * chunk, cell_ref, d, c, count_ref[d], chunk, sizes, put
             )
-            return carry
-
-        lax.fori_loop(0, lax.div(count + (chunk - 1), chunk), chunk_body, 0)
-        send(d).start()
+
+    def body(n, carry):
+        done = jnp.maximum(n - 1, 0)
+        pick(done)
+        hot = hot_ref[...]
+        found_ref[...] = dot_nn(high_ref[...], hot) + dot_nn(low_ref[...], hot)
+        build(n + 1)
+        for g in range(group):
+            here, _ = place_of(done * group + g)
+            following, _ = place_of(done * group + g + 1)
+
+            @pl.when((n > 0) & (here != following))
+            def _(here=here):
+                send(here).start()
+
         return carry
 
-    lax.fori_loop(0, owners, owner_body, 0)
+    lax.fori_loop(0, groups, body, 0)
+    pick(groups - 1)
+    for g in range(group):
+        here, _ = place_of((groups - 1) * group + g)
+        following, _ = place_of((groups - 1) * group + g + 1)
+
+        @pl.when(here != following)
+        def _(here=here):
+            send(here).start()
+
+    last, _ = place_of(total - 1)
+    send(last).start()
 
     def wait_body(d, carry):
         send(d).wait()
@@ -199,7 +251,7 @@
     lax.fori_loop(0, owners, wait_body, 0)
 
 
-def gather(mine, count, cell, field, chunk=512):
+def gather(mine, count, cell, field, chunk=256, group=4):
     fields, _, cells_i, _ = field.shape
     owners, capacity = cell.shape
     table = (fields * cells_i // 2 * 16, 2 * LANES)
@@ -208,7 +260,7 @@
     vmem = pl.BlockSpec(memory_space=pltpu.VMEM)
     hbm = pl.BlockSpec(memory_space=pltpu.HBM)
     return pl.pallas_call(
-        functools.partial(gather_kernel, chunk=chunk),
+        functools.partial(gather_kernel, chunk=chunk, group=group),
         out_shape=(
             jax.ShapeDtypeStruct(out, F32),
             pltpu.VMEM(table, BF16),
@@ -221,6 +273,9 @@
             pltpu.VMEM(field.shape, F32),
             pltpu.VMEM(out, F32),
             pltpu.VMEM((2 * LANES, LANES), BF16),
+            pltpu.VMEM((2 * LANES, group * chunk), BF16),
+            pltpu.VMEM((table[0], group * chunk), F32),
+            pltpu.SMEM((owners * capacity // chunk,), jnp.int32),
             pltpu.SemaphoreType.DMA(()),
             pltpu.SemaphoreType.DMA((fields,)),
             pltpu.SemaphoreType.DMA((owners,)),
@@ -434,6 +489,8 @@
     total_ref,
     got_ref,
     place_ref,
+    hot_ref,
+    found_ref,
     *,
     sizes,
     chunk,
@@ -451,17 +508,10 @@
         got_ref[pl.ds(f * slot_rows + row, 1), :] = value
 
     def find_body(c, carry):
-        gather_slots(
-            from_ref,
-            (high_ref, low_ref),
-            place_ref[...],
-            mine,
-            c,
-            count,
-            sizes,
-            gather_chunk,
-            put,
-        )
+        build_hot(hot_ref, 0, from_ref, place_ref[...], mine, c, gather_chunk, sizes)
+        hot = hot_ref[...]
+        found_ref[...] = dot_nn(high_ref[...], hot) + dot_nn(low_ref[...], hot)
+        pick_rows(found_ref, 0, from_ref, mine, c, count, gather_chunk, sizes, put)
         return carry
 
     lax.fori_loop(0, lax.div(count + (gather_chunk - 1), gather_chunk), find_body, 0)
@@ -497,6 +547,8 @@
         scratch_shapes=[
             pltpu.VMEM((fields * cell.shape[1] // LANES, LANES), F32),
             pltpu.VMEM((2 * LANES, LANES), BF16),
+            pltpu.VMEM((2 * LANES, gather_chunk), BF16),
+            pltpu.VMEM((tables[0].shape[0], gather_chunk), F32),
         ],
         compiler_params=PARAMS,
         name="scatter_own",

time: 65.5 us -> 63.6 us (0.971)
  Pallas kernels: 36.6 us -> 34.6 us
  waiting for transfers between devices: 10.3 us -> 11.8 us
  starting transfers between devices: 17.1 us -> 15.9 us
    all_to_all x1, starting transfers between devices: 8.61 us -> 6.81 us  [per_device(): lax.all_to_all(outgoing, 'block', split_axis=0, concat_axis=0, tiled=True)]
    pallas_call x1, Pallas kernels: 10.1 us -> 8.52 us  [gather(): pl.pallas_call(functools.partial(gather_kernel, chunk=chunk, group=group)...]
    all_to_all x1, waiting for transfers between devices: 3.28 us -> 4.85 us  [per_device(): lax.all_to_all(outgoing, 'block', split_axis=0, concat_axis=0, tiled=True)]
where the time goes in v5:
time: 63.6 us; the launch traced here: 63.5 us
  Pallas kernels  34.6 us (54%)
  starting transfers between devices  15.9 us (25%)
  waiting for transfers between devices  11.8 us (19%)
  local copies, waits for them, and re-layouts  0.97 us (2%)
    pallas_call x1, Pallas kernels, scatter(): pl.pallas_call(functools.partial(scatter_kernel, peers=peers, chunk=chunk...  13.8 us
    pallas_call x1, Pallas kernels, gather(): pl.pallas_call(functools.partial(gather_kernel, chunk=chunk, group=group)...  8.52 us
    all_to_all x1, waiting for transfers between devices, per_device(): lax.all_to_all(message, 'block', split_axis=0, concat_axis=0, tiled=True)  6.96 us
    all_to_all x1, starting transfers between devices, per_device(): lax.all_to_all(outgoing, 'block', split_axis=0, concat_axis=0, tiled=True)  6.81 us
    ppermute x6, starting transfers between devices, shifted(): lax.ppermute(value, 'line', [(s, (s + shift) % peers) for s in range(peer...  5.45 us
    all_to_all x1, waiting for transfers between devices, per_device(): lax.all_to_all(outgoing, 'block', split_axis=0, concat_axis=0, tiled=True)  4.85 us
    pallas_call x1, Pallas kernels, prepare_k(): pl.pallas_call(prepare_k_kernel, out_shape=(pltpu.VMEM((8, LANES), F32),...  4.62 us
    pallas_call x1, Pallas kernels, scatter_own(): pl.pallas_call(functools.partial(scatter_own_kernel, sizes=sizes, chunk=c...  3.79 us
  transfers between devices with their start and end apart: 8, of which 2 were waited for; matrix products, arithmetic and copies ran while one was open for 0% of the time, Pallas kernels for 14%

profile of v5, /device:TPU:0, one launch (start us, length us, event | category | flops | bytes accessed | tf_op | source)
XLA Modules:
  0.0 63.5 jit_solution(13258110575136810987)
XLA Ops:
  0.0 8.5 %gather.1 = (f32[8,96,128]{2,1,0:T(8,128)}, bf16[384,256]{1,0:T(8,128)(2,1)S(1)}, bf16[384,256]{1,0:T(8,128)(2,1)S(1)}) custom-call(s32[1]{0:T(128)} %bitcast.mine_ref.refs_1_, s32[8]{0:T(128)} %bitcast.31, s32[8,2048]{1,0:T(8,128)} %bitcast.26, f32[6,15,8,128]{3,2,1,0:T(8,128)} %bitcast.29), custom_call_target="tpu_custom_call" | custom-call | tf_op jit(solution)/shard_map/gather/pallas_call | solution.py:262
  8.5 0.0 copy-start.6
  8.5 0.0 copy-start
  8.6 6.8 %all-to-all-start = ((f32[8,96,128]{2,1,0:T(8,128)}), f32[8,96,128]{2,1,0:T(8,128)S(1)}, u32[]{:S(2)}, u32[]{:S(2)}) async-start(f32[8,96,128]{2,1,0:T(8,128)} %get-tuple-element.22), calls=%async_computation | async-start | bytes 786432 | tf_op jit(solution)/shard_map/all_to_all | solution.py:835
  15.4 0.7 %slice-done = f32[1,1,2,3,6]{4,2,3,1,0:T(2,128)S(1)} async-done(((f32[1,1,4,3,6]{4,2,3,1,0:T(4,128)}), f32[1,1,2,3,6]{4,2,3,1,0:T(2,128)S(1)}, s32[]{:S(2)}) %slice-start) | async-done | bytes 168 | tf_op jit(solution)/shard_map/slice | solution.py:839
  16.0 0.1 copy.17
  16.2 0.1 reshape.13
  16.2 0.1 reshape.12
  16.3 0.2 prepare_i.1.refs_8_.refs_1_.refs_5_
  16.5 1.4 %collective-permute-start.2 = (f32[8,128]{1,0:T(8,128)S(1)}, f32[8,128]{1,0:T(8,128)S(1)}, u32[]{:S(2)}, u32[]{:S(2)}) collective-permute-start(f32[8,128]{1,0:T(8,128)S(1)} %prepare_i.1.refs_8_.refs_1_.refs_5_), channel_id=1, source_target_pairs={{0,24},{8,0},{16,8},{24,16},{1,25},{9,1},{17,9},{25,17},{2,26},{10... | collective-permute-start | bytes 12296 | tf_op jit(solution)/shard_map/ppermute | solution.py:845
  17.9 0.9 %collective-permute-start.1 = (f32[8,128]{1,0:T(8,128)S(1)}, f32[8,128]{1,0:T(8,128)S(1)}, u32[]{:S(2)}, u32[]{:S(2)}) collective-permute-start(f32[8,128]{1,0:T(8,128)S(1)} %prepare_i.1.refs_8_.refs_1_.refs_5_), channel_id=1, source_target_pairs={{0,16},{8,24},{16,0},{24,8},{1,17},{9,25},{17,1},{25,9},{2,18},{10... | collective-permute-start | bytes 12296 | tf_op jit(solution)/shard_map/ppermute | solution.py:845
  18.8 0.2 collective-permute-start
  19.0 0.0 copy-done
  19.0 3.8 %scatter_own.1.refs_3_ = f32[720,256]{1,0:T(8,128)S(1)} custom-call(s32[1]{0:T(128)} %bitcast.mine_ref.refs_1_, s32[8]{0:T(128)} %bitcast.32, bf16[384,256]{1,0:T(8,128)(2,1)S(1)} %get-tuple-element.20.high_ref, bf16[384,256]{1,0:T(8,128)(2,1)S(1)} %get-tuple-element.21.low_ref, s32[8,2048]{1,0:T(8,128)S(1)} %bitcast.27, s32[8,2048]{1,0:T(8,128)S(1)} %bitcast.24, ...), custom_call_target="tpu_custom_call" | custom-call | tf_op jit(solution)/shard_map/scatter_own/pallas_call | solution.py:540
  22.8 0.0 collective-permute-done.2.refs_11_.refs_8_
  22.8 0.0 collective-permute-done.1.refs_10_.refs_7_
  22.8 0.0 collective-permute-done.refs_9_.refs_6_
  22.8 4.9 %all-to-all-done.refs_4_ = f32[8,96,128]{2,1,0:T(8,128)S(1)} async-done(((f32[8,96,128]{2,1,0:T(8,128)}), f32[8,96,128]{2,1,0:T(8,128)S(1)}, u32[]{:S(2)}, u32[]{:S(2)}) %all-to-all-start) | async-done | bytes 393248 | tf_op jit(solution)/shard_map/all_to_all | solution.py:835
  27.7 13.8 %scatter.1 = (f32[768,128]{1,0:T(8,128)S(1)}, f32[192,128]{1,0:T(8,128)S(1)}, f32[192,128]{1,0:T(8,128)S(1)}, f32[192,128]{1,0:T(8,128)S(1)}, f32[192,128]{1,0:T(8,128)S(1)}) custom-call(s32[1]{0:T(128)} %bitcast.1.refs_0_, s32[1]{0:T(128)} %bitcast.mine_ref.refs_1_, f32[3,8,128]{2,1,0:T(8,128)S(1)} %select_maximum_fusion.i_ref.refs_2_, ...), custom_call_target="tpu_custom_call" | custom-call | tf_op jit(solution)/shard_map/scatter/pallas_call | solution.py:639
  41.5 0.0 copy-start.5
  41.5 0.1 collective-permute-start.3
  41.6 1.6 %collective-permute-start.4 = (f32[192,128]{1,0:T(8,128)S(1)}, f32[192,128]{1,0:T(8,128)S(1)}, u32[]{:S(2)}, u32[]{:S(2)}) collective-permute-start(f32[192,128]{1,0:T(8,128)S(1)} %get-tuple-element.29), channel_id=1, source_target_pairs={{0,16},{8,24},{16,0},{24,8},{1,17},{9,25},{17,1},{25,9},{2,18},{10... | collective-permute-start | bytes 294920 | tf_op jit(solution)/shard_map/ppermute | solution.py:845
  43.1 1.4 %collective-permute-start.5 = (f32[192,128]{1,0:T(8,128)S(1)}, f32[192,128]{1,0:T(8,128)S(1)}, u32[]{:S(2)}, u32[]{:S(2)}) collective-permute-start(f32[192,128]{1,0:T(8,128)S(1)} %get-tuple-element.30), channel_id=1, source_target_pairs={{0,24},{8,0},{16,8},{24,16},{1,25},{9,1},{17,9},{25,17},{2,26},{10... | collective-permute-start | bytes 294920 | tf_op jit(solution)/shard_map/ppermute | solution.py:845
  44.5 4.6 %prepare_k.1 = (f32[8,128]{1,0:T(8,128)S(1)}, f32[6,128,128]{2,1,0:T(8,128)S(1)}, f32[6,8,128]{2,1,0:T(8,128)S(1)}, f32[4,8,128]{2,1,0:T(8,128)S(1)}) custom-call(f32[3,4,6]{2,1,0:T(4,128)S(1)} %bitcast.28, f32[2,6,128,128]{3,2,1,0:T(8,128)S(1)} %bitcast.22), custom_call_target="tpu_custom_call" | custom-call | tf_op jit(solution)/shard_map/prepare_k/pallas_call | solution.py:400
  49.1 0.0 collective-permute-done.3.refs_10_
  49.2 0.0 collective-permute-done.4.refs_11_
  49.2 0.0 collective-permute-done.5.refs_12_
  49.2 1.9 %middle.1 = (f32[768,128]{1,0:T(8,128)S(1)}, f32[8,32,128]{2,1,0:T(8,128)}) custom-call(s32[1]{0:T(128)} %bitcast.1.refs_0_, f32[8,128]{1,0:T(8,128)S(1)} %prepare_i.1.refs_8_.refs_1_.refs_5_, f32[768,128]{1,0:T(8,128)S(1)} %get-tuple-element.23.refs_2_, f32[6,8,128]{2,1,0:T(8,128)S(1)} %get-tuple-element.26.refs_3_, ...), custom_call_target="tpu_custom_call" | custom-call | tf_op jit(solution)/shard_map/middle/pallas_call | solution.py:717
  51.1 3.6 %all-to-all-start.1 = ((f32[8,32,128]{2,1,0:T(8,128)}), f32[8,32,128]{2,1,0:T(8,128)S(1)}, u32[]{:S(2)}, u32[]{:S(2)}) async-start(f32[8,32,128]{2,1,0:T(8,128)} %get-tuple-element.33), calls=%async_computation.1 | async-start | bytes 262144 | tf_op jit(solution)/shard_map/all_to_all | solution.py:876
  54.8 0.4 apply_k.1.start_ref
  55.1 7.0 %all-to-all-done.1.got_ref = f32[8,32,128]{2,1,0:T(8,128)S(1)} async-done(((f32[8,32,128]{2,1,0:T(8,128)}), f32[8,32,128]{2,1,0:T(8,128)S(1)}, u32[]{:S(2)}, u32[]{:S(2)}) %all-to-all-start.1) | async-done | bytes 131104 | tf_op jit(solution)/shard_map/all_to_all | solution.py:876
  62.1 1.4 %finish.1 = f32[6,15,8,128]{3,2,1,0:T(8,128)} custom-call(s32[1]{0:T(128)} %bitcast.mine_ref.refs_1_, f32[768,128]{1,0:T(8,128)S(1)} %apply_k.1.start_ref, f32[8,32,128]{2,1,0:T(8,128)S(1)} %all-to-all-done.1.got_ref, f32[4,8,128]{2,1,0:T(8,128)S(1)} %get-tuple-element.34.carry_ref), custom_call_target="tpu_custom_call" | custom-call | tf_op jit(solution)/shard_map/finish/pallas_call | solution.py:803
  (13 shorter events, 0.0 us)
Async XLA Ops:
  8.5 7.7 %copy-start.6 = (f32[1,2,6,8,8]{4,3,2,1,0:T(8,128)S(1)}, f32[1,2,6,8,8]{4,3,2,1,0:T(8,128)}, u32[]{:S(2)}) copy-start(f32[1,2,6,8,8]{4,3,2,1,0:T(8,128)} %param.11) | copy-start | bytes 9220
  8.5 10.4 %copy-start = (f32[1,1,3,8,2048]{4,3,2,1,0:T(8,128)S(1)}, f32[1,1,3,8,2048]{4,3,2,1,0:T(8,128)}, u32[]{:S(2)}) copy-start(f32[1,1,3,8,2048]{4,3,2,1,0:T(8,128)} %param.17) | copy-start | bytes 589828
  8.6 19.1 %all-to-all-start = ((f32[8,96,128]{2,1,0:T(8,128)}), f32[8,96,128]{2,1,0:T(8,128)S(1)}, u32[]{:S(2)}, u32[]{:S(2)}) async-start(f32[8,96,128]{2,1,0:T(8,128)} %get-tuple-element.22), calls=%async_computation | async-start | bytes 786432 | tf_op jit(solution)/shard_map/all_to_all | solution.py:835
  15.4 0.7 %slice-start = ((f32[1,1,4,3,6]{4,2,3,1,0:T(4,128)}), f32[1,1,2,3,6]{4,2,3,1,0:T(2,128)S(1)}, s32[]{:S(2)}) async-start(f32[1,1,4,3,6]{4,2,3,1,0:T(4,128)} %param.13), calls=%async_computation.2 | async-start | bytes 6144 | tf_op jit(solution)/shard_map/slice | solution.py:839
  16.1 2.8 %copy-start.3 = (s32[1,1,8,2048]{3,2,1,0:T(8,128)S(1)}, s32[1,1,8,2048]{3,2,1,0:T(8,128)}, u32[]{:S(2)}) copy-start(s32[1,1,8,2048]{3,2,1,0:T(8,128)} %param.16) | copy-start | bytes 196612
  16.1 2.8 %copy-start.4 = (s32[1,1,8,2048]{3,2,1,0:T(8,128)S(1)}, s32[1,1,8,2048]{3,2,1,0:T(8,128)}, u32[]{:S(2)}) copy-start(s32[1,1,8,2048]{3,2,1,0:T(8,128)} %param.14) | copy-start | bytes 196612
  16.5 6.2 %collective-permute-start.2 = (f32[8,128]{1,0:T(8,128)S(1)}, f32[8,128]{1,0:T(8,128)S(1)}, u32[]{:S(2)}, u32[]{:S(2)}) collective-permute-start(f32[8,128]{1,0:T(8,128)S(1)} %prepare_i.1.refs_8_.refs_1_.refs_5_), channel_id=1, source_target_pairs={{0,24},{8,0},{16,8},{24,16},{1,25},{9,1},{17,9},{25,17},{2,26},{10... | collective-permute-start | bytes 12296 | tf_op jit(solution)/shard_map/ppermute | solution.py:845
  17.9 4.9 %collective-permute-start.1 = (f32[8,128]{1,0:T(8,128)S(1)}, f32[8,128]{1,0:T(8,128)S(1)}, u32[]{:S(2)}, u32[]{:S(2)}) collective-permute-start(f32[8,128]{1,0:T(8,128)S(1)} %prepare_i.1.refs_8_.refs_1_.refs_5_), channel_id=1, source_target_pairs={{0,16},{8,24},{16,0},{24,8},{1,17},{9,25},{17,1},{25,9},{2,18},{10... | collective-permute-start | bytes 12296 | tf_op jit(solution)/shard_map/ppermute | solution.py:845
  18.8 4.0 %collective-permute-start = (f32[8,128]{1,0:T(8,128)S(1)}, f32[8,128]{1,0:T(8,128)S(1)}, u32[]{:S(2)}, u32[]{:S(2)}) collective-permute-start(f32[8,128]{1,0:T(8,128)S(1)} %prepare_i.1.refs_8_.refs_1_.refs_5_), channel_id=1, source_target_pairs={{0,8},{8,16},{16,24},{24,0},{1,9},{9,17},{17,25},{25,1},{2,10},{10... | collective-permute-start | bytes 12296 | tf_op jit(solution)/shard_map/ppermute | solution.py:845
  19.0 8.7 %copy-start.2 = (f32[6,8,15,128]{3,1,2,0:T(8,128)S(1)}, f32[6,8,15,128]{3,1,2,0:T(8,128)}, u32[]{:S(2)}) copy-start(f32[6,8,15,128]{3,1,2,0:T(8,128)} %param.9) | copy-start | bytes 1105924
  27.7 16.9 %copy-start.1 = (f32[1,2,6,128,128]{4,3,2,1,0:T(8,128)S(1)}, f32[1,2,6,128,128]{4,3,2,1,0:T(8,128)}, u32[]{:S(2)}) copy-start(f32[1,2,6,128,128]{4,3,2,1,0:T(8,128)} %param.12) | copy-start | bytes 2359300
  41.5 3.1 %copy-start.5 = (f32[1,1,4,3,6]{4,2,3,1,0:T(4,128)S(1)}, f32[1,1,4,3,6]{4,2,3,1,0:T(4,128)}, u32[]{:S(2)}) copy-start(f32[1,1,4,3,6]{4,2,3,1,0:T(4,128)} %param.13) | copy-start | bytes 868
  41.5 7.7 %collective-permute-start.3 = (f32[192,128]{1,0:T(8,128)S(1)}, f32[192,128]{1,0:T(8,128)S(1)}, u32[]{:S(2)}, u32[]{:S(2)}) collective-permute-start(f32[192,128]{1,0:T(8,128)S(1)} %get-tuple-element.28), channel_id=1, source_target_pairs={{0,8},{8,16},{16,24},{24,0},{1,9},{9,17},{17,25},{25,1},{2,10},{10... | collective-permute-start | bytes 294920 | tf_op jit(solution)/shard_map/ppermute | solution.py:845
  41.6 7.6 %collective-permute-start.4 = (f32[192,128]{1,0:T(8,128)S(1)}, f32[192,128]{1,0:T(8,128)S(1)}, u32[]{:S(2)}, u32[]{:S(2)}) collective-permute-start(f32[192,128]{1,0:T(8,128)S(1)} %get-tuple-element.29), channel_id=1, source_target_pairs={{0,16},{8,24},{16,0},{24,8},{1,17},{9,25},{17,1},{25,9},{2,18},{10... | collective-permute-start | bytes 294920 | tf_op jit(solution)/shard_map/ppermute | solution.py:845
  43.1 6.1 %collective-permute-start.5 = (f32[192,128]{1,0:T(8,128)S(1)}, f32[192,128]{1,0:T(8,128)S(1)}, u32[]{:S(2)}, u32[]{:S(2)}) collective-permute-start(f32[192,128]{1,0:T(8,128)S(1)} %get-tuple-element.30), channel_id=1, source_target_pairs={{0,24},{8,0},{16,8},{24,16},{1,25},{9,1},{17,9},{25,17},{2,26},{10... | collective-permute-start | bytes 294920 | tf_op jit(solution)/shard_map/ppermute | solution.py:845
  51.1 11.0 %all-to-all-start.1 = ((f32[8,32,128]{2,1,0:T(8,128)}), f32[8,32,128]{2,1,0:T(8,128)S(1)}, u32[]{:S(2)}, u32[]{:S(2)}) async-start(f32[8,32,128]{2,1,0:T(8,128)} %get-tuple-element.33), calls=%async_computation.1 | async-start | bytes 262144 | tf_op jit(solution)/shard_map/all_to_all | solution.py:876

commit v6 on v5

--- a/solution.py
+++ b/solution.py
@@ -336,62 +336,51 @@
     )(near(i_tiles))
 
 
-def prepare_k_kernel(couple_ref, k_ref, k_tile, k_map, k_rows, k_carry, f_ref):
+def prepare_k_kernel(couple_ref, k_ref, k_tile, k_map, k_rows, k_carry):
     fields, length = k_ref.shape[1], k_ref.shape[2]
-    lane = lax.broadcasted_iota(jnp.int32, (8, LANES), 1)
     row8 = lax.broadcasted_iota(jnp.int32, (8, LANES), 0)
     row_n = lax.broadcasted_iota(jnp.int32, (length, length), 0)
     lane_n = lax.broadcasted_iota(jnp.int32, (length, length), 1)
     turn = jnp.where(row_n + lane_n == length - 1, 1.0, 0.0).astype(BF16)
-
-    def edge_rows(direction, f):
-        e0 = couple_ref[0, direction, f]
-        e1 = couple_ref[1, direction, f]
-        e2 = couple_ref[2, direction, f]
-        first = jnp.where((row8 == 0) & (lane == 0), e0, 0.0)
-        first = jnp.where((row8 == 0) & (lane == 1), e2, first)
-        return jnp.where((row8 == 1) & (lane == 0), e1, first)
-
-    f_ref[...] = jnp.zeros(f_ref.shape, F32)
-    k_carry[...] = jnp.zeros(k_carry.shape, F32)
+    columns = jnp.zeros((length, length), F32)
     for f in range(fields):
         low, up = k_ref[0, f], k_ref[1, f]
-        whole = turn_rows(product_nn(up, turn_rows(low, turn)), turn)
+        whole = product_nn(up, turn_rows(low, turn))
         k_map[f] = whole
-        low_rows = product_nt(edge_rows(2, f), low)
-        across = product_nt(turn_lanes(low_rows, turn), up)
-        up_rows = product_nt(edge_rows(3, f), up)
-        both = jnp.concatenate([across[0:2], up_rows[0:2], jnp.zeros((4, length), F32)], axis=0)
-        both = turn_lanes(both, turn)
         k_rows[f] = jnp.concatenate(
-            [
-                low[length - 1 : length],
-                low[length - 2 : length - 1],
-                whole[0:2],
-                jnp.zeros((4, length), F32),
-            ],
+            [x[length - q : length - q + 1] for x in (low, whole) for q in (1, 2)]
+            + [jnp.zeros((4, length), F32)],
             axis=0,
         )
-        for a in range(4):
-            k_carry[a, f : f + 1, :] = both[a : a + 1]
-        for a in range(2):
-            f_ref[a, f : f + 1, :] = low_rows[a : a + 1]
-    end = length - 1
+        for m, matrix in enumerate((low, up, whole)):
+            for q in range(2):
+                value = jnp.broadcast_to(matrix[:, q : q + 1], (length, length))
+                columns = jnp.where(lane_n == 16 * m + 8 * q + f, value, columns)
+    columns = columns.T
+    low0, low1, up0, up1, all0, all1 = (columns[8 * q : 8 * q + 8] for q in range(6))
+
+    def edges(direction):
+        table = []
+        for c in range(3):
+            value = jnp.zeros((8, LANES), F32)
+            for f in range(fields):
+                value = jnp.where(row8 == f, couple_ref[c, direction, f], value)
+            table.append(value)
+        return table
+
+    e0, e1, e2 = edges(2)
+    d0, d1, d2 = edges(3)
+    first = (low0 * e0 + low1 * e2, low0 * e1)
+    through = (all0 * e0 + all1 * e2, all0 * e1)
+    second = (up0 * d0 + up1 * d2, up0 * d1)
+    turned = turn_lanes(jnp.concatenate(through + second, axis=0), turn)
+    for a in range(4):
+        k_carry[a] = turned[8 * a : 8 * a + 8]
+    ends = [(pair, p) for p in (length - 1, length - 2) for pair in (0, 1)]
     k_tile[...] = lay_out(
-        [
-            -col(f_ref[0], end),
-            -col(f_ref[1], end),
-            -col(f_ref[0], end - 1),
-            -col(f_ref[1], end - 1),
-            -col(k_carry[2], 0),
-            -col(k_carry[3], 0),
-            -col(k_carry[2], 1),
-            -col(k_carry[3], 1),
-            col(k_carry[0], 0),
-            col(k_carry[1], 0),
-            col(k_carry[0], 1),
-            col(k_carry[1], 1),
-        ]
+        [-col(first[pair], p) for pair, p in ends]
+        + [-col(second[pair], p) for pair, p in ends]
+        + [col(through[pair], p) for pair, p in ends]
     )
 
 
@@ -410,7 +399,6 @@
             pl.BlockSpec(memory_space=pltpu.VMEM),
         ],
         out_specs=(pl.BlockSpec(memory_space=pltpu.VMEM),) * 4,
-        scratch_shapes=[pltpu.VMEM((2, 8, length), F32)],
         compiler_params=PARAMS,
         name="prepare_k",
     )(couplings, near(k_factors))
@@ -705,7 +693,13 @@
         ends = product_nt(rows_ref[f], block)
         for a in range(4):
             end_ref[a * fields + f : a * fields + f + 1, :] = ends[a : a + 1]
-    end_ref[4 * fields : 4 * fields + 8] = k_tile_ref[...]
+    lane = lax.broadcasted_iota(jnp.int32, (fields, LANES), 1)
+    for a in range(4):
+        part = end_ref[a * fields : (a + 1) * fields]
+        for q in range(3):
+            entry = col(k_tile_ref[0:fields], 3 * a + q)
+            part = jnp.where(lane == rows_j * q + rows_j - 1, entry, part)
+        end_ref[a * fields : (a + 1) * fields] = part
     for d in range(send_ref.shape[0]):
         send_ref[d] = end_ref[...]
 
@@ -718,11 +712,11 @@
         functools.partial(middle_kernel, peers=peers, base=base, fields=fields, cells_i=cells_i),
         out_shape=(
             pltpu.VMEM(start.shape, F32),
-            pltpu.VMEM((owners, 4 * fields + 8, LANES), F32),
+            pltpu.VMEM((owners, 4 * fields, LANES), F32),
         ),
         in_specs=[smem, smem] + [vmem] * (3 + 2 * peers),
         out_specs=(vmem, vmem),
-        scratch_shapes=[pltpu.VMEM((4 * fields + 8, LANES), F32)],
+        scratch_shapes=[pltpu.VMEM((4 * fields, LANES), F32)],
         compiler_params=PARAMS,
         name="middle",
     )(mine, own, *map(near, (start, k_rows, k_tile, *tiles, *got)))
@@ -731,9 +725,13 @@
 def apply_k_kernel(field_ref, map_ref, out_ref):
     fields = map_ref.shape[0]
     rows = field_ref.shape[0] // fields
+    length = map_ref.shape[1]
+    row_n = lax.broadcasted_iota(jnp.int32, (length, length), 0)
+    lane_n = lax.broadcasted_iota(jnp.int32, (length, length), 1)
+    turn = jnp.where(row_n + lane_n == length - 1, 1.0, 0.0).astype(BF16)
     for f in range(fields):
         at = slice(f * rows, (f + 1) * rows)
-        out_ref[at] = product_nt(field_ref[at], map_ref[f])
+        out_ref[at] = turn_lanes(product_nt(field_ref[at], map_ref[f]), turn)
 
 
 def apply_k(field, k_map):
@@ -754,9 +752,14 @@
     rows = cells_i * rows_j
     blocks = got_ref.shape[0]
     mine = mine_ref[0]
-    zero = jnp.zeros((8, LANES), F32)
-    entry = [[col(got_ref[m, 4 * fields : 4 * fields + 8], c) for c in range(12)] for m in range(blocks)]
-    part = [[got_ref[m, fields * a : fields * a + 8] for a in range(4)] for m in range(blocks)]
+    zero = jnp.zeros((fields, LANES), F32)
+    part = [
+        [got_ref[m, fields * a : fields * (a + 1)] for a in range(4)] for m in range(blocks)
+    ]
+    entry = [
+        [col(part[m][c // 3], rows_j * (c % 3) + rows_j - 1) for c in range(12)]
+        for m in range(blocks)
+    ]
     states = []
     state = [zero, zero]
     for m in range(blocks):
@@ -845,6 +848,10 @@
         return lax.ppermute(value, "line", [(s, (s + shift) % peers) for s in range(peers)])
 
     tiles = [own] + [shifted(own, m) for m in range(1, peers)]
+    couple = couplings[0, 0].transpose(1, 0, 2)
+    couple, _ = lax.optimization_barrier((couple, outgoing))
+    k_tile, k_map, k_rows, k_carry = prepare_k(couple, k_factors[0])
+    counts, _ = lax.optimization_barrier((counts, k_tile))
     begun = scatter_own(
         block,
         counts,
@@ -867,9 +874,6 @@
         base,
     )
     got = [ends[0]] + [shifted(ends[m], m) for m in range(1, peers)]
-    couple = couplings[0, 0].transpose(1, 0, 2)
-    couple, _ = lax.optimization_barrier((couple, ends[0]))
-    k_tile, k_map, k_rows, k_carry = prepare_k(couple, k_factors[0])
     start, message = middle(
         line, own, start, k_rows, k_tile, tiles, got, base, owners, fields, cells_i
     )

time: 63.6 us -> 62.5 us (0.983)
  Pallas kernels: 34.6 us -> 32.3 us
  waiting for transfers between devices: 11.8 us -> 12.6 us
    ppermute x6, waiting for transfers between devices: 0.03 us -> 3.38 us  [shifted(): lax.ppermute(value, 'line', [(s, (s + shift) % peers) for s in range(peer...]
    pallas_call x1, Pallas kernels: 4.62 us -> 2.21 us  [prepare_k(): pl.pallas_call(prepare_k_kernel, out_shape=(pltpu.VMEM((8, LANES), F32),...]
    all_to_all x1, waiting for transfers between devices: 4.85 us -> 2.58 us  [per_device(): lax.all_to_all(outgoing, 'block', split_axis=0, concat_axis=0, tiled=True)]
    pallas_call x1, Pallas kernels: 0.38 us -> 1.09 us  [apply_k(): pl.pallas_call(apply_k_kernel, out_shape=pltpu.VMEM(field.shape, F32), in...]
  transfers between devices with their start and end apart: 8 -> 8, of which waited for: 2 -> 4; matrix products, arithmetic and copies ran while one was open for 0% -> 0% of each run, Pallas kernels for 14% -> 12%
where the time goes in v6:
time: 62.5 us; the launch traced here: 62.2 us
  Pallas kernels  32.3 us (52%)
  starting transfers between devices  16.1 us (26%)
  waiting for transfers between devices  12.6 us (20%)
  local copies, waits for them, and re-layouts  0.98 us (2%)
    pallas_call x1, Pallas kernels, scatter(): pl.pallas_call(functools.partial(scatter_kernel, peers=peers, chunk=chunk...  13.8 us
    pallas_call x1, Pallas kernels, gather(): pl.pallas_call(functools.partial(gather_kernel, chunk=chunk, group=group)...  7.95 us
    all_to_all x1, starting transfers between devices, per_device(): lax.all_to_all(outgoing, 'block', split_axis=0, concat_axis=0, tiled=True)  7.43 us
    all_to_all x1, waiting for transfers between devices, per_device(): lax.all_to_all(message, 'block', split_axis=0, concat_axis=0, tiled=True)  6.66 us
    ppermute x6, starting transfers between devices, shifted(): lax.ppermute(value, 'line', [(s, (s + shift) % peers) for s in range(peer...  4.82 us
    all_to_all x1, starting transfers between devices, per_device(): lax.all_to_all(message, 'block', split_axis=0, concat_axis=0, tiled=True)  3.83 us
    pallas_call x1, Pallas kernels, scatter_own(): pl.pallas_call(functools.partial(scatter_own_kernel, sizes=sizes, chunk=c...  3.8 us
    ppermute x6, waiting for transfers between devices, shifted(): lax.ppermute(value, 'line', [(s, (s + shift) % peers) for s in range(peer...  3.38 us
  transfers between devices with their start and end apart: 8, of which 4 were waited for; matrix products, arithmetic and copies ran while one was open for 0% of the time, Pallas kernels for 12%

profile of v6, /device:TPU:0, one launch (start us, length us, event | category | flops | bytes accessed | tf_op | source)
XLA Modules:
  0.0 62.2 jit_solution(11522835219447579669)
XLA Ops:
  0.0 7.9 %gather.1 = (f32[8,96,128]{2,1,0:T(8,128)}, bf16[384,256]{1,0:T(8,128)(2,1)S(1)}, bf16[384,256]{1,0:T(8,128)(2,1)S(1)}) custom-call(s32[1]{0:T(128)} %bitcast.mine_ref.refs_1_, s32[8]{0:T(128)} %bitcast.31, s32[8,2048]{1,0:T(8,128)} %bitcast.26, f32[6,15,8,128]{3,2,1,0:T(8,128)} %bitcast.29), custom_call_target="tpu_custom_call" | custom-call | tf_op jit(solution)/shard_map/gather/pallas_call | solution.py:262
  8.0 0.0 copy-start.6
  8.0 7.4 %all-to-all-start = ((f32[8,96,128]{2,1,0:T(8,128)}), f32[8,96,128]{2,1,0:T(8,128)S(1)}, u32[]{:S(2)}, u32[]{:S(2)}) async-start(f32[8,96,128]{2,1,0:T(8,128)} %get-tuple-element.21), calls=%async_computation | async-start | bytes 786432 | tf_op jit(solution)/shard_map/all_to_all | solution.py:838
  15.4 0.7 %slice-done = f32[1,1,2,3,6]{4,2,3,1,0:T(2,128)S(1)} async-done(((f32[1,1,4,3,6]{4,2,3,1,0:T(4,128)}), f32[1,1,2,3,6]{4,2,3,1,0:T(2,128)S(1)}, s32[]{:S(2)}) %slice-start) | async-done | bytes 168 | tf_op jit(solution)/shard_map/slice | solution.py:842
  16.1 0.1 copy.17
  16.2 0.1 reshape.13
  16.3 0.1 reshape.12
  16.4 0.2 prepare_i.1.refs_8_.refs_1_.refs_5_
  16.6 0.0 copy-start.5
  16.6 0.7 %collective-permute-start.2 = (f32[8,128]{1,0:T(8,128)S(1)}, f32[8,128]{1,0:T(8,128)S(1)}, u32[]{:S(2)}, u32[]{:S(2)}) collective-permute-start(f32[8,128]{1,0:T(8,128)S(1)} %prepare_i.1.refs_8_.refs_1_.refs_5_), channel_id=1, source_target_pairs={{0,24},{8,0},{16,8},{24,16},{1,25},{9,1},{17,9},{25,17},{2,26},{10... | collective-permute-start | bytes 12296 | tf_op jit(solution)/shard_map/ppermute | solution.py:848
  17.3 1.5 %collective-permute-start.1 = (f32[8,128]{1,0:T(8,128)S(1)}, f32[8,128]{1,0:T(8,128)S(1)}, u32[]{:S(2)}, u32[]{:S(2)}) collective-permute-start(f32[8,128]{1,0:T(8,128)S(1)} %prepare_i.1.refs_8_.refs_1_.refs_5_), channel_id=1, source_target_pairs={{0,16},{8,24},{16,0},{24,8},{1,17},{9,25},{17,1},{25,9},{2,18},{10... | collective-permute-start | bytes 12296 | tf_op jit(solution)/shard_map/ppermute | solution.py:848
  18.8 0.2 collective-permute-start
  19.0 0.0 copy-start.4
  19.0 2.2 %prepare_k.1 = (f32[8,128]{1,0:T(8,128)S(1)}, f32[6,128,128]{2,1,0:T(8,128)S(1)}, f32[6,8,128]{2,1,0:T(8,128)S(1)}, f32[4,8,128]{2,1,0:T(8,128)S(1)}) custom-call(f32[3,4,6]{2,1,0:T(4,128)S(1)} %bitcast.28, f32[2,6,128,128]{3,2,1,0:T(8,128)S(1)} %bitcast.22), custom_call_target="tpu_custom_call" | custom-call | tf_op jit(solution)/shard_map/prepare_k/pallas_call | solution.py:389
  21.2 0.0 copy-done.3
  21.3 0.0 copy-start.2
  21.3 3.8 %scatter_own.1.refs_3_ = f32[720,256]{1,0:T(8,128)S(1)} custom-call(s32[1]{0:T(128)} %bitcast.mine_ref.refs_1_, s32[8]{0:T(128)} %bitcast.32, bf16[384,256]{1,0:T(8,128)(2,1)S(1)} %get-tuple-element.25.high_ref, bf16[384,256]{1,0:T(8,128)(2,1)S(1)} %get-tuple-element.26.low_ref, s32[8,2048]{1,0:T(8,128)S(1)} %bitcast.27, s32[8,2048]{1,0:T(8,128)S(1)} %bitcast.24, ...), custom_call_target="tpu_custom_call" | custom-call | tf_op jit(solution)/shard_map/scatter_own/pallas_call | solution.py:528
  25.1 0.0 collective-permute-done.2.refs_11_.refs_8_
  25.1 0.0 collective-permute-done.1.refs_10_.refs_7_
  25.1 0.0 collective-permute-done.refs_9_.refs_6_
  25.1 2.6 %all-to-all-done.refs_4_ = f32[8,96,128]{2,1,0:T(8,128)S(1)} async-done(((f32[8,96,128]{2,1,0:T(8,128)}), f32[8,96,128]{2,1,0:T(8,128)S(1)}, u32[]{:S(2)}, u32[]{:S(2)}) %all-to-all-start) | async-done | bytes 393248 | tf_op jit(solution)/shard_map/all_to_all | solution.py:838
  27.7 13.8 %scatter.1 = (f32[768,128]{1,0:T(8,128)S(1)}, f32[192,128]{1,0:T(8,128)S(1)}, f32[192,128]{1,0:T(8,128)S(1)}, f32[192,128]{1,0:T(8,128)S(1)}, f32[192,128]{1,0:T(8,128)S(1)}) custom-call(s32[1]{0:T(128)} %bitcast.1.refs_0_, s32[1]{0:T(128)} %bitcast.mine_ref.refs_1_, f32[3,8,128]{2,1,0:T(8,128)S(1)} %select_maximum_fusion.i_ref.refs_2_, ...), custom_call_target="tpu_custom_call" | custom-call | tf_op jit(solution)/shard_map/scatter/pallas_call | solution.py:627
  41.5 0.1 collective-permute-start.3
  41.6 1.0 %collective-permute-start.4 = (f32[192,128]{1,0:T(8,128)S(1)}, f32[192,128]{1,0:T(8,128)S(1)}, u32[]{:S(2)}, u32[]{:S(2)}) collective-permute-start(f32[192,128]{1,0:T(8,128)S(1)} %get-tuple-element.31), channel_id=1, source_target_pairs={{0,16},{8,24},{16,0},{24,8},{1,17},{9,25},{17,1},{25,9},{2,18},{10... | collective-permute-start | bytes 294920 | tf_op jit(solution)/shard_map/ppermute | solution.py:848
  42.5 1.4 %collective-permute-start.5 = (f32[192,128]{1,0:T(8,128)S(1)}, f32[192,128]{1,0:T(8,128)S(1)}, u32[]{:S(2)}, u32[]{:S(2)}) collective-permute-start(f32[192,128]{1,0:T(8,128)S(1)} %get-tuple-element.32), channel_id=1, source_target_pairs={{0,24},{8,0},{16,8},{24,16},{1,25},{9,1},{17,9},{25,17},{2,26},{10... | collective-permute-start | bytes 294920 | tf_op jit(solution)/shard_map/ppermute | solution.py:848
  43.9 2.1 %collective-permute-done.3.refs_10_ = f32[192,128]{1,0:T(8,128)S(1)} collective-permute-done((f32[192,128]{1,0:T(8,128)S(1)}, f32[192,128]{1,0:T(8,128)S(1)}, u32[]{:S(2)}, u32[]{:S(2)}) %collective-permute-start.3) | collective-permute-done | bytes 98336 | tf_op jit(solution)/shard_map/ppermute | solution.py:848
  46.0 1.3 %collective-permute-done.4.refs_11_ = f32[192,128]{1,0:T(8,128)S(1)} collective-permute-done((f32[192,128]{1,0:T(8,128)S(1)}, f32[192,128]{1,0:T(8,128)S(1)}, u32[]{:S(2)}, u32[]{:S(2)}) %collective-permute-start.4) | collective-permute-done | bytes 98336 | tf_op jit(solution)/shard_map/ppermute | solution.py:848
  47.3 1.9 %middle.1 = (f32[768,128]{1,0:T(8,128)S(1)}, f32[8,24,128]{2,1,0:T(8,128)}) custom-call(s32[1]{0:T(128)} %bitcast.1.refs_0_, f32[8,128]{1,0:T(8,128)S(1)} %prepare_i.1.refs_8_.refs_1_.refs_5_, f32[768,128]{1,0:T(8,128)S(1)} %get-tuple-element.27.refs_2_, f32[6,8,128]{2,1,0:T(8,128)S(1)} %get-tuple-element.28.refs_3_, ...), custom_call_target="tpu_custom_call" | custom-call | tf_op jit(solution)/shard_map/middle/pallas_call | solution.py:711
  49.2 3.8 %all-to-all-start.1 = ((f32[8,24,128]{2,1,0:T(8,128)}), f32[8,24,128]{2,1,0:T(8,128)S(1)}, u32[]{:S(2)}, u32[]{:S(2)}) async-start(f32[8,24,128]{2,1,0:T(8,128)} %get-tuple-element.35), calls=%async_computation.1 | async-start | bytes 196608 | tf_op jit(solution)/shard_map/all_to_all | solution.py:880
  53.0 1.1 %apply_k.1.start_ref = f32[768,128]{1,0:T(8,128)S(1)} custom-call(f32[768,128]{1,0:T(8,128)S(1)} %get-tuple-element.33.field_ref, f32[6,128,128]{2,1,0:T(8,128)S(1)} %get-tuple-element.34.map_ref), custom_call_target="tpu_custom_call" | custom-call | tf_op jit(solution)/shard_map/apply_k/pallas_call | solution.py:739
  54.1 6.7 %all-to-all-done.1.got_ref = f32[8,24,128]{2,1,0:T(8,128)S(1)} async-done(((f32[8,24,128]{2,1,0:T(8,128)}), f32[8,24,128]{2,1,0:T(8,128)S(1)}, u32[]{:S(2)}, u32[]{:S(2)}) %all-to-all-start.1) | async-done | bytes 98336 | tf_op jit(solution)/shard_map/all_to_all | solution.py:880
  60.8 1.4 %finish.1 = f32[6,15,8,128]{3,2,1,0:T(8,128)} custom-call(s32[1]{0:T(128)} %bitcast.mine_ref.refs_1_, f32[768,128]{1,0:T(8,128)S(1)} %apply_k.1.start_ref, f32[8,24,128]{2,1,0:T(8,128)S(1)} %all-to-all-done.1.got_ref, f32[4,8,128]{2,1,0:T(8,128)S(1)} %get-tuple-element.36.carry_ref), custom_call_target="tpu_custom_call" | custom-call | tf_op jit(solution)/shard_map/finish/pallas_call | solution.py:806
  (13 shorter events, 0.0 us)
Async XLA Ops:
  0.0 19.0 %copy-start.1 = (f32[1,2,6,128,128]{4,3,2,1,0:T(8,128)S(1)}, f32[1,2,6,128,128]{4,3,2,1,0:T(8,128)}, u32[]{:S(2)}) copy-start(f32[1,2,6,128,128]{4,3,2,1,0:T(8,128)} %param.12) | copy-start | bytes 2359300
  8.0 8.3 %copy-start.6 = (f32[1,2,6,8,8]{4,3,2,1,0:T(8,128)S(1)}, f32[1,2,6,8,8]{4,3,2,1,0:T(8,128)}, u32[]{:S(2)}) copy-start(f32[1,2,6,8,8]{4,3,2,1,0:T(8,128)} %param.11) | copy-start | bytes 9220
  8.0 19.7 %all-to-all-start = ((f32[8,96,128]{2,1,0:T(8,128)}), f32[8,96,128]{2,1,0:T(8,128)S(1)}, u32[]{:S(2)}, u32[]{:S(2)}) async-start(f32[8,96,128]{2,1,0:T(8,128)} %get-tuple-element.21), calls=%async_computation | async-start | bytes 786432 | tf_op jit(solution)/shard_map/all_to_all | solution.py:838
  15.4 0.7 %slice-start = ((f32[1,1,4,3,6]{4,2,3,1,0:T(4,128)}), f32[1,1,2,3,6]{4,2,3,1,0:T(2,128)S(1)}, s32[]{:S(2)}) async-start(f32[1,1,4,3,6]{4,2,3,1,0:T(4,128)} %param.13), calls=%async_computation.2 | async-start | bytes 6144 | tf_op jit(solution)/shard_map/slice | solution.py:842
  16.6 2.4 %copy-start.5 = (f32[1,1,4,3,6]{4,2,3,1,0:T(4,128)S(1)}, f32[1,1,4,3,6]{4,2,3,1,0:T(4,128)}, u32[]{:S(2)}) copy-start(f32[1,1,4,3,6]{4,2,3,1,0:T(4,128)} %param.13) | copy-start | bytes 868
  16.6 8.5 %collective-permute-start.2 = (f32[8,128]{1,0:T(8,128)S(1)}, f32[8,128]{1,0:T(8,128)S(1)}, u32[]{:S(2)}, u32[]{:S(2)}) collective-permute-start(f32[8,128]{1,0:T(8,128)S(1)} %prepare_i.1.refs_8_.refs_1_.refs_5_), channel_id=1, source_target_pairs={{0,24},{8,0},{16,8},{24,16},{1,25},{9,1},{17,9},{25,17},{2,26},{10... | collective-permute-start | bytes 12296 | tf_op jit(solution)/shard_map/ppermute | solution.py:848
  17.3 7.8 %collective-permute-start.1 = (f32[8,128]{1,0:T(8,128)S(1)}, f32[8,128]{1,0:T(8,128)S(1)}, u32[]{:S(2)}, u32[]{:S(2)}) collective-permute-start(f32[8,128]{1,0:T(8,128)S(1)} %prepare_i.1.refs_8_.refs_1_.refs_5_), channel_id=1, source_target_pairs={{0,16},{8,24},{16,0},{24,8},{1,17},{9,25},{17,1},{25,9},{2,18},{10... | collective-permute-start | bytes 12296 | tf_op jit(solution)/shard_map/ppermute | solution.py:848
  18.8 6.3 %collective-permute-start = (f32[8,128]{1,0:T(8,128)S(1)}, f32[8,128]{1,0:T(8,128)S(1)}, u32[]{:S(2)}, u32[]{:S(2)}) collective-permute-start(f32[8,128]{1,0:T(8,128)S(1)} %prepare_i.1.refs_8_.refs_1_.refs_5_), channel_id=1, source_target_pairs={{0,8},{8,16},{16,24},{24,0},{1,9},{9,17},{17,25},{25,1},{2,10},{10... | collective-permute-start | bytes 12296 | tf_op jit(solution)/shard_map/ppermute | solution.py:848
  19.0 2.2 %copy-start = (f32[1,1,3,8,2048]{4,3,2,1,0:T(8,128)S(1)}, f32[1,1,3,8,2048]{4,3,2,1,0:T(8,128)}, u32[]{:S(2)}) copy-start(f32[1,1,3,8,2048]{4,3,2,1,0:T(8,128)} %param.17) | copy-start | bytes 589828
  19.0 2.2 %copy-start.3 = (s32[1,1,8,2048]{3,2,1,0:T(8,128)S(1)}, s32[1,1,8,2048]{3,2,1,0:T(8,128)}, u32[]{:S(2)}) copy-start(s32[1,1,8,2048]{3,2,1,0:T(8,128)} %param.16) | copy-start | bytes 196612
  19.0 2.2 %copy-start.4 = (s32[1,1,8,2048]{3,2,1,0:T(8,128)S(1)}, s32[1,1,8,2048]{3,2,1,0:T(8,128)}, u32[]{:S(2)}) copy-start(s32[1,1,8,2048]{3,2,1,0:T(8,128)} %param.14) | copy-start | bytes 196612
  21.3 6.4 %copy-start.2 = (f32[6,8,15,128]{3,1,2,0:T(8,128)S(1)}, f32[6,8,15,128]{3,1,2,0:T(8,128)}, u32[]{:S(2)}) copy-start(f32[6,8,15,128]{3,1,2,0:T(8,128)} %param.9) | copy-start | bytes 1105924
  41.5 4.5 %collective-permute-start.3 = (f32[192,128]{1,0:T(8,128)S(1)}, f32[192,128]{1,0:T(8,128)S(1)}, u32[]{:S(2)}, u32[]{:S(2)}) collective-permute-start(f32[192,128]{1,0:T(8,128)S(1)} %get-tuple-element.30), channel_id=1, source_target_pairs={{0,8},{8,16},{16,24},{24,0},{1,9},{9,17},{17,25},{25,1},{2,10},{10... | collective-permute-start | bytes 294920 | tf_op jit(solution)/shard_map/ppermute | solution.py:848
  41.6 5.7 %collective-permute-start.4 = (f32[192,128]{1,0:T(8,128)S(1)}, f32[192,128]{1,0:T(8,128)S(1)}, u32[]{:S(2)}, u32[]{:S(2)}) collective-permute-start(f32[192,128]{1,0:T(8,128)S(1)} %get-tuple-element.31), channel_id=1, source_target_pairs={{0,16},{8,24},{16,0},{24,8},{1,17},{9,25},{17,1},{25,9},{2,18},{10... | collective-permute-start | bytes 294920 | tf_op jit(solution)/shard_map/ppermute | solution.py:848
  42.5 4.8 %collective-permute-start.5 = (f32[192,128]{1,0:T(8,128)S(1)}, f32[192,128]{1,0:T(8,128)S(1)}, u32[]{:S(2)}, u32[]{:S(2)}) collective-permute-start(f32[192,128]{1,0:T(8,128)S(1)} %get-tuple-element.32), channel_id=1, source_target_pairs={{0,24},{8,0},{16,8},{24,16},{1,25},{9,1},{17,9},{25,17},{2,26},{10... | collective-permute-start | bytes 294920 | tf_op jit(solution)/shard_map/ppermute | solution.py:848
  49.2 11.6 %all-to-all-start.1 = ((f32[8,24,128]{2,1,0:T(8,128)}), f32[8,24,128]{2,1,0:T(8,128)S(1)}, u32[]{:S(2)}, u32[]{:S(2)}) async-start(f32[8,24,128]{2,1,0:T(8,128)} %get-tuple-element.35), calls=%async_computation.1 | async-start | bytes 196608 | tf_op jit(solution)/shard_map/all_to_all | solution.py:880

commit v7 on v6

--- a/solution.py
+++ b/solution.py
@@ -125,8 +125,7 @@
 
 
 def gather_kernel(
-    mine_ref,
-    count_ref,
+    count_hbm,
     cell_hbm,
     field_hbm,
     out_hbm,
@@ -139,6 +138,8 @@
     hot_ref,
     found_ref,
     list_ref,
+    count_ref,
+    count_sem,
     cell_sem,
     field_sem,
     out_sem,
@@ -158,10 +159,12 @@
         for f in range(fields)
     ]
     cell_load = pltpu.make_async_copy(cell_hbm, cell_ref, cell_sem)
+    count_load = pltpu.make_async_copy(count_hbm, count_ref, count_sem)
+    count_load.start()
     cell_load.start()
     for load in loads:
         load.start()
-    mine = mine_ref[0]
+    mine = lax.axis_index("block")
 
     def send(d):
         return pltpu.make_async_copy(out_ref.at[d], out_hbm.at[d], out_sem.at[d])
@@ -169,6 +172,8 @@
     out_ref[...] = jnp.zeros(out_ref.shape, F32)
     send(mine).start()
     place_ref[...] = places(2 * LANES, LANES)
+
+    count_load.wait()
 
     def list_owner(d, total):
         live = jnp.maximum(lax.div(count_ref[d] + (chunk - 1), chunk), 1)
@@ -251,12 +256,11 @@
     lax.fori_loop(0, owners, wait_body, 0)
 
 
-def gather(mine, count, cell, field, chunk=256, group=4):
+def gather(count, cell, field, chunk=256, group=4):
     fields, _, cells_i, _ = field.shape
     owners, capacity = cell.shape
     table = (fields * cells_i // 2 * 16, 2 * LANES)
     out = (owners, fields * capacity // LANES, LANES)
-    smem = pl.BlockSpec(memory_space=pltpu.SMEM)
     vmem = pl.BlockSpec(memory_space=pltpu.VMEM)
     hbm = pl.BlockSpec(memory_space=pltpu.HBM)
     return pl.pallas_call(
@@ -266,7 +270,7 @@
             pltpu.VMEM(table, BF16),
             pltpu.VMEM(table, BF16),
         ),
-        in_specs=[smem, smem, hbm, hbm],
+        in_specs=[hbm, hbm, hbm],
         out_specs=(hbm, vmem, vmem),
         scratch_shapes=[
             pltpu.VMEM(cell.shape, jnp.int32),
@@ -276,13 +280,15 @@
             pltpu.VMEM((2 * LANES, group * chunk), BF16),
             pltpu.VMEM((table[0], group * chunk), F32),
             pltpu.SMEM((owners * capacity // chunk,), jnp.int32),
+            pltpu.SMEM((owners,), jnp.int32),
+            pltpu.SemaphoreType.DMA(()),
             pltpu.SemaphoreType.DMA(()),
             pltpu.SemaphoreType.DMA((fields,)),
             pltpu.SemaphoreType.DMA((owners,)),
         ],
         compiler_params=PARAMS,
         name="gather",
-    )(mine, far(count), far(cell), far(field))
+    )(far(count), far(cell), far(field))
 
 
 def lay_out(entries):
@@ -293,11 +299,22 @@
     return tile
 
 
-def prepare_i_kernel(i_ref, i_out, *, cells_i):
-    lower, upper, edge = i_ref[0], i_ref[1], i_ref[2]
-
-    def edges(matrix, at):
-        e0, e1, e2 = col(edge, at), col(edge, at + 1), col(edge, at + 2)
+def edge_entries(couple_ref, direction):
+    row = lax.broadcasted_iota(jnp.int32, (8, LANES), 0)
+    table = []
+    for c in range(3):
+        value = jnp.zeros((8, LANES), F32)
+        for f in range(couple_ref.shape[2]):
+            value = jnp.where(row == f, couple_ref[c, direction, f], value)
+        table.append(value)
+    return table
+
+
+def prepare_i_kernel(couple_ref, i_ref, i_out, *, cells_i):
+    lower, upper = i_ref[0], i_ref[1]
+
+    def edges(matrix, direction):
+        e0, e1, e2 = edge_entries(couple_ref, direction)
         table = []
         for p in range(cells_i):
             first, second = col(matrix, p * cells_i), col(matrix, p * cells_i + 1)
@@ -305,7 +322,7 @@
         return table
 
     low_edge = edges(lower, 0)
-    up_edge = edges(upper, 3)
+    up_edge = edges(upper, 1)
     through = []
     for p in range(cells_i):
         total = [jnp.zeros((8, LANES), F32), jnp.zeros((8, LANES), F32)]
@@ -325,20 +342,22 @@
     i_out[...] = lay_out(entries)
 
 
-def prepare_i(i_tiles, cells_i):
+def prepare_i(couplings, i_tiles, cells_i):
     return pl.pallas_call(
         functools.partial(prepare_i_kernel, cells_i=cells_i),
         out_shape=pltpu.VMEM((8, LANES), F32),
-        in_specs=[pl.BlockSpec(memory_space=pltpu.VMEM)],
+        in_specs=[
+            pl.BlockSpec(memory_space=pltpu.SMEM),
+            pl.BlockSpec(memory_space=pltpu.VMEM),
+        ],
         out_specs=pl.BlockSpec(memory_space=pltpu.VMEM),
         compiler_params=PARAMS,
         name="prepare_i",
-    )(near(i_tiles))
+    )(couplings, near(i_tiles))
 
 
 def prepare_k_kernel(couple_ref, k_ref, k_tile, k_map, k_rows, k_carry):
     fields, length = k_ref.shape[1], k_ref.shape[2]
-    row8 = lax.broadcasted_iota(jnp.int32, (8, LANES), 0)
     row_n = lax.broadcasted_iota(jnp.int32, (length, length), 0)
     lane_n = lax.broadcasted_iota(jnp.int32, (length, length), 1)
     turn = jnp.where(row_n + lane_n == length - 1, 1.0, 0.0).astype(BF16)
@@ -359,17 +378,8 @@
     columns = columns.T
     low0, low1, up0, up1, all0, all1 = (columns[8 * q : 8 * q + 8] for q in range(6))
 
-    def edges(direction):
-        table = []
-        for c in range(3):
-            value = jnp.zeros((8, LANES), F32)
-            for f in range(fields):
-                value = jnp.where(row8 == f, couple_ref[c, direction, f], value)
-            table.append(value)
-        return table
-
-    e0, e1, e2 = edges(2)
-    d0, d1, d2 = edges(3)
+    e0, e1, e2 = edge_entries(couple_ref, 2)
+    d0, d1, d2 = edge_entries(couple_ref, 3)
     first = (low0 * e0 + low1 * e2, low0 * e1)
     through = (all0 * e0 + all1 * e2, all0 * e1)
     second = (up0 * d0 + up1 * d2, up0 * d1)
@@ -467,7 +477,6 @@
 
 
 def scatter_own_kernel(
-    mine_ref,
     count_ref,
     high_ref,
     low_ref,
@@ -489,7 +498,7 @@
     total_ref[...] = jnp.zeros(total_ref.shape, F32)
     got_ref[...] = jnp.zeros(got_ref.shape, F32)
     place_ref[...] = places(2 * LANES, LANES)
-    mine = mine_ref[0]
+    mine = lax.axis_index("block")
     count = count_ref[mine]
 
     def put(f, row, value):
@@ -521,7 +530,7 @@
     lax.fori_loop(0, capacity // chunk, chunk_body, 0)
 
 
-def scatter_own(mine, count, tables, receptor, cell, weight, sizes, chunk=2048, gather_chunk=512):
+def scatter_own(count, tables, receptor, cell, weight, sizes, chunk=2048, gather_chunk=512):
     vmem = pl.BlockSpec(memory_space=pltpu.VMEM)
     smem = pl.BlockSpec(memory_space=pltpu.SMEM)
     fields, cells_j, cells_i = sizes
@@ -530,7 +539,7 @@
             scatter_own_kernel, sizes=sizes, chunk=chunk, gather_chunk=gather_chunk
         ),
         out_shape=pltpu.VMEM((fields * cells_i * cells_j, 2 * LANES), F32),
-        in_specs=[smem, smem] + [vmem] * 5,
+        in_specs=[smem] + [vmem] * 5,
         out_specs=vmem,
         scratch_shapes=[
             pltpu.VMEM((fields * cell.shape[1] // LANES, LANES), F32),
@@ -540,23 +549,25 @@
         ],
         compiler_params=PARAMS,
         name="scatter_own",
-    )(mine, far(count), *map(near, (*tables, receptor, cell, weight)))
+    )(far(count), *map(near, (*tables, receptor, cell, weight)))
 
 
 def scatter_kernel(*refs, peers, chunk, base):
-    mine_ref, block_ref, solve_ref, begun_ref, got_ref, cell_ref, weight_ref, residual_ref = refs[:8]
-    refs = refs[8:]
+    factor_ref, begun_ref, got_ref, cell_ref, weight_ref, residual_ref = refs[:6]
+    refs = refs[6:]
     tile_refs = refs[:peers]
     start_ref = refs[peers]
     send_refs = refs[1 + peers : 1 + 2 * peers]
-    total_ref, place_ref, fold_ref = refs[1 + 2 * peers :]
+    total_ref, place_ref, fold_ref, solve_ref, solve_sem = refs[1 + 2 * peers :]
     fields, cells_j, cells_i, _ = residual_ref.shape
     sources, capacity = cell_ref.shape
     rows_j = 16
     slot_rows = capacity // LANES
+    solve_load = pltpu.make_async_copy(factor_ref, solve_ref, solve_sem)
+    solve_load.start()
     total_ref[...] = begun_ref[...]
     place_ref[...] = places(LANES, LANES)
-    own = block_ref[0]
+    own = lax.axis_index("block")
 
     def source_body(at, carry):
         b = at + (at >= own).astype(jnp.int32)
@@ -580,7 +591,8 @@
     lax.fori_loop(0, sources - 1, source_body, 0)
 
     fold_ref[...] = total_ref[:, :LANES] + total_ref[:, LANES:]
-    mine = mine_ref[0]
+    solve_load.wait()
+    mine = lax.axis_index("line")
     tiles = [ref[...] for ref in tile_refs]
     onward = downstream_map(tiles, base, mine)
     turned = mat2([col(tiles[0], base + 4 + c) for c in range(4)], onward)
@@ -618,7 +630,7 @@
             send_refs[shift][at : at + rows_j] = jnp.where(ahead, e1, h1)
 
 
-def scatter(mine, block, solve_tiles, begun, got, cell, weight, residual, tiles, base, chunk=2048):
+def scatter(solve_tiles, begun, got, cell, weight, residual, tiles, base, chunk=2048):
     fields, cells_j, cells_i, _ = residual.shape
     peers = len(tiles)
     rows = fields * cells_i * 16
@@ -628,31 +640,36 @@
         functools.partial(scatter_kernel, peers=peers, chunk=chunk, base=base),
         out_shape=(pltpu.VMEM((rows, LANES), F32),)
         + (pltpu.VMEM((2 * fields * 16, LANES), F32),) * peers,
-        in_specs=[smem, smem, smem] + [vmem] * (5 + peers),
+        in_specs=[vmem] * (6 + peers),
         out_specs=(vmem,) * (1 + peers),
         scratch_shapes=[
             pltpu.VMEM((fields * cells_i * cells_j, 2 * LANES), F32),
             pltpu.VMEM((LANES, LANES), BF16),
             pltpu.VMEM((fields * cells_i * cells_j, LANES), F32),
+            pltpu.SMEM(solve_tiles.shape, F32),
+            pltpu.SemaphoreType.DMA(()),
         ],
         compiler_params=PARAMS,
         name="scatter",
-    )(mine, block, solve_tiles, *map(near, (begun, got, cell, weight, residual, *tiles)))
+    )(*map(near, (solve_tiles, begun, got, cell, weight, residual, *tiles)))
 
 
 def middle_kernel(*refs, peers, base, fields, cells_i):
-    mine_ref, own_ref, start_ref, rows_ref, k_tile_ref = refs[:5]
-    tile_refs = refs[5 : 5 + peers]
-    got_refs = refs[5 + peers : 5 + 2 * peers]
-    field_ref, send_ref, end_ref = refs[5 + 2 * peers :]
+    start_ref, rows_ref, k_tile_ref = refs[:3]
+    tile_refs = refs[3 : 3 + peers]
+    got_refs = refs[3 + peers : 3 + 2 * peers]
+    field_ref, send_hbm, end_ref, own_ref, own_sem, send_sem = refs[3 + 2 * peers :]
+    own_load = pltpu.make_async_copy(tile_refs[0], own_ref, own_sem)
+    own_load.start()
     rows_j = 16
-    mine = mine_ref[0]
+    mine = lax.axis_index("line")
     tiles = [ref[...] for ref in tile_refs]
     onward = downstream_map(tiles, base, mine)
     forward = [[col(tile, base + c) for c in range(4)] for tile in tiles]
     backward = [[col(tile, base + 4 + c) for c in range(4)] for tile in tiles]
     end_ref[...] = jnp.zeros(end_ref.shape, F32)
     rows = cells_i * rows_j
+    own_load.wait()
     for f in range(fields):
 
         def wide(entry):
@@ -700,11 +717,17 @@
             entry = col(k_tile_ref[0:fields], 3 * a + q)
             part = jnp.where(lane == rows_j * q + rows_j - 1, entry, part)
         end_ref[a * fields : (a + 1) * fields] = part
-    for d in range(send_ref.shape[0]):
-        send_ref[d] = end_ref[...]
-
-
-def middle(mine, own, start, k_rows, k_tile, tiles, got, base, owners, fields, cells_i):
+    sends = [
+        pltpu.make_async_copy(end_ref, send_hbm.at[d], send_sem.at[d])
+        for d in range(send_hbm.shape[0])
+    ]
+    for copy in sends:
+        copy.start()
+    for copy in sends:
+        copy.wait()
+
+
+def middle(start, k_rows, k_tile, tiles, got, base, owners, fields, cells_i):
     peers = len(tiles)
     vmem = pl.BlockSpec(memory_space=pltpu.VMEM)
     smem = pl.BlockSpec(memory_space=pltpu.SMEM)
@@ -712,14 +735,19 @@
         functools.partial(middle_kernel, peers=peers, base=base, fields=fields, cells_i=cells_i),
         out_shape=(
             pltpu.VMEM(start.shape, F32),
-            pltpu.VMEM((owners, 4 * fields, LANES), F32),
+            jax.ShapeDtypeStruct((owners, 4 * fields, LANES), F32),
         ),
-        in_specs=[smem, smem] + [vmem] * (3 + 2 * peers),
-        out_specs=(vmem, vmem),
-        scratch_shapes=[pltpu.VMEM((4 * fields, LANES), F32)],
+        in_specs=[vmem] * (3 + 2 * peers),
+        out_specs=(vmem, pl.BlockSpec(memory_space=pltpu.HBM)),
+        scratch_shapes=[
+            pltpu.VMEM((4 * fields, LANES), F32),
+            pltpu.SMEM((8, LANES), F32),
+            pltpu.SemaphoreType.DMA(()),
+            pltpu.SemaphoreType.DMA((owners,)),
+        ],
         compiler_params=PARAMS,
         name="middle",
-    )(mine, own, *map(near, (start, k_rows, k_tile, *tiles, *got)))
+    )(*map(near, (start, k_rows, k_tile, *tiles, *got)))
 
 
 def apply_k_kernel(field_ref, map_ref, out_ref):
@@ -746,12 +774,12 @@
     )(near(field), near(k_map))
 
 
-def finish_kernel(mine_ref, start_ref, got_ref, carry_ref, out_hbm, out_ref, out_sem):
+def finish_kernel(start_ref, got_ref, carry_ref, out_hbm, out_ref, out_sem):
     fields, cells_j, cells_i, _ = out_ref.shape
     rows_j = 16
     rows = cells_i * rows_j
     blocks = got_ref.shape[0]
-    mine = mine_ref[0]
+    mine = lax.axis_index("block")
     zero = jnp.zeros((fields, LANES), F32)
     part = [
         [got_ref[m, fields * a : fields * (a + 1)] for a in range(4)] for m in range(blocks)
@@ -800,18 +828,18 @@
         pltpu.make_async_copy(out_ref.at[f], out_hbm.at[f], out_sem.at[f]).wait()
 
 
-def finish(mine, start, got, carry, shape):
+def finish(start, got, carry, shape):
     vmem = pl.BlockSpec(memory_space=pltpu.VMEM)
     smem = pl.BlockSpec(memory_space=pltpu.SMEM)
     return pl.pallas_call(
         finish_kernel,
         out_shape=jax.ShapeDtypeStruct(shape, F32),
-        in_specs=[smem, vmem, vmem, vmem],
+        in_specs=[vmem, vmem, vmem],
         out_specs=pl.BlockSpec(memory_space=pltpu.HBM),
         scratch_shapes=[pltpu.VMEM(shape, F32), pltpu.SemaphoreType.DMA((shape[0],))],
         compiler_params=PARAMS,
         name="finish",
-    )(mine, near(start), near(got), near(carry))
+    )(near(start), near(got), near(carry))
 
 
 def per_device(
@@ -828,32 +856,23 @@
     fields, cells_i, cells_j, cells_k = adjoint.shape
     owners = receptor_cell.shape[2]
     peers = lax.axis_size("line")
-    line = lax.axis_index("line").astype(jnp.int32).reshape(1)
-    block = lax.axis_index("block").astype(jnp.int32).reshape(1)
     base = 4 * cells_i
 
     adjoint, residual = (x.transpose(0, 2, 1, 3) for x in (adjoint, residual))
     counts = send_count.reshape(owners)
-    outgoing, *tables = gather(block, counts, receptor_cell[0, 0], adjoint)
+    outgoing, *tables = gather(counts, receptor_cell[0, 0], adjoint)
     incoming = lax.all_to_all(outgoing, "block", split_axis=0, concat_axis=0, tiled=True)
 
     square = i_factors[0].reshape(2, fields, cells_i * cells_i)
-    square = jnp.pad(square, ((0, 0), (0, 8 - fields), (0, LANES - cells_i * cells_i)))
-    edge = couplings[0, 0, 0:2].reshape(6, fields).T
-    edge = jnp.pad(edge, ((0, 8 - fields), (0, LANES - 6)))
-    i_tiles = jnp.concatenate([square, edge[None]], axis=0)
-    own = prepare_i(i_tiles, cells_i)
+    i_tiles = jnp.pad(square, ((0, 0), (0, 8 - fields), (0, LANES - cells_i * cells_i)))
+    couple = couplings[0, 0].transpose(1, 0, 2)
+    own = prepare_i(couple, i_tiles, cells_i)
 
     def shifted(value, shift):
         return lax.ppermute(value, "line", [(s, (s + shift) % peers) for s in range(peers)])
 
     tiles = [own] + [shifted(own, m) for m in range(1, peers)]
-    couple = couplings[0, 0].transpose(1, 0, 2)
-    couple, _ = lax.optimization_barrier((couple, outgoing))
-    k_tile, k_map, k_rows, k_carry = prepare_k(couple, k_factors[0])
-    counts, _ = lax.optimization_barrier((counts, k_tile))
     begun = scatter_own(
-        block,
         counts,
         tables,
         receptor_cell[0, 0],
@@ -862,8 +881,6 @@
         (fields, cells_j, cells_i),
     )
     start, *ends = scatter(
-        line,
-        block,
         i_tiles,
         begun,
         incoming,
@@ -874,12 +891,14 @@
         base,
     )
     got = [ends[0]] + [shifted(ends[m], m) for m in range(1, peers)]
+    couple, _ = lax.optimization_barrier((couple, ends[0]))
+    k_tile, k_map, k_rows, k_carry = prepare_k(couple, k_factors[0])
     start, message = middle(
-        line, own, start, k_rows, k_tile, tiles, got, base, owners, fields, cells_i
+        start, k_rows, k_tile, tiles, got, base, owners, fields, cells_i
     )
     message = lax.all_to_all(message, "block", split_axis=0, concat_axis=0, tiled=True)
     start = apply_k(start, k_map)
-    return finish(block, start, message, k_carry, residual.shape).transpose(0, 2, 1, 3)
+    return finish(start, message, k_carry, residual.shape).transpose(0, 2, 1, 3)
 
 
 def solution(mesh):

time: 62.5 us -> 61.2 us (0.979)
    ppermute x6, waiting for transfers between devices: 3.38 us -> 1.04 us  [shifted(): lax.ppermute(value, 'line', [(s, (s + shift) % peers) for s in range(peer...]
    all_to_all x1, waiting for transfers between devices: 2.58 us -> 4.82 us  [per_device(): lax.all_to_all(outgoing, 'block', split_axis=0, concat_axis=0, tiled=True)]
    pallas_call x1, Pallas kernels: 13.8 us -> 13 us  [scatter(): pl.pallas_call(functools.partial(scatter_kernel, peers=peers, chunk=chunk...]
    slice x2 -> x0, local copies, waits for them, and re-layouts: 0.68 us -> none  [per_device(): edge = couplings[0, 0, 0:2].reshape(6, fields).T]
    unnamed x14, local copies, waits for them, and re-layouts: 0.04 us -> 0.71 us
where the time goes in v7:
time: 61.2 us; the launch traced here: 60.9 us
  Pallas kernels  31.8 us (52%)
  starting transfers between devices  15.9 us (26%)
  waiting for transfers between devices  12.2 us (20%)
  local copies, waits for them, and re-layouts  0.79 us (1%)
    pallas_call x1, Pallas kernels, scatter(): pl.pallas_call(functools.partial(scatter_kernel, peers=peers, chunk=chunk...  13 us
    pallas_call x1, Pallas kernels, gather(): pl.pallas_call(functools.partial(gather_kernel, chunk=chunk, group=group)...  8.05 us
    all_to_all x1, starting transfers between devices, per_device(): lax.all_to_all(outgoing, 'block', split_axis=0, concat_axis=0, tiled=True)  7.42 us
    all_to_all x1, waiting for transfers between devices, per_device(): lax.all_to_all(message, 'block', split_axis=0, concat_axis=0, tiled=True)  6.37 us
    ppermute x6, starting transfers between devices, shifted(): lax.ppermute(value, 'line', [(s, (s + shift) % peers) for s in range(peer...  4.83 us
    all_to_all x1, waiting for transfers between devices, per_device(): lax.all_to_all(outgoing, 'block', split_axis=0, concat_axis=0, tiled=True)  4.82 us
    all_to_all x1, starting transfers between devices, per_device(): lax.all_to_all(message, 'block', split_axis=0, concat_axis=0, tiled=True)  3.65 us
    pallas_call x1, Pallas kernels, scatter_own(): pl.pallas_call(functools.partial(scatter_own_kernel, sizes=sizes, chunk=c...  3.4 us
  transfers between devices with their start and end apart: 8, of which 4 were waited for; matrix products, arithmetic and copies ran while one was open for 0% of the time, Pallas kernels for 12%

profile of v7, /device:TPU:0, one launch (start us, length us, event | category | flops | bytes accessed | tf_op | source)
XLA Modules:
  0.0 60.9 jit_solution(16035754591555522396)
XLA Ops:
  0.0 8.1 %gather.1 = (f32[8,96,128]{2,1,0:T(8,128)}, bf16[384,256]{1,0:T(8,128)(2,1)S(1)}, bf16[384,256]{1,0:T(8,128)(2,1)S(1)}) custom-call(s32[8]{0:T(128)} %bitcast.24, s32[8,2048]{1,0:T(8,128)} %bitcast.19, f32[6,15,8,128]{3,2,1,0:T(8,128)} %bitcast.23), custom_call_target="tpu_custom_call" | custom-call | tf_op jit(solution)/shard_map/gather/pallas_call | solution.py:266
  8.1 0.0 copy-start.6
  8.1 0.0 copy-start.1
  8.1 0.0 copy-start.4
  8.1 7.4 %all-to-all-start = ((f32[8,96,128]{2,1,0:T(8,128)}), f32[8,96,128]{2,1,0:T(8,128)S(1)}, u32[]{:S(2)}, u32[]{:S(2)}) async-start(f32[8,96,128]{2,1,0:T(8,128)} %get-tuple-element.22), calls=%async_computation | async-start | bytes 786432 | tf_op jit(solution)/shard_map/all_to_all | solution.py:864
  15.5 0.0 copy-start.3
  15.5 0.1 reshape.4
  15.6 0.0 copy-start.5
  15.6 0.7 %copy-done.5 = f32[1,1,4,3,6]{4,2,3,1,0:T(4,128)S(1)} copy-done((f32[1,1,4,3,6]{4,2,3,1,0:T(4,128)S(1)}, f32[1,1,4,3,6]{4,2,3,1,0:T(4,128)}, u32[]{:S(2)}) %copy-start.5) | copy-done | bytes 312
  16.3 0.8 %prepare_i.1.refs_6_.refs_3_ = f32[8,128]{1,0:T(8,128)S(1)} custom-call(f32[3,4,6]{2,1,0:T(4,128)S(1)} %bitcast.21, f32[2,8,128]{2,1,0:T(8,128)S(1)} %pad.4.i_ref.refs_0_), custom_call_target="tpu_custom_call" | custom-call | tf_op jit(solution)/shard_map/prepare_i/pallas_call | solution.py:346
  17.1 0.7 %collective-permute-start.2 = (f32[8,128]{1,0:T(8,128)S(1)}, f32[8,128]{1,0:T(8,128)S(1)}, u32[]{:S(2)}, u32[]{:S(2)}) collective-permute-start(f32[8,128]{1,0:T(8,128)S(1)} %prepare_i.1.refs_6_.refs_3_), channel_id=1, source_target_pairs={{0,24},{8,0},{16,8},{24,16},{1,25},{9,1},{17,9},{25,17},{2,26},{10... | collective-permute-start | bytes 12296 | tf_op jit(solution)/shard_map/ppermute | solution.py:872
  17.9 0.9 %collective-permute-start.1 = (f32[8,128]{1,0:T(8,128)S(1)}, f32[8,128]{1,0:T(8,128)S(1)}, u32[]{:S(2)}, u32[]{:S(2)}) collective-permute-start(f32[8,128]{1,0:T(8,128)S(1)} %prepare_i.1.refs_6_.refs_3_), channel_id=1, source_target_pairs={{0,16},{8,24},{16,0},{24,8},{1,17},{9,25},{17,1},{25,9},{2,18},{10... | collective-permute-start | bytes 12296 | tf_op jit(solution)/shard_map/ppermute | solution.py:872
  18.8 0.2 collective-permute-start
  18.9 0.0 copy-done.1
  18.9 3.4 %scatter_own.1.refs_1_ = f32[720,256]{1,0:T(8,128)S(1)} custom-call(s32[8]{0:T(128)} %bitcast.25, bf16[384,256]{1,0:T(8,128)(2,1)S(1)} %get-tuple-element.20.high_ref, bf16[384,256]{1,0:T(8,128)(2,1)S(1)} %get-tuple-element.21.low_ref, s32[8,2048]{1,0:T(8,128)S(1)} %bitcast.20, s32[8,2048]{1,0:T(8,128)S(1)} %bitcast.17, f32[3,8,2048]{2,1,0:T(8,128)S(1)} %bitcast.14), custom_call_target="tpu_custom_call" | custom-call | tf_op jit(solution)/shard_map/scatter_own/pallas_call | solution.py:537
  22.4 0.0 collective-permute-done.2.refs_9_.refs_6_
  22.4 0.0 collective-permute-done.1.refs_8_.refs_5_
  22.4 0.0 collective-permute-done.refs_7_.refs_4_
  22.4 4.8 %all-to-all-done.refs_2_ = f32[8,96,128]{2,1,0:T(8,128)S(1)} async-done(((f32[8,96,128]{2,1,0:T(8,128)}), f32[8,96,128]{2,1,0:T(8,128)S(1)}, u32[]{:S(2)}, u32[]{:S(2)}) %all-to-all-start) | async-done | bytes 393248 | tf_op jit(solution)/shard_map/all_to_all | solution.py:864
  27.2 13.0 %scatter.1 = (f32[768,128]{1,0:T(8,128)S(1)}, f32[192,128]{1,0:T(8,128)S(1)}, f32[192,128]{1,0:T(8,128)S(1)}, f32[192,128]{1,0:T(8,128)S(1)}, f32[192,128]{1,0:T(8,128)S(1)}) custom-call(f32[2,8,128]{2,1,0:T(8,128)S(1)} %pad.4.i_ref.refs_0_, f32[720,256]{1,0:T(8,128)S(1)} %scatter_own.1.refs_1_, f32[8,96,128]{2,1,0:T(8,128)S(1)} %all-to-all-done.refs_2_, ...), custom_call_target="tpu_custom_call" | custom-call | tf_op jit(solution)/shard_map/scatter/pallas_call | solution.py:639
  40.2 0.1 collective-permute-start.3
  40.3 1.6 %collective-permute-start.4 = (f32[192,128]{1,0:T(8,128)S(1)}, f32[192,128]{1,0:T(8,128)S(1)}, u32[]{:S(2)}, u32[]{:S(2)}) collective-permute-start(f32[192,128]{1,0:T(8,128)S(1)} %get-tuple-element.29), channel_id=1, source_target_pairs={{0,16},{8,24},{16,0},{24,8},{1,17},{9,25},{17,1},{25,9},{2,18},{10... | collective-permute-start | bytes 294920 | tf_op jit(solution)/shard_map/ppermute | solution.py:872
  41.8 1.4 %collective-permute-start.5 = (f32[192,128]{1,0:T(8,128)S(1)}, f32[192,128]{1,0:T(8,128)S(1)}, u32[]{:S(2)}, u32[]{:S(2)}) collective-permute-start(f32[192,128]{1,0:T(8,128)S(1)} %get-tuple-element.30), channel_id=1, source_target_pairs={{0,24},{8,0},{16,8},{24,16},{1,25},{9,1},{17,9},{25,17},{2,26},{10... | collective-permute-start | bytes 294920 | tf_op jit(solution)/shard_map/ppermute | solution.py:872
  43.2 2.2 %prepare_k.1 = (f32[8,128]{1,0:T(8,128)S(1)}, f32[6,128,128]{2,1,0:T(8,128)S(1)}, f32[6,8,128]{2,1,0:T(8,128)S(1)}, f32[4,8,128]{2,1,0:T(8,128)S(1)}) custom-call(f32[3,4,6]{2,1,0:T(4,128)S(1)} %bitcast.22, f32[2,6,128,128]{3,2,1,0:T(8,128)S(1)} %bitcast.13), custom_call_target="tpu_custom_call" | custom-call | tf_op jit(solution)/shard_map/prepare_k/pallas_call | solution.py:399
  45.4 0.0 collective-permute-done.3.refs_8_
  45.4 0.6 collective-permute-done.4.refs_9_
  46.0 0.5 collective-permute-done.5.refs_10_
  46.5 1.9 %middle.1 = (f32[768,128]{1,0:T(8,128)S(1)}, f32[8,24,128]{2,1,0:T(8,128)}) custom-call(f32[768,128]{1,0:T(8,128)S(1)} %get-tuple-element.23.refs_0_, f32[6,8,128]{2,1,0:T(8,128)S(1)} %get-tuple-element.26.refs_1_, f32[8,128]{1,0:T(8,128)S(1)} %get-tuple-element.27.refs_2_, f32[8,128]{1,0:T(8,128)S(1)} %prepare_i.1.refs_6_.refs_3_, ...), custom_call_target="tpu_custom_call" | custom-call | tf_op jit(solution)/shard_map/middle/pallas_call | solution.py:734
  48.4 3.6 %all-to-all-start.1 = ((f32[8,24,128]{2,1,0:T(8,128)}), f32[8,24,128]{2,1,0:T(8,128)S(1)}, u32[]{:S(2)}, u32[]{:S(2)}) async-start(f32[8,24,128]{2,1,0:T(8,128)} %get-tuple-element.33), calls=%async_computation.1 | async-start | bytes 196608 | tf_op jit(solution)/shard_map/all_to_all | solution.py:899
  52.0 1.1 %apply_k.1.start_ref = f32[768,128]{1,0:T(8,128)S(1)} custom-call(f32[768,128]{1,0:T(8,128)S(1)} %get-tuple-element.31.field_ref, f32[6,128,128]{2,1,0:T(8,128)S(1)} %get-tuple-element.32.map_ref), custom_call_target="tpu_custom_call" | custom-call | tf_op jit(solution)/shard_map/apply_k/pallas_call | solution.py:767
  53.1 6.4 %all-to-all-done.1.got_ref = f32[8,24,128]{2,1,0:T(8,128)S(1)} async-done(((f32[8,24,128]{2,1,0:T(8,128)}), f32[8,24,128]{2,1,0:T(8,128)S(1)}, u32[]{:S(2)}, u32[]{:S(2)}) %all-to-all-start.1) | async-done | bytes 98336 | tf_op jit(solution)/shard_map/all_to_all | solution.py:899
  59.5 1.4 %finish.1 = f32[6,15,8,128]{3,2,1,0:T(8,128)} custom-call(f32[768,128]{1,0:T(8,128)S(1)} %apply_k.1.start_ref, f32[8,24,128]{2,1,0:T(8,128)S(1)} %all-to-all-done.1.got_ref, f32[4,8,128]{2,1,0:T(8,128)S(1)} %get-tuple-element.34.carry_ref), custom_call_target="tpu_custom_call" | custom-call | tf_op jit(solution)/shard_map/finish/pallas_call | solution.py:834
  (8 shorter events, 0.0 us)
Async XLA Ops:
  8.1 7.5 %copy-start.6 = (f32[1,2,6,8,8]{4,3,2,1,0:T(8,128)S(1)}, f32[1,2,6,8,8]{4,3,2,1,0:T(8,128)}, u32[]{:S(2)}) copy-start(f32[1,2,6,8,8]{4,3,2,1,0:T(8,128)} %param.11) | copy-start | bytes 9220
  8.1 10.9 %copy-start.1 = (f32[1,1,3,8,2048]{4,3,2,1,0:T(8,128)S(1)}, f32[1,1,3,8,2048]{4,3,2,1,0:T(8,128)}, u32[]{:S(2)}) copy-start(f32[1,1,3,8,2048]{4,3,2,1,0:T(8,128)} %param.17) | copy-start | bytes 589828
  8.1 10.9 %copy-start.4 = (s32[1,1,8,2048]{3,2,1,0:T(8,128)S(1)}, s32[1,1,8,2048]{3,2,1,0:T(8,128)}, u32[]{:S(2)}) copy-start(s32[1,1,8,2048]{3,2,1,0:T(8,128)} %param.14) | copy-start | bytes 196612
  8.1 19.1 %all-to-all-start = ((f32[8,96,128]{2,1,0:T(8,128)}), f32[8,96,128]{2,1,0:T(8,128)S(1)}, u32[]{:S(2)}, u32[]{:S(2)}) async-start(f32[8,96,128]{2,1,0:T(8,128)} %get-tuple-element.22), calls=%async_computation | async-start | bytes 786432 | tf_op jit(solution)/shard_map/all_to_all | solution.py:864
  15.5 3.4 %copy-start.3 = (s32[1,1,8,2048]{3,2,1,0:T(8,128)S(1)}, s32[1,1,8,2048]{3,2,1,0:T(8,128)}, u32[]{:S(2)}) copy-start(s32[1,1,8,2048]{3,2,1,0:T(8,128)} %param.16) | copy-start | bytes 196612
  15.6 0.7 %copy-start.5 = (f32[1,1,4,3,6]{4,2,3,1,0:T(4,128)S(1)}, f32[1,1,4,3,6]{4,2,3,1,0:T(4,128)}, u32[]{:S(2)}) copy-start(f32[1,1,4,3,6]{4,2,3,1,0:T(4,128)} %param.13) | copy-start | bytes 868
  17.1 5.2 %collective-permute-start.2 = (f32[8,128]{1,0:T(8,128)S(1)}, f32[8,128]{1,0:T(8,128)S(1)}, u32[]{:S(2)}, u32[]{:S(2)}) collective-permute-start(f32[8,128]{1,0:T(8,128)S(1)} %prepare_i.1.refs_6_.refs_3_), channel_id=1, source_target_pairs={{0,24},{8,0},{16,8},{24,16},{1,25},{9,1},{17,9},{25,17},{2,26},{10... | collective-permute-start | bytes 12296 | tf_op jit(solution)/shard_map/ppermute | solution.py:872
  17.9 4.5 %collective-permute-start.1 = (f32[8,128]{1,0:T(8,128)S(1)}, f32[8,128]{1,0:T(8,128)S(1)}, u32[]{:S(2)}, u32[]{:S(2)}) collective-permute-start(f32[8,128]{1,0:T(8,128)S(1)} %prepare_i.1.refs_6_.refs_3_), channel_id=1, source_target_pairs={{0,16},{8,24},{16,0},{24,8},{1,17},{9,25},{17,1},{25,9},{2,18},{10... | collective-permute-start | bytes 12296 | tf_op jit(solution)/shard_map/ppermute | solution.py:872
  18.8 3.6 %collective-permute-start = (f32[8,128]{1,0:T(8,128)S(1)}, f32[8,128]{1,0:T(8,128)S(1)}, u32[]{:S(2)}, u32[]{:S(2)}) collective-permute-start(f32[8,128]{1,0:T(8,128)S(1)} %prepare_i.1.refs_6_.refs_3_), channel_id=1, source_target_pairs={{0,8},{8,16},{16,24},{24,0},{1,9},{9,17},{17,25},{25,1},{2,10},{10... | collective-permute-start | bytes 12296 | tf_op jit(solution)/shard_map/ppermute | solution.py:872
  18.9 8.3 %copy-start.2 = (f32[6,8,15,128]{3,1,2,0:T(8,128)S(1)}, f32[6,8,15,128]{3,1,2,0:T(8,128)}, u32[]{:S(2)}) copy-start(f32[6,8,15,128]{3,1,2,0:T(8,128)} %param.9) | copy-start | bytes 1105924
  27.2 16.0 %copy-start = (f32[1,2,6,128,128]{4,3,2,1,0:T(8,128)S(1)}, f32[1,2,6,128,128]{4,3,2,1,0:T(8,128)}, u32[]{:S(2)}) copy-start(f32[1,2,6,128,128]{4,3,2,1,0:T(8,128)} %param.12) | copy-start | bytes 2359300
  40.2 5.2 %collective-permute-start.3 = (f32[192,128]{1,0:T(8,128)S(1)}, f32[192,128]{1,0:T(8,128)S(1)}, u32[]{:S(2)}, u32[]{:S(2)}) collective-permute-start(f32[192,128]{1,0:T(8,128)S(1)} %get-tuple-element.28), channel_id=1, source_target_pairs={{0,8},{8,16},{16,24},{24,0},{1,9},{9,17},{17,25},{25,1},{2,10},{10... | collective-permute-start | bytes 294920 | tf_op jit(solution)/shard_map/ppermute | solution.py:872
  40.3 5.7 %collective-permute-start.4 = (f32[192,128]{1,0:T(8,128)S(1)}, f32[192,128]{1,0:T(8,128)S(1)}, u32[]{:S(2)}, u32[]{:S(2)}) collective-permute-start(f32[192,128]{1,0:T(8,128)S(1)} %get-tuple-element.29), channel_id=1, source_target_pairs={{0,16},{8,24},{16,0},{24,8},{1,17},{9,25},{17,1},{25,9},{2,18},{10... | collective-permute-start | bytes 294920 | tf_op jit(solution)/shard_map/ppermute | solution.py:872
  41.8 4.6 %collective-permute-start.5 = (f32[192,128]{1,0:T(8,128)S(1)}, f32[192,128]{1,0:T(8,128)S(1)}, u32[]{:S(2)}, u32[]{:S(2)}) collective-permute-start(f32[192,128]{1,0:T(8,128)S(1)} %get-tuple-element.30), channel_id=1, source_target_pairs={{0,24},{8,0},{16,8},{24,16},{1,25},{9,1},{17,9},{25,17},{2,26},{10... | collective-permute-start | bytes 294920 | tf_op jit(solution)/shard_map/ppermute | solution.py:872
  48.4 11.1 %all-to-all-start.1 = ((f32[8,24,128]{2,1,0:T(8,128)}), f32[8,24,128]{2,1,0:T(8,128)S(1)}, u32[]{:S(2)}, u32[]{:S(2)}) async-start(f32[8,24,128]{2,1,0:T(8,128)} %get-tuple-element.33), calls=%async_computation.1 | async-start | bytes 196608 | tf_op jit(solution)/shard_map/all_to_all | solution.py:899

commit v8 on v7

--- a/solution.py
+++ b/solution.py
@@ -435,15 +435,17 @@
     return total
 
 
-def spread_slots(total_ref, place_ref, value_of, cell_ref, weight_ref, b, c, sizes, chunk):
+def spread_slots(total_ref, place_ref, value_of, cell_ref, weight_ref, units, sizes, size):
     fields, cells_j, cells_i = sizes
     rows_j = 16
+    chunk = size * len(units)
     per = chunk // LANES
-    start = pl.multiple_of(c * chunk, chunk)
-    cell = cell_ref[pl.ds(b, 1), pl.ds(start, chunk)]
-    x = weight_ref[0, pl.ds(b, 1), pl.ds(start, chunk)]
-    y = weight_ref[1, pl.ds(b, 1), pl.ds(start, chunk)]
-    z = weight_ref[2, pl.ds(b, 1), pl.ds(start, chunk)]
+
+    def joined(pick):
+        return jnp.concatenate([pick(pl.ds(b, 1), pl.ds(at, size)) for b, at in units], axis=1)
+
+    cell = joined(lambda b, at: cell_ref[b, at])
+    x, y, z = (joined(lambda b, at, axis=axis: weight_ref[axis, b, at]) for axis in range(3))
     i, j, k = split_cell(cell, cells_i, cells_j)
 
     def hat(size, at, t):
@@ -467,7 +469,14 @@
     along_k = jnp.concatenate(along_k, axis=0)
     blocks = []
     for f in range(fields):
-        value = jnp.concatenate([value_of(f, c * per + q) for q in range(per)], axis=1)
+        value = jnp.concatenate(
+            [
+                value_of(f, b, at // LANES + q)
+                for b, at in units
+                for q in range(size // LANES)
+            ],
+            axis=1,
+        )
         scaled = along_j * value
         blocks += [along_i * scaled[q : q + 1] for q in range(cells_j)]
     high, low = split(jnp.concatenate(blocks, axis=0))
@@ -490,7 +499,6 @@
     found_ref,
     *,
     sizes,
-    chunk,
     gather_chunk,
 ):
     capacity = cell_ref.shape[1]
@@ -513,31 +521,24 @@
 
     lax.fori_loop(0, lax.div(count + (gather_chunk - 1), gather_chunk), find_body, 0)
 
-    def chunk_body(c, carry):
-        spread_slots(
-            total_ref,
-            place_ref,
-            lambda f, q: got_ref[pl.ds(f * slot_rows + q, 1), :],
-            cell_ref,
-            weight_ref,
-            mine,
-            c,
-            sizes,
-            chunk,
-        )
-        return carry
-
-    lax.fori_loop(0, capacity // chunk, chunk_body, 0)
-
-
-def scatter_own(count, tables, receptor, cell, weight, sizes, chunk=2048, gather_chunk=512):
+    spread_slots(
+        total_ref,
+        place_ref,
+        lambda f, b, q: got_ref[pl.ds(f * slot_rows + q, 1), :],
+        cell_ref,
+        weight_ref,
+        [(mine, 0)],
+        sizes,
+        capacity,
+    )
+
+
+def scatter_own(count, tables, receptor, cell, weight, sizes, gather_chunk=512):
     vmem = pl.BlockSpec(memory_space=pltpu.VMEM)
     smem = pl.BlockSpec(memory_space=pltpu.SMEM)
     fields, cells_j, cells_i = sizes
     return pl.pallas_call(
-        functools.partial(
-            scatter_own_kernel, sizes=sizes, chunk=chunk, gather_chunk=gather_chunk
-        ),
+        functools.partial(scatter_own_kernel, sizes=sizes, gather_chunk=gather_chunk),
         out_shape=pltpu.VMEM((fields * cells_i * cells_j, 2 * LANES), F32),
         in_specs=[smem] + [vmem] * 5,
         out_specs=vmem,
@@ -569,26 +570,30 @@
     place_ref[...] = places(LANES, LANES)
     own = lax.axis_index("block")
 
-    def source_body(at, carry):
-        b = at + (at >= own).astype(jnp.int32)
-
-        def chunk_body(c, carry):
-            spread_slots(
-                total_ref,
-                place_ref,
-                lambda f, q: got_ref[b, pl.ds(f * slot_rows + q, 1), :],
-                cell_ref,
-                weight_ref,
-                b,
-                c,
-                (fields, cells_j, cells_i),
-                chunk,
-            )
-            return carry
-
-        return lax.fori_loop(0, capacity // chunk, chunk_body, carry)
-
-    lax.fori_loop(0, sources - 1, source_body, 0)
+    parts = capacity // chunk
+    count = (sources - 1) * parts
+    group = max(g for g in range(1, 8) if count % g == 0)
+
+    def step_body(step, carry):
+        units = []
+        for g in range(group):
+            unit = step * group + g
+            b = lax.div(unit, parts)
+            b = b + (b >= own).astype(jnp.int32)
+            units.append((b, pl.multiple_of(lax.rem(unit, parts) * chunk, chunk)))
+        spread_slots(
+            total_ref,
+            place_ref,
+            lambda f, b, q: got_ref[b, pl.ds(f * slot_rows + q, 1), :],
+            cell_ref,
+            weight_ref,
+            units,
+            (fields, cells_j, cells_i),
+            chunk,
+        )
+        return carry
+
+    lax.fori_loop(0, count // group, step_body, 0)
 
     fold_ref[...] = total_ref[:, :LANES] + total_ref[:, LANES:]
     solve_load.wait()
@@ -630,7 +635,7 @@
             send_refs[shift][at : at + rows_j] = jnp.where(ahead, e1, h1)
 
 
-def scatter(solve_tiles, begun, got, cell, weight, residual, tiles, base, chunk=2048):
+def scatter(solve_tiles, begun, got, cell, weight, residual, tiles, base, chunk=1024):
     fields, cells_j, cells_i, _ = residual.shape
     peers = len(tiles)
     rows = fields * cells_i * 16

time: 61.2 us -> 59.7 us (0.975)
  Pallas kernels: 31.8 us -> 30.6 us
  waiting for transfers between devices: 12.2 us -> 11.2 us
  starting transfers between devices: 15.9 us -> 16.6 us
    ppermute x6, starting transfers between devices: 4.83 us -> 6.09 us  [shifted(): lax.ppermute(value, 'line', [(s, (s + shift) % peers) for s in range(peer...]
    pallas_call x1, Pallas kernels: 13 us -> 11.8 us  [scatter(): pl.pallas_call(functools.partial(scatter_kernel, peers=peers, chunk=chunk...]
    all_to_all x1, waiting for transfers between devices: 4.82 us -> 4.15 us  [per_device(): lax.all_to_all(outgoing, 'block', split_axis=0, concat_axis=0, tiled=True)]
  transfers between devices with their start and end apart: 8 -> 8, of which waited for: 4 -> 3; matrix products, arithmetic and copies ran while one was open for 0% -> 0% of each run, Pallas kernels for 12% -> 13%
where the time goes in v8:
time: 59.7 us; the launch traced here: 59.5 us
  Pallas kernels  30.6 us (51%)
  starting transfers between devices  16.6 us (28%)
  waiting for transfers between devices  11.2 us (19%)
  local copies, waits for them, and re-layouts  0.79 us (1%)
    pallas_call x1, Pallas kernels, scatter(): pl.pallas_call(functools.partial(scatter_kernel, peers=peers, chunk=chunk...  11.8 us
    pallas_call x1, Pallas kernels, gather(): pl.pallas_call(functools.partial(gather_kernel, chunk=chunk, group=group)...  8.04 us
    all_to_all x1, starting transfers between devices, per_device(): lax.all_to_all(outgoing, 'block', split_axis=0, concat_axis=0, tiled=True)  6.82 us
    ppermute x6, starting transfers between devices, shifted(): lax.ppermute(value, 'line', [(s, (s + shift) % peers) for s in range(peer...  6.09 us
    all_to_all x1, waiting for transfers between devices, per_device(): lax.all_to_all(message, 'block', split_axis=0, concat_axis=0, tiled=True)  6.03 us
    all_to_all x1, waiting for transfers between devices, per_device(): lax.all_to_all(outgoing, 'block', split_axis=0, concat_axis=0, tiled=True)  4.15 us
    all_to_all x1, starting transfers between devices, per_device(): lax.all_to_all(message, 'block', split_axis=0, concat_axis=0, tiled=True)  3.65 us
    pallas_call x1, Pallas kernels, scatter_own(): pl.pallas_call(functools.partial(scatter_own_kernel, sizes=sizes, gather_...  3.41 us
  transfers between devices with their start and end apart: 8, of which 3 were waited for; matrix products, arithmetic and copies ran while one was open for 0% of the time, Pallas kernels for 13%

profile of v8, /device:TPU:0, one launch (start us, length us, event | category | flops | bytes accessed | tf_op | source)
XLA Modules:
  0.0 59.5 jit_solution(1943063642541066103)
XLA Ops:
  0.0 8.0 %gather.1 = (f32[8,96,128]{2,1,0:T(8,128)}, bf16[384,256]{1,0:T(8,128)(2,1)S(1)}, bf16[384,256]{1,0:T(8,128)(2,1)S(1)}) custom-call(s32[8]{0:T(128)} %bitcast.24, s32[8,2048]{1,0:T(8,128)} %bitcast.19, f32[6,15,8,128]{3,2,1,0:T(8,128)} %bitcast.23), custom_call_target="tpu_custom_call" | custom-call | tf_op jit(solution)/shard_map/gather/pallas_call | solution.py:266
  8.0 0.0 copy-start.6
  8.1 0.0 copy-start.1
  8.1 0.0 copy-start.4
  8.1 6.8 %all-to-all-start = ((f32[8,96,128]{2,1,0:T(8,128)}), f32[8,96,128]{2,1,0:T(8,128)S(1)}, u32[]{:S(2)}, u32[]{:S(2)}) async-start(f32[8,96,128]{2,1,0:T(8,128)} %get-tuple-element.22), calls=%async_computation | async-start | bytes 786432 | tf_op jit(solution)/shard_map/all_to_all | solution.py:869
  14.9 0.0 copy-start.3
  14.9 0.1 reshape.4
  15.0 0.0 copy-start.5
  15.0 0.7 %copy-done.5 = f32[1,1,4,3,6]{4,2,3,1,0:T(4,128)S(1)} copy-done((f32[1,1,4,3,6]{4,2,3,1,0:T(4,128)S(1)}, f32[1,1,4,3,6]{4,2,3,1,0:T(4,128)}, u32[]{:S(2)}) %copy-start.5) | copy-done | bytes 312
  15.7 0.8 %prepare_i.1.refs_6_.refs_3_ = f32[8,128]{1,0:T(8,128)S(1)} custom-call(f32[3,4,6]{2,1,0:T(4,128)S(1)} %bitcast.21, f32[2,8,128]{2,1,0:T(8,128)S(1)} %pad.4.i_ref.refs_0_), custom_call_target="tpu_custom_call" | custom-call | tf_op jit(solution)/shard_map/prepare_i/pallas_call | solution.py:346
  16.5 1.3 %collective-permute-start.2 = (f32[8,128]{1,0:T(8,128)S(1)}, f32[8,128]{1,0:T(8,128)S(1)}, u32[]{:S(2)}, u32[]{:S(2)}) collective-permute-start(f32[8,128]{1,0:T(8,128)S(1)} %prepare_i.1.refs_6_.refs_3_), channel_id=1, source_target_pairs={{0,24},{8,0},{16,8},{24,16},{1,25},{9,1},{17,9},{25,17},{2,26},{10... | collective-permute-start | bytes 12296 | tf_op jit(solution)/shard_map/ppermute | solution.py:877
  17.9 0.9 %collective-permute-start.1 = (f32[8,128]{1,0:T(8,128)S(1)}, f32[8,128]{1,0:T(8,128)S(1)}, u32[]{:S(2)}, u32[]{:S(2)}) collective-permute-start(f32[8,128]{1,0:T(8,128)S(1)} %prepare_i.1.refs_6_.refs_3_), channel_id=1, source_target_pairs={{0,16},{8,24},{16,0},{24,8},{1,17},{9,25},{17,1},{25,9},{2,18},{10... | collective-permute-start | bytes 12296 | tf_op jit(solution)/shard_map/ppermute | solution.py:877
  18.8 0.2 collective-permute-start
  18.9 0.0 copy-done.1
  19.0 3.4 %scatter_own.1.refs_1_ = f32[720,256]{1,0:T(8,128)S(1)} custom-call(s32[8]{0:T(128)} %bitcast.25, bf16[384,256]{1,0:T(8,128)(2,1)S(1)} %get-tuple-element.20.high_ref, bf16[384,256]{1,0:T(8,128)(2,1)S(1)} %get-tuple-element.21.low_ref, s32[8,2048]{1,0:T(8,128)S(1)} %bitcast.20, s32[8,2048]{1,0:T(8,128)S(1)} %bitcast.17, f32[3,8,2048]{2,1,0:T(8,128)S(1)} %bitcast.14), custom_call_target="tpu_custom_call" | custom-call | tf_op jit(solution)/shard_map/scatter_own/pallas_call | solution.py:540
  22.4 0.0 collective-permute-done.2.refs_9_.refs_6_
  22.4 0.0 collective-permute-done.1.refs_8_.refs_5_
  22.4 0.0 collective-permute-done.refs_7_.refs_4_
  22.4 4.1 %all-to-all-done.refs_2_ = f32[8,96,128]{2,1,0:T(8,128)S(1)} async-done(((f32[8,96,128]{2,1,0:T(8,128)}), f32[8,96,128]{2,1,0:T(8,128)S(1)}, u32[]{:S(2)}, u32[]{:S(2)}) %all-to-all-start) | async-done | bytes 393248 | tf_op jit(solution)/shard_map/all_to_all | solution.py:869
  26.6 11.8 %scatter.1 = (f32[768,128]{1,0:T(8,128)S(1)}, f32[192,128]{1,0:T(8,128)S(1)}, f32[192,128]{1,0:T(8,128)S(1)}, f32[192,128]{1,0:T(8,128)S(1)}, f32[192,128]{1,0:T(8,128)S(1)}) custom-call(f32[2,8,128]{2,1,0:T(8,128)S(1)} %pad.4.i_ref.refs_0_, f32[720,256]{1,0:T(8,128)S(1)} %scatter_own.1.refs_1_, f32[8,96,128]{2,1,0:T(8,128)S(1)} %all-to-all-done.refs_2_, ...), custom_call_target="tpu_custom_call" | custom-call | tf_op jit(solution)/shard_map/scatter/pallas_call | solution.py:644
  38.3 0.1 collective-permute-start.3
  38.4 2.2 %collective-permute-start.4 = (f32[192,128]{1,0:T(8,128)S(1)}, f32[192,128]{1,0:T(8,128)S(1)}, u32[]{:S(2)}, u32[]{:S(2)}) collective-permute-start(f32[192,128]{1,0:T(8,128)S(1)} %get-tuple-element.29), channel_id=1, source_target_pairs={{0,16},{8,24},{16,0},{24,8},{1,17},{9,25},{17,1},{25,9},{2,18},{10... | collective-permute-start | bytes 294920 | tf_op jit(solution)/shard_map/ppermute | solution.py:877
  40.6 1.4 %collective-permute-start.5 = (f32[192,128]{1,0:T(8,128)S(1)}, f32[192,128]{1,0:T(8,128)S(1)}, u32[]{:S(2)}, u32[]{:S(2)}) collective-permute-start(f32[192,128]{1,0:T(8,128)S(1)} %get-tuple-element.30), channel_id=1, source_target_pairs={{0,24},{8,0},{16,8},{24,16},{1,25},{9,1},{17,9},{25,17},{2,26},{10... | collective-permute-start | bytes 294920 | tf_op jit(solution)/shard_map/ppermute | solution.py:877
  42.0 2.2 %prepare_k.1 = (f32[8,128]{1,0:T(8,128)S(1)}, f32[6,128,128]{2,1,0:T(8,128)S(1)}, f32[6,8,128]{2,1,0:T(8,128)S(1)}, f32[4,8,128]{2,1,0:T(8,128)S(1)}) custom-call(f32[3,4,6]{2,1,0:T(4,128)S(1)} %bitcast.22, f32[2,6,128,128]{3,2,1,0:T(8,128)S(1)} %bitcast.13), custom_call_target="tpu_custom_call" | custom-call | tf_op jit(solution)/shard_map/prepare_k/pallas_call | solution.py:399
  44.2 0.0 collective-permute-done.3.refs_8_
  44.2 0.0 collective-permute-done.4.refs_9_
  44.2 1.0 %collective-permute-done.5.refs_10_ = f32[192,128]{1,0:T(8,128)S(1)} collective-permute-done((f32[192,128]{1,0:T(8,128)S(1)}, f32[192,128]{1,0:T(8,128)S(1)}, u32[]{:S(2)}, u32[]{:S(2)}) %collective-permute-start.5) | collective-permute-done | bytes 98336 | tf_op jit(solution)/shard_map/ppermute | solution.py:877
  45.2 1.9 %middle.1 = (f32[768,128]{1,0:T(8,128)S(1)}, f32[8,24,128]{2,1,0:T(8,128)}) custom-call(f32[768,128]{1,0:T(8,128)S(1)} %get-tuple-element.23.refs_0_, f32[6,8,128]{2,1,0:T(8,128)S(1)} %get-tuple-element.26.refs_1_, f32[8,128]{1,0:T(8,128)S(1)} %get-tuple-element.27.refs_2_, f32[8,128]{1,0:T(8,128)S(1)} %prepare_i.1.refs_6_.refs_3_, ...), custom_call_target="tpu_custom_call" | custom-call | tf_op jit(solution)/shard_map/middle/pallas_call | solution.py:739
  47.2 3.6 %all-to-all-start.1 = ((f32[8,24,128]{2,1,0:T(8,128)}), f32[8,24,128]{2,1,0:T(8,128)S(1)}, u32[]{:S(2)}, u32[]{:S(2)}) async-start(f32[8,24,128]{2,1,0:T(8,128)} %get-tuple-element.33), calls=%async_computation.1 | async-start | bytes 196608 | tf_op jit(solution)/shard_map/all_to_all | solution.py:904
  50.8 1.1 %apply_k.1.start_ref = f32[768,128]{1,0:T(8,128)S(1)} custom-call(f32[768,128]{1,0:T(8,128)S(1)} %get-tuple-element.31.field_ref, f32[6,128,128]{2,1,0:T(8,128)S(1)} %get-tuple-element.32.map_ref), custom_call_target="tpu_custom_call" | custom-call | tf_op jit(solution)/shard_map/apply_k/pallas_call | solution.py:772
  51.9 6.0 %all-to-all-done.1.got_ref = f32[8,24,128]{2,1,0:T(8,128)S(1)} async-done(((f32[8,24,128]{2,1,0:T(8,128)}), f32[8,24,128]{2,1,0:T(8,128)S(1)}, u32[]{:S(2)}, u32[]{:S(2)}) %all-to-all-start.1) | async-done | bytes 98336 | tf_op jit(solution)/shard_map/all_to_all | solution.py:904
  57.9 1.4 %finish.1 = f32[6,15,8,128]{3,2,1,0:T(8,128)} custom-call(f32[768,128]{1,0:T(8,128)S(1)} %apply_k.1.start_ref, f32[8,24,128]{2,1,0:T(8,128)S(1)} %all-to-all-done.1.got_ref, f32[4,8,128]{2,1,0:T(8,128)S(1)} %get-tuple-element.34.carry_ref), custom_call_target="tpu_custom_call" | custom-call | tf_op jit(solution)/shard_map/finish/pallas_call | solution.py:839
  (8 shorter events, 0.0 us)
Async XLA Ops:
  8.0 6.9 %copy-start.6 = (f32[1,2,6,8,8]{4,3,2,1,0:T(8,128)S(1)}, f32[1,2,6,8,8]{4,3,2,1,0:T(8,128)}, u32[]{:S(2)}) copy-start(f32[1,2,6,8,8]{4,3,2,1,0:T(8,128)} %param.11) | copy-start | bytes 9220
  8.1 10.9 %copy-start.1 = (f32[1,1,3,8,2048]{4,3,2,1,0:T(8,128)S(1)}, f32[1,1,3,8,2048]{4,3,2,1,0:T(8,128)}, u32[]{:S(2)}) copy-start(f32[1,1,3,8,2048]{4,3,2,1,0:T(8,128)} %param.17) | copy-start | bytes 589828
  8.1 10.9 %copy-start.4 = (s32[1,1,8,2048]{3,2,1,0:T(8,128)S(1)}, s32[1,1,8,2048]{3,2,1,0:T(8,128)}, u32[]{:S(2)}) copy-start(s32[1,1,8,2048]{3,2,1,0:T(8,128)} %param.14) | copy-start | bytes 196612
  8.1 18.5 %all-to-all-start = ((f32[8,96,128]{2,1,0:T(8,128)}), f32[8,96,128]{2,1,0:T(8,128)S(1)}, u32[]{:S(2)}, u32[]{:S(2)}) async-start(f32[8,96,128]{2,1,0:T(8,128)} %get-tuple-element.22), calls=%async_computation | async-start | bytes 786432 | tf_op jit(solution)/shard_map/all_to_all | solution.py:869
  14.9 4.0 %copy-start.3 = (s32[1,1,8,2048]{3,2,1,0:T(8,128)S(1)}, s32[1,1,8,2048]{3,2,1,0:T(8,128)}, u32[]{:S(2)}) copy-start(s32[1,1,8,2048]{3,2,1,0:T(8,128)} %param.16) | copy-start | bytes 196612
  15.0 0.7 %copy-start.5 = (f32[1,1,4,3,6]{4,2,3,1,0:T(4,128)S(1)}, f32[1,1,4,3,6]{4,2,3,1,0:T(4,128)}, u32[]{:S(2)}) copy-start(f32[1,1,4,3,6]{4,2,3,1,0:T(4,128)} %param.13) | copy-start | bytes 868
  16.5 5.9 %collective-permute-start.2 = (f32[8,128]{1,0:T(8,128)S(1)}, f32[8,128]{1,0:T(8,128)S(1)}, u32[]{:S(2)}, u32[]{:S(2)}) collective-permute-start(f32[8,128]{1,0:T(8,128)S(1)} %prepare_i.1.refs_6_.refs_3_), channel_id=1, source_target_pairs={{0,24},{8,0},{16,8},{24,16},{1,25},{9,1},{17,9},{25,17},{2,26},{10... | collective-permute-start | bytes 12296 | tf_op jit(solution)/shard_map/ppermute | solution.py:877
  17.9 4.5 %collective-permute-start.1 = (f32[8,128]{1,0:T(8,128)S(1)}, f32[8,128]{1,0:T(8,128)S(1)}, u32[]{:S(2)}, u32[]{:S(2)}) collective-permute-start(f32[8,128]{1,0:T(8,128)S(1)} %prepare_i.1.refs_6_.refs_3_), channel_id=1, source_target_pairs={{0,16},{8,24},{16,0},{24,8},{1,17},{9,25},{17,1},{25,9},{2,18},{10... | collective-permute-start | bytes 12296 | tf_op jit(solution)/shard_map/ppermute | solution.py:877
  18.8 3.6 %collective-permute-start = (f32[8,128]{1,0:T(8,128)S(1)}, f32[8,128]{1,0:T(8,128)S(1)}, u32[]{:S(2)}, u32[]{:S(2)}) collective-permute-start(f32[8,128]{1,0:T(8,128)S(1)} %prepare_i.1.refs_6_.refs_3_), channel_id=1, source_target_pairs={{0,8},{8,16},{16,24},{24,0},{1,9},{9,17},{17,25},{25,1},{2,10},{10... | collective-permute-start | bytes 12296 | tf_op jit(solution)/shard_map/ppermute | solution.py:877
  18.9 7.6 %copy-start.2 = (f32[6,8,15,128]{3,1,2,0:T(8,128)S(1)}, f32[6,8,15,128]{3,1,2,0:T(8,128)}, u32[]{:S(2)}) copy-start(f32[6,8,15,128]{3,1,2,0:T(8,128)} %param.9) | copy-start | bytes 1105924
  26.6 15.4 %copy-start = (f32[1,2,6,128,128]{4,3,2,1,0:T(8,128)S(1)}, f32[1,2,6,128,128]{4,3,2,1,0:T(8,128)}, u32[]{:S(2)}) copy-start(f32[1,2,6,128,128]{4,3,2,1,0:T(8,128)} %param.12) | copy-start | bytes 2359300
  38.3 5.9 %collective-permute-start.3 = (f32[192,128]{1,0:T(8,128)S(1)}, f32[192,128]{1,0:T(8,128)S(1)}, u32[]{:S(2)}, u32[]{:S(2)}) collective-permute-start(f32[192,128]{1,0:T(8,128)S(1)} %get-tuple-element.28), channel_id=1, source_target_pairs={{0,8},{8,16},{16,24},{24,0},{1,9},{9,17},{17,25},{25,1},{2,10},{10... | collective-permute-start | bytes 294920 | tf_op jit(solution)/shard_map/ppermute | solution.py:877
  38.4 5.8 %collective-permute-start.4 = (f32[192,128]{1,0:T(8,128)S(1)}, f32[192,128]{1,0:T(8,128)S(1)}, u32[]{:S(2)}, u32[]{:S(2)}) collective-permute-start(f32[192,128]{1,0:T(8,128)S(1)} %get-tuple-element.29), channel_id=1, source_target_pairs={{0,16},{8,24},{16,0},{24,8},{1,17},{9,25},{17,1},{25,9},{2,18},{10... | collective-permute-start | bytes 294920 | tf_op jit(solution)/shard_map/ppermute | solution.py:877
  40.6 4.6 %collective-permute-start.5 = (f32[192,128]{1,0:T(8,128)S(1)}, f32[192,128]{1,0:T(8,128)S(1)}, u32[]{:S(2)}, u32[]{:S(2)}) collective-permute-start(f32[192,128]{1,0:T(8,128)S(1)} %get-tuple-element.30), channel_id=1, source_target_pairs={{0,24},{8,0},{16,8},{24,16},{1,25},{9,1},{17,9},{25,17},{2,26},{10... | collective-permute-start | bytes 294920 | tf_op jit(solution)/shard_map/ppermute | solution.py:877
  47.2 10.8 %all-to-all-start.1 = ((f32[8,24,128]{2,1,0:T(8,128)}), f32[8,24,128]{2,1,0:T(8,128)S(1)}, u32[]{:S(2)}, u32[]{:S(2)}) async-start(f32[8,24,128]{2,1,0:T(8,128)} %get-tuple-element.33), calls=%async_computation.1 | async-start | bytes 196608 | tf_op jit(solution)/shard_map/all_to_all | solution.py:904

commit v9 on v8

--- a/solution.py
+++ b/solution.py
@@ -106,19 +106,25 @@
 
 def pick_rows(found_ref, lane, cell_ref, d, c, count, chunk, sizes, put):
     fields, cells_j, cells_i = sizes
-    rows_j = 16
-    rows = cells_i // 2 * rows_j
+    half_i = cells_i // 2
+    rows = half_i * cells_j
     per = chunk // LANES
     start = pl.multiple_of(c * chunk, chunk)
     cell = cell_ref[pl.ds(d, 1), pl.ds(start, chunk)]
     i, j, _ = split_cell(cell, cells_i, cells_j)
     slot = start + lax.broadcasted_iota(jnp.int32, cell.shape, 1)
-    row = lax.shift_right_logical(i, 1) * rows_j + j
-    row = jnp.where(slot < count, row, -1)
-    pick = lax.broadcasted_iota(jnp.int32, (rows, chunk), 0) == row
+    row = j * half_i + lax.shift_right_logical(i, 1)
+    row = jnp.where(slot < count, row, -8)
+    picks = {}
     for f in range(fields):
-        value = found_ref[f * rows : (f + 1) * rows, lane : lane + chunk]
-        value = jnp.where(pick, value, 0.0)
+        base = f * rows // 8 * 8
+        offset = f * rows - base
+        size = -(-(offset + rows) // 8) * 8
+        if offset not in picks:
+            place = lax.broadcasted_iota(jnp.int32, (size, chunk), 0)
+            picks[offset] = place == row + offset
+        value = found_ref[base : base + size, lane : lane + chunk]
+        value = jnp.where(picks[offset], value, 0.0)
         value = jnp.sum(value, axis=0, keepdims=True)
         for q in range(per):
             put(f, c * per + q, value[:, q * LANES : (q + 1) * LANES])
@@ -146,16 +152,17 @@
     *,
     chunk,
     group,
+    sizes,
 ):
-    fields, cells_j, cells_i, _ = field_ref.shape
+    fields, cells_j, cells_i = sizes
     owners, capacity = cell_ref.shape
-    sizes = (fields, cells_j, cells_i)
-    rows_j = 16
-    half_i = cells_i // 2
+    rows = cells_j * cells_i
     slot_rows = capacity // LANES
     steps = capacity // chunk
     loads = [
-        pltpu.make_async_copy(field_hbm.at[f], field_ref.at[f], field_sem.at[f])
+        pltpu.make_async_copy(
+            field_hbm.at[pl.ds(f * rows, rows)], field_ref.at[pl.ds(f * rows, rows)], field_sem.at[f]
+        )
         for f in range(fields)
     ]
     cell_load = pltpu.make_async_copy(cell_hbm, cell_ref, cell_sem)
@@ -199,15 +206,13 @@
 
     cell_load.wait()
     build(0)
-    pad = jnp.zeros((rows_j - cells_j, LANES), F32)
-    for f in range(fields):
-        loads[f].wait()
-        for i in range(cells_i):
-            high, low = split(jnp.concatenate([field_ref[f, :, i, :], pad], axis=0))
-            at = (f * half_i + i // 2) * rows_j
-            lane = (i % 2) * LANES
-            high_ref[at : at + rows_j, lane : lane + LANES] = high
-            low_ref[at : at + rows_j, lane : lane + LANES] = low
+    for load in loads:
+        load.wait()
+    for parity in range(2):
+        part = field_ref[pl.ds(parity, fields * rows // 2, stride=2), :]
+        high, low = split(part)
+        high_ref[:, parity * LANES : (parity + 1) * LANES] = high
+        low_ref[:, parity * LANES : (parity + 1) * LANES] = low
 
     def pick(n):
         for g in range(group):
@@ -256,15 +261,18 @@
     lax.fori_loop(0, owners, wait_body, 0)
 
 
-def gather(count, cell, field, chunk=256, group=4):
-    fields, _, cells_i, _ = field.shape
+def gather(count, cell, field, chunk=256, group=6):
+    fields, cells_j, cells_i, _ = field.shape
     owners, capacity = cell.shape
-    table = (fields * cells_i // 2 * 16, 2 * LANES)
+    field = field.reshape(-1, LANES)
+    table = (field.shape[0] // 2, 2 * LANES)
     out = (owners, fields * capacity // LANES, LANES)
     vmem = pl.BlockSpec(memory_space=pltpu.VMEM)
     hbm = pl.BlockSpec(memory_space=pltpu.HBM)
     return pl.pallas_call(
-        functools.partial(gather_kernel, chunk=chunk, group=group),
+        functools.partial(
+            gather_kernel, chunk=chunk, group=group, sizes=(fields, cells_j, cells_i)
+        ),
         out_shape=(
             jax.ShapeDtypeStruct(out, F32),
             pltpu.VMEM(table, BF16),
@@ -712,7 +720,11 @@
             value = value - own_ref[f, shift + 2 * p + 1] * after[1]
             field_ref[at : at + rows_j] = value
         block = field_ref[f * rows : (f + 1) * rows]
-        ends = product_nt(rows_ref[f], block)
+        r_high, r_low = split(rows_ref[f])
+        both = dot_nt(
+            jnp.concatenate([r_high, r_low], axis=0), jnp.concatenate(split(block), axis=0)
+        )
+        ends = both[:8, :rows] + both[:8, rows:] + both[8:, :rows]
         for a in range(4):
             end_ref[a * fields + f : a * fields + f + 1, :] = ends[a : a + 1]
     lane = lax.broadcasted_iota(jnp.int32, (fields, LANES), 1)

time: 59.7 us -> 59.8 us (level)
    all_to_all x1, starting transfers between devices: 6.82 us -> 8.32 us  [per_device(): lax.all_to_all(outgoing, 'block', split_axis=0, concat_axis=0, tiled=True)]
    ppermute x6, starting transfers between devices: 6.09 us -> 4.83 us  [shifted(): lax.ppermute(value, 'line', [(s, (s + shift) % peers) for s in range(peer...]
    all_to_all x1, waiting for transfers between devices: 4.15 us -> 3.53 us  [per_device(): lax.all_to_all(outgoing, 'block', split_axis=0, concat_axis=0, tiled=True)]
  transfers between devices with their start and end apart: 8 -> 8, of which waited for: 3 -> 4; matrix products, arithmetic and copies ran while one was open for 0% -> 0% of each run, Pallas kernels for 13% -> 13%
where the time goes in v9:
time: 59.8 us; the launch traced here: 59.4 us
  Pallas kernels  30.5 us (51%)
  starting transfers between devices  16.8 us (28%)
  waiting for transfers between devices  10.9 us (18%)
  local copies, waits for them, and re-layouts  0.79 us (1%)
    pallas_call x1, Pallas kernels, scatter(): pl.pallas_call(functools.partial(scatter_kernel, peers=peers, chunk=chunk...  11.8 us
    all_to_all x1, starting transfers between devices, per_device(): lax.all_to_all(outgoing, 'block', split_axis=0, concat_axis=0, tiled=True)  8.32 us
    pallas_call x1, Pallas kernels, gather(): pl.pallas_call(functools.partial(gather_kernel, chunk=chunk, group=group,...  7.64 us
    all_to_all x1, waiting for transfers between devices, per_device(): lax.all_to_all(message, 'block', split_axis=0, concat_axis=0, tiled=True)  6.35 us
    ppermute x6, starting transfers between devices, shifted(): lax.ppermute(value, 'line', [(s, (s + shift) % peers) for s in range(peer...  4.83 us
    pallas_call x1, Pallas kernels, scatter_own(): pl.pallas_call(functools.partial(scatter_own_kernel, sizes=sizes, gather_...  3.79 us
    all_to_all x1, starting transfers between devices, per_device(): lax.all_to_all(message, 'block', split_axis=0, concat_axis=0, tiled=True)  3.69 us
    all_to_all x1, waiting for transfers between devices, per_device(): lax.all_to_all(outgoing, 'block', split_axis=0, concat_axis=0, tiled=True)  3.53 us
  transfers between devices with their start and end apart: 8, of which 4 were waited for; matrix products, arithmetic and copies ran while one was open for 0% of the time, Pallas kernels for 13%

profile of v9, /device:TPU:0, one launch (start us, length us, event | category | flops | bytes accessed | tf_op | source)
XLA Modules:
  0.0 59.4 jit_solution(13852609054317161678)
XLA Ops:
  0.0 7.6 %gather.1 = (f32[8,96,128]{2,1,0:T(8,128)}, bf16[360,256]{1,0:T(8,128)(2,1)S(1)}, bf16[360,256]{1,0:T(8,128)(2,1)S(1)}) custom-call(s32[8]{0:T(128)} %bitcast.26, s32[8,2048]{1,0:T(8,128)} %bitcast.21, f32[720,128]{1,0:T(8,128)} %bitcast.25), custom_call_target="tpu_custom_call" | custom-call | tf_op jit(solution)/shard_map/gather/pallas_call | solution.py:272
  7.6 0.0 copy-start.6
  7.7 0.0 copy-start.1
  7.7 0.0 copy-start.4
  7.7 8.3 %all-to-all-start = ((f32[8,96,128]{2,1,0:T(8,128)}), f32[8,96,128]{2,1,0:T(8,128)S(1)}, u32[]{:S(2)}, u32[]{:S(2)}) async-start(f32[8,96,128]{2,1,0:T(8,128)} %get-tuple-element.22), calls=%async_computation | async-start | bytes 786432 | tf_op jit(solution)/shard_map/all_to_all | solution.py:881
  16.0 0.0 copy-start.3
  16.0 0.1 reshape.8
  16.1 0.0 copy-start.5
  16.1 0.7 %copy-done.5 = f32[1,1,4,3,6]{4,2,3,1,0:T(4,128)S(1)} copy-done((f32[1,1,4,3,6]{4,2,3,1,0:T(4,128)S(1)}, f32[1,1,4,3,6]{4,2,3,1,0:T(4,128)}, u32[]{:S(2)}) %copy-start.5) | copy-done | bytes 312
  16.8 0.8 %prepare_i.1.refs_6_.refs_3_ = f32[8,128]{1,0:T(8,128)S(1)} custom-call(f32[3,4,6]{2,1,0:T(4,128)S(1)} %bitcast.23, f32[2,8,128]{2,1,0:T(8,128)S(1)} %pad.4.i_ref.refs_0_), custom_call_target="tpu_custom_call" | custom-call | tf_op jit(solution)/shard_map/prepare_i/pallas_call | solution.py:354
  17.6 0.1 collective-permute-start.2
  17.7 1.6 %collective-permute-start.1 = (f32[8,128]{1,0:T(8,128)S(1)}, f32[8,128]{1,0:T(8,128)S(1)}, u32[]{:S(2)}, u32[]{:S(2)}) collective-permute-start(f32[8,128]{1,0:T(8,128)S(1)} %prepare_i.1.refs_6_.refs_3_), channel_id=1, source_target_pairs={{0,16},{8,24},{16,0},{24,8},{1,17},{9,25},{17,1},{25,9},{2,18},{10... | collective-permute-start | bytes 12296 | tf_op jit(solution)/shard_map/ppermute | solution.py:889
  19.3 0.2 collective-permute-start
  19.4 0.0 copy-done.4
  19.4 3.8 %scatter_own.1.refs_1_ = f32[720,256]{1,0:T(8,128)S(1)} custom-call(s32[8]{0:T(128)} %bitcast.27, bf16[360,256]{1,0:T(8,128)(2,1)S(1)} %get-tuple-element.20.high_ref, bf16[360,256]{1,0:T(8,128)(2,1)S(1)} %get-tuple-element.21.low_ref, s32[8,2048]{1,0:T(8,128)S(1)} %bitcast.22, s32[8,2048]{1,0:T(8,128)S(1)} %bitcast.19, f32[3,8,2048]{2,1,0:T(8,128)S(1)} %bitcast.16), custom_call_target="tpu_custom_call" | custom-call | tf_op jit(solution)/shard_map/scatter_own/pallas_call | solution.py:548
  23.2 0.0 collective-permute-done.2.refs_9_.refs_6_
  23.2 0.0 collective-permute-done.1.refs_8_.refs_5_
  23.3 0.0 collective-permute-done.refs_7_.refs_4_
  23.3 3.5 %all-to-all-done.refs_2_ = f32[8,96,128]{2,1,0:T(8,128)S(1)} async-done(((f32[8,96,128]{2,1,0:T(8,128)}), f32[8,96,128]{2,1,0:T(8,128)S(1)}, u32[]{:S(2)}, u32[]{:S(2)}) %all-to-all-start) | async-done | bytes 393248 | tf_op jit(solution)/shard_map/all_to_all | solution.py:881
  26.8 11.8 %scatter.1 = (f32[768,128]{1,0:T(8,128)S(1)}, f32[192,128]{1,0:T(8,128)S(1)}, f32[192,128]{1,0:T(8,128)S(1)}, f32[192,128]{1,0:T(8,128)S(1)}, f32[192,128]{1,0:T(8,128)S(1)}) custom-call(f32[2,8,128]{2,1,0:T(8,128)S(1)} %pad.4.i_ref.refs_0_, f32[720,256]{1,0:T(8,128)S(1)} %scatter_own.1.refs_1_, f32[8,96,128]{2,1,0:T(8,128)S(1)} %all-to-all-done.refs_2_, ...), custom_call_target="tpu_custom_call" | custom-call | tf_op jit(solution)/shard_map/scatter/pallas_call | solution.py:652
  38.6 0.1 collective-permute-start.3
  38.6 1.6 %collective-permute-start.4 = (f32[192,128]{1,0:T(8,128)S(1)}, f32[192,128]{1,0:T(8,128)S(1)}, u32[]{:S(2)}, u32[]{:S(2)}) collective-permute-start(f32[192,128]{1,0:T(8,128)S(1)} %get-tuple-element.29), channel_id=1, source_target_pairs={{0,16},{8,24},{16,0},{24,8},{1,17},{9,25},{17,1},{25,9},{2,18},{10... | collective-permute-start | bytes 294920 | tf_op jit(solution)/shard_map/ppermute | solution.py:889
  40.2 1.4 %collective-permute-start.5 = (f32[192,128]{1,0:T(8,128)S(1)}, f32[192,128]{1,0:T(8,128)S(1)}, u32[]{:S(2)}, u32[]{:S(2)}) collective-permute-start(f32[192,128]{1,0:T(8,128)S(1)} %get-tuple-element.30), channel_id=1, source_target_pairs={{0,24},{8,0},{16,8},{24,16},{1,25},{9,1},{17,9},{25,17},{2,26},{10... | collective-permute-start | bytes 294920 | tf_op jit(solution)/shard_map/ppermute | solution.py:889
  41.6 2.2 %prepare_k.1 = (f32[8,128]{1,0:T(8,128)S(1)}, f32[6,128,128]{2,1,0:T(8,128)S(1)}, f32[6,8,128]{2,1,0:T(8,128)S(1)}, f32[4,8,128]{2,1,0:T(8,128)S(1)}) custom-call(f32[3,4,6]{2,1,0:T(4,128)S(1)} %bitcast.24, f32[2,6,128,128]{3,2,1,0:T(8,128)S(1)} %bitcast.15), custom_call_target="tpu_custom_call" | custom-call | tf_op jit(solution)/shard_map/prepare_k/pallas_call | solution.py:407
  43.8 0.0 collective-permute-done.3.refs_8_
  43.8 0.5 collective-permute-done.4.refs_9_
  44.4 0.5 collective-permute-done.5.refs_10_
  44.9 1.9 %middle.1 = (f32[768,128]{1,0:T(8,128)S(1)}, f32[8,24,128]{2,1,0:T(8,128)}) custom-call(f32[768,128]{1,0:T(8,128)S(1)} %get-tuple-element.23.refs_0_, f32[6,8,128]{2,1,0:T(8,128)S(1)} %get-tuple-element.26.refs_1_, f32[8,128]{1,0:T(8,128)S(1)} %get-tuple-element.27.refs_2_, f32[8,128]{1,0:T(8,128)S(1)} %prepare_i.1.refs_6_.refs_3_, ...), custom_call_target="tpu_custom_call" | custom-call | tf_op jit(solution)/shard_map/middle/pallas_call | solution.py:751
  46.7 3.7 %all-to-all-start.1 = ((f32[8,24,128]{2,1,0:T(8,128)}), f32[8,24,128]{2,1,0:T(8,128)S(1)}, u32[]{:S(2)}, u32[]{:S(2)}) async-start(f32[8,24,128]{2,1,0:T(8,128)} %get-tuple-element.33), calls=%async_computation.1 | async-start | bytes 196608 | tf_op jit(solution)/shard_map/all_to_all | solution.py:916
  50.4 1.1 %apply_k.1.start_ref = f32[768,128]{1,0:T(8,128)S(1)} custom-call(f32[768,128]{1,0:T(8,128)S(1)} %get-tuple-element.31.field_ref, f32[6,128,128]{2,1,0:T(8,128)S(1)} %get-tuple-element.32.map_ref), custom_call_target="tpu_custom_call" | custom-call | tf_op jit(solution)/shard_map/apply_k/pallas_call | solution.py:784
  51.5 6.4 %all-to-all-done.1.got_ref = f32[8,24,128]{2,1,0:T(8,128)S(1)} async-done(((f32[8,24,128]{2,1,0:T(8,128)}), f32[8,24,128]{2,1,0:T(8,128)S(1)}, u32[]{:S(2)}, u32[]{:S(2)}) %all-to-all-start.1) | async-done | bytes 98336 | tf_op jit(solution)/shard_map/all_to_all | solution.py:916
  57.9 1.4 %finish.1 = f32[6,15,8,128]{3,2,1,0:T(8,128)} custom-call(f32[768,128]{1,0:T(8,128)S(1)} %apply_k.1.start_ref, f32[8,24,128]{2,1,0:T(8,128)S(1)} %all-to-all-done.1.got_ref, f32[4,8,128]{2,1,0:T(8,128)S(1)} %get-tuple-element.34.carry_ref), custom_call_target="tpu_custom_call" | custom-call | tf_op jit(solution)/shard_map/finish/pallas_call | solution.py:851
  (8 shorter events, 0.0 us)
Async XLA Ops:
  7.6 8.4 %copy-start.6 = (f32[1,2,6,8,8]{4,3,2,1,0:T(8,128)S(1)}, f32[1,2,6,8,8]{4,3,2,1,0:T(8,128)}, u32[]{:S(2)}) copy-start(f32[1,2,6,8,8]{4,3,2,1,0:T(8,128)} %param.11) | copy-start | bytes 9220
  7.7 11.8 %copy-start.1 = (f32[1,1,3,8,2048]{4,3,2,1,0:T(8,128)S(1)}, f32[1,1,3,8,2048]{4,3,2,1,0:T(8,128)}, u32[]{:S(2)}) copy-start(f32[1,1,3,8,2048]{4,3,2,1,0:T(8,128)} %param.17) | copy-start | bytes 589828
  7.7 11.8 %copy-start.4 = (s32[1,1,8,2048]{3,2,1,0:T(8,128)S(1)}, s32[1,1,8,2048]{3,2,1,0:T(8,128)}, u32[]{:S(2)}) copy-start(s32[1,1,8,2048]{3,2,1,0:T(8,128)} %param.14) | copy-start | bytes 196612
  7.7 19.1 %all-to-all-start = ((f32[8,96,128]{2,1,0:T(8,128)}), f32[8,96,128]{2,1,0:T(8,128)S(1)}, u32[]{:S(2)}, u32[]{:S(2)}) async-start(f32[8,96,128]{2,1,0:T(8,128)} %get-tuple-element.22), calls=%async_computation | async-start | bytes 786432 | tf_op jit(solution)/shard_map/all_to_all | solution.py:881
  16.0 3.4 %copy-start.3 = (s32[1,1,8,2048]{3,2,1,0:T(8,128)S(1)}, s32[1,1,8,2048]{3,2,1,0:T(8,128)}, u32[]{:S(2)}) copy-start(s32[1,1,8,2048]{3,2,1,0:T(8,128)} %param.16) | copy-start | bytes 196612
  16.1 0.7 %copy-start.5 = (f32[1,1,4,3,6]{4,2,3,1,0:T(4,128)S(1)}, f32[1,1,4,3,6]{4,2,3,1,0:T(4,128)}, u32[]{:S(2)}) copy-start(f32[1,1,4,3,6]{4,2,3,1,0:T(4,128)} %param.13) | copy-start | bytes 868
  17.6 5.6 %collective-permute-start.2 = (f32[8,128]{1,0:T(8,128)S(1)}, f32[8,128]{1,0:T(8,128)S(1)}, u32[]{:S(2)}, u32[]{:S(2)}) collective-permute-start(f32[8,128]{1,0:T(8,128)S(1)} %prepare_i.1.refs_6_.refs_3_), channel_id=1, source_target_pairs={{0,24},{8,0},{16,8},{24,16},{1,25},{9,1},{17,9},{25,17},{2,26},{10... | collective-permute-start | bytes 12296 | tf_op jit(solution)/shard_map/ppermute | solution.py:889
  17.7 5.6 %collective-permute-start.1 = (f32[8,128]{1,0:T(8,128)S(1)}, f32[8,128]{1,0:T(8,128)S(1)}, u32[]{:S(2)}, u32[]{:S(2)}) collective-permute-start(f32[8,128]{1,0:T(8,128)S(1)} %prepare_i.1.refs_6_.refs_3_), channel_id=1, source_target_pairs={{0,16},{8,24},{16,0},{24,8},{1,17},{9,25},{17,1},{25,9},{2,18},{10... | collective-permute-start | bytes 12296 | tf_op jit(solution)/shard_map/ppermute | solution.py:889
  19.3 4.0 %collective-permute-start = (f32[8,128]{1,0:T(8,128)S(1)}, f32[8,128]{1,0:T(8,128)S(1)}, u32[]{:S(2)}, u32[]{:S(2)}) collective-permute-start(f32[8,128]{1,0:T(8,128)S(1)} %prepare_i.1.refs_6_.refs_3_), channel_id=1, source_target_pairs={{0,8},{8,16},{16,24},{24,0},{1,9},{9,17},{17,25},{25,1},{2,10},{10... | collective-permute-start | bytes 12296 | tf_op jit(solution)/shard_map/ppermute | solution.py:889
  19.4 7.4 %copy-start.2 = (f32[6,8,15,128]{3,1,2,0:T(8,128)S(1)}, f32[6,8,15,128]{3,1,2,0:T(8,128)}, u32[]{:S(2)}) copy-start(f32[6,8,15,128]{3,1,2,0:T(8,128)} %param.9) | copy-start | bytes 1105924
  26.8 14.8 %copy-start = (f32[1,2,6,128,128]{4,3,2,1,0:T(8,128)S(1)}, f32[1,2,6,128,128]{4,3,2,1,0:T(8,128)}, u32[]{:S(2)}) copy-start(f32[1,2,6,128,128]{4,3,2,1,0:T(8,128)} %param.12) | copy-start | bytes 2359300
  38.6 5.3 %collective-permute-start.3 = (f32[192,128]{1,0:T(8,128)S(1)}, f32[192,128]{1,0:T(8,128)S(1)}, u32[]{:S(2)}, u32[]{:S(2)}) collective-permute-start(f32[192,128]{1,0:T(8,128)S(1)} %get-tuple-element.28), channel_id=1, source_target_pairs={{0,8},{8,16},{16,24},{24,0},{1,9},{9,17},{17,25},{25,1},{2,10},{10... | collective-permute-start | bytes 294920 | tf_op jit(solution)/shard_map/ppermute | solution.py:889
  38.6 5.7 %collective-permute-start.4 = (f32[192,128]{1,0:T(8,128)S(1)}, f32[192,128]{1,0:T(8,128)S(1)}, u32[]{:S(2)}, u32[]{:S(2)}) collective-permute-start(f32[192,128]{1,0:T(8,128)S(1)} %get-tuple-element.29), channel_id=1, source_target_pairs={{0,16},{8,24},{16,0},{24,8},{1,17},{9,25},{17,1},{25,9},{2,18},{10... | collective-permute-start | bytes 294920 | tf_op jit(solution)/shard_map/ppermute | solution.py:889
  40.2 4.6 %collective-permute-start.5 = (f32[192,128]{1,0:T(8,128)S(1)}, f32[192,128]{1,0:T(8,128)S(1)}, u32[]{:S(2)}, u32[]{:S(2)}) collective-permute-start(f32[192,128]{1,0:T(8,128)S(1)} %get-tuple-element.30), channel_id=1, source_target_pairs={{0,24},{8,0},{16,8},{24,16},{1,25},{9,1},{17,9},{25,17},{2,26},{10... | collective-permute-start | bytes 294920 | tf_op jit(solution)/shard_map/ppermute | solution.py:889
  46.7 11.1 %all-to-all-start.1 = ((f32[8,24,128]{2,1,0:T(8,128)}), f32[8,24,128]{2,1,0:T(8,128)S(1)}, u32[]{:S(2)}, u32[]{:S(2)}) async-start(f32[8,24,128]{2,1,0:T(8,128)} %get-tuple-element.33), calls=%async_computation.1 | async-start | bytes 196608 | tf_op jit(solution)/shard_map/all_to_all | solution.py:916

commit v10 on v9

--- a/solution.py
+++ b/solution.py
@@ -174,7 +174,8 @@
     mine = lax.axis_index("block")
 
     def send(d):
-        return pltpu.make_async_copy(out_ref.at[d], out_hbm.at[d], out_sem.at[d])
+        part = out_ref.at[d, pl.ds(0, out_hbm.shape[1])]
+        return pltpu.make_async_copy(part, out_hbm.at[d], out_sem.at[d])
 
     out_ref[...] = jnp.zeros(out_ref.shape, F32)
     send(mine).start()
@@ -283,7 +284,7 @@
         scratch_shapes=[
             pltpu.VMEM(cell.shape, jnp.int32),
             pltpu.VMEM(field.shape, F32),
-            pltpu.VMEM(out, F32),
+            pltpu.VMEM((out[0], out[1] + 8, LANES), F32),
             pltpu.VMEM((2 * LANES, LANES), BF16),
             pltpu.VMEM((2 * LANES, group * chunk), BF16),
             pltpu.VMEM((table[0], group * chunk), F32),
@@ -477,14 +478,12 @@
     along_k = jnp.concatenate(along_k, axis=0)
     blocks = []
     for f in range(fields):
-        value = jnp.concatenate(
-            [
-                value_of(f, b, at // LANES + q)
-                for b, at in units
-                for q in range(size // LANES)
-            ],
-            axis=1,
-        )
+        rows = []
+        for b, at in units:
+            for q in range(0, size // LANES, 8):
+                block = value_of(f, b, lax.div(at, LANES) + q)
+                rows += [block[r : r + 1] for r in range(8)]
+        value = jnp.concatenate(rows, axis=1)
         scaled = along_j * value
         blocks += [along_i * scaled[q : q + 1] for q in range(cells_j)]
     high, low = split(jnp.concatenate(blocks, axis=0))
@@ -532,7 +531,7 @@
     spread_slots(
         total_ref,
         place_ref,
-        lambda f, b, q: got_ref[pl.ds(f * slot_rows + q, 1), :],
+        lambda f, b, q: got_ref[pl.ds(pl.multiple_of(f * slot_rows + q, 8), 8), :],
         cell_ref,
         weight_ref,
         [(mine, 0)],
@@ -551,7 +550,7 @@
         in_specs=[smem] + [vmem] * 5,
         out_specs=vmem,
         scratch_shapes=[
-            pltpu.VMEM((fields * cell.shape[1] // LANES, LANES), F32),
+            pltpu.VMEM((fields * cell.shape[1] // LANES + 8, LANES), F32),
             pltpu.VMEM((2 * LANES, LANES), BF16),
             pltpu.VMEM((2 * LANES, gather_chunk), BF16),
             pltpu.VMEM((tables[0].shape[0], gather_chunk), F32),
@@ -561,14 +560,14 @@
     )(far(count), *map(near, (*tables, receptor, cell, weight)))
 
 
-def scatter_kernel(*refs, peers, chunk, base):
+def scatter_kernel(*refs, peers, chunk, base, sizes):
     factor_ref, begun_ref, got_ref, cell_ref, weight_ref, residual_ref = refs[:6]
     refs = refs[6:]
     tile_refs = refs[:peers]
     start_ref = refs[peers]
     send_refs = refs[1 + peers : 1 + 2 * peers]
     total_ref, place_ref, fold_ref, solve_ref, solve_sem = refs[1 + 2 * peers :]
-    fields, cells_j, cells_i, _ = residual_ref.shape
+    fields, cells_j, cells_i = sizes
     sources, capacity = cell_ref.shape
     rows_j = 16
     slot_rows = capacity // LANES
@@ -592,7 +591,7 @@
         spread_slots(
             total_ref,
             place_ref,
-            lambda f, b, q: got_ref[b, pl.ds(f * slot_rows + q, 1), :],
+            lambda f, b, q: got_ref[b, pl.ds(pl.multiple_of(f * slot_rows + q, 8), 8), :],
             cell_ref,
             weight_ref,
             units,
@@ -603,7 +602,8 @@
 
     lax.fori_loop(0, count // group, step_body, 0)
 
-    fold_ref[...] = total_ref[:, :LANES] + total_ref[:, LANES:]
+    count = fields * cells_j * cells_i
+    fold_ref[:count] = total_ref[:, :LANES] + total_ref[:, LANES:] + residual_ref[...]
     solve_load.wait()
     mine = lax.axis_index("line")
     tiles = [ref[...] for ref in tile_refs]
@@ -614,7 +614,7 @@
         data = []
         for i in range(cells_i):
             at = pl.ds(f * cells_i * cells_j + i, cells_j, stride=cells_i)
-            data.append(jnp.concatenate([fold_ref[at, :] + residual_ref[f, :, i, :], pad], axis=0))
+            data.append(jnp.concatenate([fold_ref[at, :], pad], axis=0))
 
         def solve(direction, columns):
             result = []
@@ -650,7 +650,13 @@
     vmem = pl.BlockSpec(memory_space=pltpu.VMEM)
     smem = pl.BlockSpec(memory_space=pltpu.SMEM)
     return pl.pallas_call(
-        functools.partial(scatter_kernel, peers=peers, chunk=chunk, base=base),
+        functools.partial(
+            scatter_kernel,
+            peers=peers,
+            chunk=chunk,
+            base=base,
+            sizes=(fields, cells_j, cells_i),
+        ),
         out_shape=(pltpu.VMEM((rows, LANES), F32),)
         + (pltpu.VMEM((2 * fields * 16, LANES), F32),) * peers,
         in_specs=[vmem] * (6 + peers),
@@ -658,13 +664,13 @@
         scratch_shapes=[
             pltpu.VMEM((fields * cells_i * cells_j, 2 * LANES), F32),
             pltpu.VMEM((LANES, LANES), BF16),
-            pltpu.VMEM((fields * cells_i * cells_j, LANES), F32),
+            pltpu.VMEM((fields * cells_i * cells_j + 8 * cells_i, LANES), F32),
             pltpu.SMEM(solve_tiles.shape, F32),
             pltpu.SemaphoreType.DMA(()),
         ],
         compiler_params=PARAMS,
         name="scatter",
-    )(*map(near, (solve_tiles, begun, got, cell, weight, residual, *tiles)))
+    )(*map(near, (solve_tiles, begun, got, cell, weight, residual.reshape(-1, LANES), *tiles)))
 
 
 def middle_kernel(*refs, peers, base, fields, cells_i):
@@ -735,7 +741,9 @@
             part = jnp.where(lane == rows_j * q + rows_j - 1, entry, part)
         end_ref[a * fields : (a + 1) * fields] = part
     sends = [
-        pltpu.make_async_copy(end_ref, send_hbm.at[d], send_sem.at[d])
+        pltpu.make_async_copy(
+            end_ref.at[pl.ds(0, 4 * fields)], send_hbm.at[d], send_sem.at[d]
+        )
         for d in range(send_hbm.shape[0])
     ]
     for copy in sends:
@@ -757,7 +765,7 @@
         in_specs=[vmem] * (3 + 2 * peers),
         out_specs=(vmem, pl.BlockSpec(memory_space=pltpu.HBM)),
         scratch_shapes=[
-            pltpu.VMEM((4 * fields, LANES), F32),
+            pltpu.VMEM((4 * fields + 8, LANES), F32),
             pltpu.SMEM((8, LANES), F32),
             pltpu.SemaphoreType.DMA(()),
             pltpu.SemaphoreType.DMA((owners,)),
@@ -792,10 +800,15 @@
 
 
 def finish_kernel(start_ref, got_ref, carry_ref, out_hbm, out_ref, out_sem):
-    fields, cells_j, cells_i, _ = out_ref.shape
+    fields, cells_j, cells_i, _ = out_hbm.shape
     rows_j = 16
     rows = cells_i * rows_j
     blocks = got_ref.shape[0]
+
+    def send(f):
+        part = out_ref.at[f, pl.ds(0, cells_j)]
+        return pltpu.make_async_copy(part, out_hbm.at[f], out_sem.at[f])
+
     mine = lax.axis_index("block")
     zero = jnp.zeros((fields, LANES), F32)
     part = [
@@ -839,10 +852,10 @@
         change = dot3(dot_tn, carried, response, 0, 0)
         value = start_ref[f * rows : (f + 1) * rows] - change
         for i in range(cells_i):
-            out_ref[f, :, i, :] = value[i * rows_j : i * rows_j + cells_j]
-        pltpu.make_async_copy(out_ref.at[f], out_hbm.at[f], out_sem.at[f]).start()
+            out_ref[f, :, i, :] = value[i * rows_j : (i + 1) * rows_j]
+        send(f).start()
     for f in range(fields):
-        pltpu.make_async_copy(out_ref.at[f], out_hbm.at[f], out_sem.at[f]).wait()
+        send(f).wait()
 
 
 def finish(start, got, carry, shape):
@@ -853,7 +866,10 @@
         out_shape=jax.ShapeDtypeStruct(shape, F32),
         in_specs=[vmem, vmem, vmem],
         out_specs=pl.BlockSpec(memory_space=pltpu.HBM),
-        scratch_shapes=[pltpu.VMEM(shape, F32), pltpu.SemaphoreType.DMA((shape[0],))],
+        scratch_shapes=[
+            pltpu.VMEM((shape[0], 16) + shape[2:], F32),
+            pltpu.SemaphoreType.DMA((shape[0],)),
+        ],
         compiler_params=PARAMS,
         name="finish",
     )(near(start), near(got), near(carry))

time: 59.8 us -> 59.2 us (0.990)
  starting transfers between devices: 16.8 us -> 16 us
    all_to_all x1, starting transfers between devices: 8.32 us -> 6.55 us  [per_device(): lax.all_to_all(outgoing, 'block', split_axis=0, concat_axis=0, tiled=True)]
    ppermute x6, starting transfers between devices: 4.83 us -> 5.78 us  [shifted(): lax.ppermute(value, 'line', [(s, (s + shift) % peers) for s in range(peer...]
  transfers between devices with their start and end apart: 8 -> 8, of which waited for: 4 -> 4; matrix products, arithmetic and copies ran while one was open for 0% -> 0% of each run, Pallas kernels for 13% -> 14%
where the time goes in v10:
time: 59.2 us; the launch traced here: 58.4 us
  Pallas kernels  30.4 us (51%)
  starting transfers between devices  16 us (27%)
  waiting for transfers between devices  10.8 us (18%)
  local copies, waits for them, and re-layouts  0.79 us (1%)
    pallas_call x1, Pallas kernels, scatter(): pl.pallas_call(functools.partial(scatter_kernel, peers=peers, chunk=chunk...  11.6 us
    pallas_call x1, Pallas kernels, gather(): pl.pallas_call(functools.partial(gather_kernel, chunk=chunk, group=group,...  7.68 us
    all_to_all x1, starting transfers between devices, per_device(): lax.all_to_all(outgoing, 'block', split_axis=0, concat_axis=0, tiled=True)  6.55 us
    all_to_all x1, waiting for transfers between devices, per_device(): lax.all_to_all(message, 'block', split_axis=0, concat_axis=0, tiled=True)  6.29 us
    ppermute x6, starting transfers between devices, shifted(): lax.ppermute(value, 'line', [(s, (s + shift) % peers) for s in range(peer...  5.78 us
    pallas_call x1, Pallas kernels, scatter_own(): pl.pallas_call(functools.partial(scatter_own_kernel, sizes=sizes, gather_...  3.79 us
    all_to_all x1, starting transfers between devices, per_device(): lax.all_to_all(message, 'block', split_axis=0, concat_axis=0, tiled=True)  3.69 us
    all_to_all x1, waiting for transfers between devices, per_device(): lax.all_to_all(outgoing, 'block', split_axis=0, concat_axis=0, tiled=True)  3.48 us
  transfers between devices with their start and end apart: 8, of which 4 were waited for; matrix products, arithmetic and copies ran while one was open for 0% of the time, Pallas kernels for 14%

profile of v10, /device:TPU:0, one launch (start us, length us, event | category | flops | bytes accessed | tf_op | source)
XLA Modules:
  0.0 58.4 jit_solution(7889743420860567074)
XLA Ops:
  0.0 7.7 %gather.1 = (f32[8,96,128]{2,1,0:T(8,128)}, bf16[360,256]{1,0:T(8,128)(2,1)S(1)}, bf16[360,256]{1,0:T(8,128)(2,1)S(1)}) custom-call(s32[8]{0:T(128)} %bitcast.28, s32[8,2048]{1,0:T(8,128)} %bitcast.23, f32[720,128]{1,0:T(8,128)} %bitcast.27), custom_call_target="tpu_custom_call" | custom-call | tf_op jit(solution)/shard_map/gather/pallas_call | solution.py:273
  7.7 0.0 copy-start.6
  7.7 0.0 copy-start.1
  7.7 0.0 copy-start.4
  7.7 6.5 %all-to-all-start = ((f32[8,96,128]{2,1,0:T(8,128)}), f32[8,96,128]{2,1,0:T(8,128)S(1)}, u32[]{:S(2)}, u32[]{:S(2)}) async-start(f32[8,96,128]{2,1,0:T(8,128)} %get-tuple-element.22), calls=%async_computation | async-start | bytes 786432 | tf_op jit(solution)/shard_map/all_to_all | solution.py:897
  14.3 0.0 copy-done.6
  14.3 0.0 copy-start.3
  14.3 0.1 reshape.12
  14.4 0.0 copy-start.5
  14.4 0.7 %copy-done.5 = f32[1,1,4,3,6]{4,2,3,1,0:T(4,128)S(1)} copy-done((f32[1,1,4,3,6]{4,2,3,1,0:T(4,128)S(1)}, f32[1,1,4,3,6]{4,2,3,1,0:T(4,128)}, u32[]{:S(2)}) %copy-start.5) | copy-done | bytes 312
  15.1 0.8 %prepare_i.1.refs_6_.refs_3_ = f32[8,128]{1,0:T(8,128)S(1)} custom-call(f32[3,4,6]{2,1,0:T(4,128)S(1)} %bitcast.25, f32[2,8,128]{2,1,0:T(8,128)S(1)} %pad.4.i_ref.refs_0_), custom_call_target="tpu_custom_call" | custom-call | tf_op jit(solution)/shard_map/prepare_i/pallas_call | solution.py:355
  15.9 0.7 %collective-permute-start.2 = (f32[8,128]{1,0:T(8,128)S(1)}, f32[8,128]{1,0:T(8,128)S(1)}, u32[]{:S(2)}, u32[]{:S(2)}) collective-permute-start(f32[8,128]{1,0:T(8,128)S(1)} %prepare_i.1.refs_6_.refs_3_), channel_id=1, source_target_pairs={{0,24},{8,0},{16,8},{24,16},{1,25},{9,1},{17,9},{25,17},{2,26},{10... | collective-permute-start | bytes 12296 | tf_op jit(solution)/shard_map/ppermute | solution.py:905
  16.6 1.8 %collective-permute-start.1 = (f32[8,128]{1,0:T(8,128)S(1)}, f32[8,128]{1,0:T(8,128)S(1)}, u32[]{:S(2)}, u32[]{:S(2)}) collective-permute-start(f32[8,128]{1,0:T(8,128)S(1)} %prepare_i.1.refs_6_.refs_3_), channel_id=1, source_target_pairs={{0,16},{8,24},{16,0},{24,8},{1,17},{9,25},{17,1},{25,9},{2,18},{10... | collective-permute-start | bytes 12296 | tf_op jit(solution)/shard_map/ppermute | solution.py:905
  18.5 0.2 collective-permute-start
  18.6 3.8 %scatter_own.1.refs_1_ = f32[720,256]{1,0:T(8,128)S(1)} custom-call(s32[8]{0:T(128)} %bitcast.29, bf16[360,256]{1,0:T(8,128)(2,1)S(1)} %get-tuple-element.20.high_ref, bf16[360,256]{1,0:T(8,128)(2,1)S(1)} %get-tuple-element.21.low_ref, s32[8,2048]{1,0:T(8,128)S(1)} %bitcast.24, s32[8,2048]{1,0:T(8,128)S(1)} %bitcast.21, f32[3,8,2048]{2,1,0:T(8,128)S(1)} %bitcast.18), custom_call_target="tpu_custom_call" | custom-call | tf_op jit(solution)/shard_map/scatter_own/pallas_call | solution.py:547
  22.4 0.0 collective-permute-done.2.refs_9_.refs_6_
  22.4 0.0 collective-permute-done.1.refs_8_.refs_5_
  22.4 0.0 collective-permute-done.refs_7_.refs_4_
  22.5 3.5 %all-to-all-done.refs_2_ = f32[8,96,128]{2,1,0:T(8,128)S(1)} async-done(((f32[8,96,128]{2,1,0:T(8,128)}), f32[8,96,128]{2,1,0:T(8,128)S(1)}, u32[]{:S(2)}, u32[]{:S(2)}) %all-to-all-start) | async-done | bytes 393248 | tf_op jit(solution)/shard_map/all_to_all | solution.py:897
  25.9 11.6 %scatter.1 = (f32[768,128]{1,0:T(8,128)S(1)}, f32[192,128]{1,0:T(8,128)S(1)}, f32[192,128]{1,0:T(8,128)S(1)}, f32[192,128]{1,0:T(8,128)S(1)}, f32[192,128]{1,0:T(8,128)S(1)}) custom-call(f32[2,8,128]{2,1,0:T(8,128)S(1)} %pad.4.i_ref.refs_0_, f32[720,256]{1,0:T(8,128)S(1)} %scatter_own.1.refs_1_, f32[8,96,128]{2,1,0:T(8,128)S(1)} %all-to-all-done.refs_2_, ...), custom_call_target="tpu_custom_call" | custom-call | tf_op jit(solution)/shard_map/scatter/pallas_call | solution.py:652
  37.5 0.1 collective-permute-start.3
  37.6 1.6 %collective-permute-start.4 = (f32[192,128]{1,0:T(8,128)S(1)}, f32[192,128]{1,0:T(8,128)S(1)}, u32[]{:S(2)}, u32[]{:S(2)}) collective-permute-start(f32[192,128]{1,0:T(8,128)S(1)} %get-tuple-element.29), channel_id=1, source_target_pairs={{0,16},{8,24},{16,0},{24,8},{1,17},{9,25},{17,1},{25,9},{2,18},{10... | collective-permute-start | bytes 294920 | tf_op jit(solution)/shard_map/ppermute | solution.py:905
  39.2 1.4 %collective-permute-start.5 = (f32[192,128]{1,0:T(8,128)S(1)}, f32[192,128]{1,0:T(8,128)S(1)}, u32[]{:S(2)}, u32[]{:S(2)}) collective-permute-start(f32[192,128]{1,0:T(8,128)S(1)} %get-tuple-element.30), channel_id=1, source_target_pairs={{0,24},{8,0},{16,8},{24,16},{1,25},{9,1},{17,9},{25,17},{2,26},{10... | collective-permute-start | bytes 294920 | tf_op jit(solution)/shard_map/ppermute | solution.py:905
  40.6 2.2 %prepare_k.1 = (f32[8,128]{1,0:T(8,128)S(1)}, f32[6,128,128]{2,1,0:T(8,128)S(1)}, f32[6,8,128]{2,1,0:T(8,128)S(1)}, f32[4,8,128]{2,1,0:T(8,128)S(1)}) custom-call(f32[3,4,6]{2,1,0:T(4,128)S(1)} %bitcast.26, f32[2,6,128,128]{3,2,1,0:T(8,128)S(1)} %bitcast.17), custom_call_target="tpu_custom_call" | custom-call | tf_op jit(solution)/shard_map/prepare_k/pallas_call | solution.py:408
  42.8 0.0 collective-permute-done.3.refs_8_
  42.8 0.5 collective-permute-done.4.refs_9_
  43.3 0.5 collective-permute-done.5.refs_10_
  43.8 1.9 %middle.1 = (f32[768,128]{1,0:T(8,128)S(1)}, f32[8,24,128]{2,1,0:T(8,128)}) custom-call(f32[768,128]{1,0:T(8,128)S(1)} %get-tuple-element.23.refs_0_, f32[6,8,128]{2,1,0:T(8,128)S(1)} %get-tuple-element.26.refs_1_, f32[8,128]{1,0:T(8,128)S(1)} %get-tuple-element.27.refs_2_, f32[8,128]{1,0:T(8,128)S(1)} %prepare_i.1.refs_6_.refs_3_, ...), custom_call_target="tpu_custom_call" | custom-call | tf_op jit(solution)/shard_map/middle/pallas_call | solution.py:759
  45.7 3.7 %all-to-all-start.1 = ((f32[8,24,128]{2,1,0:T(8,128)}), f32[8,24,128]{2,1,0:T(8,128)S(1)}, u32[]{:S(2)}, u32[]{:S(2)}) async-start(f32[8,24,128]{2,1,0:T(8,128)} %get-tuple-element.33), calls=%async_computation.1 | async-start | bytes 196608 | tf_op jit(solution)/shard_map/all_to_all | solution.py:932
  49.4 1.1 %apply_k.1.start_ref = f32[768,128]{1,0:T(8,128)S(1)} custom-call(f32[768,128]{1,0:T(8,128)S(1)} %get-tuple-element.31.field_ref, f32[6,128,128]{2,1,0:T(8,128)S(1)} %get-tuple-element.32.map_ref), custom_call_target="tpu_custom_call" | custom-call | tf_op jit(solution)/shard_map/apply_k/pallas_call | solution.py:792
  50.5 6.3 %all-to-all-done.1.got_ref = f32[8,24,128]{2,1,0:T(8,128)S(1)} async-done(((f32[8,24,128]{2,1,0:T(8,128)}), f32[8,24,128]{2,1,0:T(8,128)S(1)}, u32[]{:S(2)}, u32[]{:S(2)}) %all-to-all-start.1) | async-done | bytes 98336 | tf_op jit(solution)/shard_map/all_to_all | solution.py:932
  56.8 1.4 %finish.1 = f32[6,15,8,128]{3,2,1,0:T(8,128)} custom-call(f32[768,128]{1,0:T(8,128)S(1)} %apply_k.1.start_ref, f32[8,24,128]{2,1,0:T(8,128)S(1)} %all-to-all-done.1.got_ref, f32[4,8,128]{2,1,0:T(8,128)S(1)} %get-tuple-element.34.carry_ref), custom_call_target="tpu_custom_call" | custom-call | tf_op jit(solution)/shard_map/finish/pallas_call | solution.py:864
  (8 shorter events, 0.0 us)
Async XLA Ops:
  7.7 6.6 %copy-start.6 = (f32[1,2,6,8,8]{4,3,2,1,0:T(8,128)S(1)}, f32[1,2,6,8,8]{4,3,2,1,0:T(8,128)}, u32[]{:S(2)}) copy-start(f32[1,2,6,8,8]{4,3,2,1,0:T(8,128)} %param.11) | copy-start | bytes 9220
  7.7 10.9 %copy-start.1 = (f32[1,1,3,8,2048]{4,3,2,1,0:T(8,128)S(1)}, f32[1,1,3,8,2048]{4,3,2,1,0:T(8,128)}, u32[]{:S(2)}) copy-start(f32[1,1,3,8,2048]{4,3,2,1,0:T(8,128)} %param.17) | copy-start | bytes 589828
  7.7 10.9 %copy-start.4 = (s32[1,1,8,2048]{3,2,1,0:T(8,128)S(1)}, s32[1,1,8,2048]{3,2,1,0:T(8,128)}, u32[]{:S(2)}) copy-start(s32[1,1,8,2048]{3,2,1,0:T(8,128)} %param.14) | copy-start | bytes 196612
  7.7 18.2 %all-to-all-start = ((f32[8,96,128]{2,1,0:T(8,128)}), f32[8,96,128]{2,1,0:T(8,128)S(1)}, u32[]{:S(2)}, u32[]{:S(2)}) async-start(f32[8,96,128]{2,1,0:T(8,128)} %get-tuple-element.22), calls=%async_computation | async-start | bytes 786432 | tf_op jit(solution)/shard_map/all_to_all | solution.py:897
  14.3 4.3 %copy-start.3 = (s32[1,1,8,2048]{3,2,1,0:T(8,128)S(1)}, s32[1,1,8,2048]{3,2,1,0:T(8,128)}, u32[]{:S(2)}) copy-start(s32[1,1,8,2048]{3,2,1,0:T(8,128)} %param.16) | copy-start | bytes 196612
  14.4 0.7 %copy-start.5 = (f32[1,1,4,3,6]{4,2,3,1,0:T(4,128)S(1)}, f32[1,1,4,3,6]{4,2,3,1,0:T(4,128)}, u32[]{:S(2)}) copy-start(f32[1,1,4,3,6]{4,2,3,1,0:T(4,128)} %param.13) | copy-start | bytes 868
  15.9 6.5 %collective-permute-start.2 = (f32[8,128]{1,0:T(8,128)S(1)}, f32[8,128]{1,0:T(8,128)S(1)}, u32[]{:S(2)}, u32[]{:S(2)}) collective-permute-start(f32[8,128]{1,0:T(8,128)S(1)} %prepare_i.1.refs_6_.refs_3_), channel_id=1, source_target_pairs={{0,24},{8,0},{16,8},{24,16},{1,25},{9,1},{17,9},{25,17},{2,26},{10... | collective-permute-start | bytes 12296 | tf_op jit(solution)/shard_map/ppermute | solution.py:905
  16.6 5.8 %collective-permute-start.1 = (f32[8,128]{1,0:T(8,128)S(1)}, f32[8,128]{1,0:T(8,128)S(1)}, u32[]{:S(2)}, u32[]{:S(2)}) collective-permute-start(f32[8,128]{1,0:T(8,128)S(1)} %prepare_i.1.refs_6_.refs_3_), channel_id=1, source_target_pairs={{0,16},{8,24},{16,0},{24,8},{1,17},{9,25},{17,1},{25,9},{2,18},{10... | collective-permute-start | bytes 12296 | tf_op jit(solution)/shard_map/ppermute | solution.py:905
  18.5 4.0 %collective-permute-start = (f32[8,128]{1,0:T(8,128)S(1)}, f32[8,128]{1,0:T(8,128)S(1)}, u32[]{:S(2)}, u32[]{:S(2)}) collective-permute-start(f32[8,128]{1,0:T(8,128)S(1)} %prepare_i.1.refs_6_.refs_3_), channel_id=1, source_target_pairs={{0,8},{8,16},{16,24},{24,0},{1,9},{9,17},{17,25},{25,1},{2,10},{10... | collective-permute-start | bytes 12296 | tf_op jit(solution)/shard_map/ppermute | solution.py:905
  18.6 7.3 %copy-start.2 = (f32[6,8,15,128]{3,1,2,0:T(8,128)S(1)}, f32[6,8,15,128]{3,1,2,0:T(8,128)}, u32[]{:S(2)}) copy-start(f32[6,8,15,128]{3,1,2,0:T(8,128)} %param.9) | copy-start | bytes 1105924
  25.9 14.7 %copy-start = (f32[1,2,6,128,128]{4,3,2,1,0:T(8,128)S(1)}, f32[1,2,6,128,128]{4,3,2,1,0:T(8,128)}, u32[]{:S(2)}) copy-start(f32[1,2,6,128,128]{4,3,2,1,0:T(8,128)} %param.12) | copy-start | bytes 2359300
  37.5 5.3 %collective-permute-start.3 = (f32[192,128]{1,0:T(8,128)S(1)}, f32[192,128]{1,0:T(8,128)S(1)}, u32[]{:S(2)}, u32[]{:S(2)}) collective-permute-start(f32[192,128]{1,0:T(8,128)S(1)} %get-tuple-element.28), channel_id=1, source_target_pairs={{0,8},{8,16},{16,24},{24,0},{1,9},{9,17},{17,25},{25,1},{2,10},{10... | collective-permute-start | bytes 294920 | tf_op jit(solution)/shard_map/ppermute | solution.py:905
  37.6 5.7 %collective-permute-start.4 = (f32[192,128]{1,0:T(8,128)S(1)}, f32[192,128]{1,0:T(8,128)S(1)}, u32[]{:S(2)}, u32[]{:S(2)}) collective-permute-start(f32[192,128]{1,0:T(8,128)S(1)} %get-tuple-element.29), channel_id=1, source_target_pairs={{0,16},{8,24},{16,0},{24,8},{1,17},{9,25},{17,1},{25,9},{2,18},{10... | collective-permute-start | bytes 294920 | tf_op jit(solution)/shard_map/ppermute | solution.py:905
  39.2 4.6 %collective-permute-start.5 = (f32[192,128]{1,0:T(8,128)S(1)}, f32[192,128]{1,0:T(8,128)S(1)}, u32[]{:S(2)}, u32[]{:S(2)}) collective-permute-start(f32[192,128]{1,0:T(8,128)S(1)} %get-tuple-element.30), channel_id=1, source_target_pairs={{0,24},{8,0},{16,8},{24,16},{1,25},{9,1},{17,9},{25,17},{2,26},{10... | collective-permute-start | bytes 294920 | tf_op jit(solution)/shard_map/ppermute | solution.py:905
  45.7 11.1 %all-to-all-start.1 = ((f32[8,24,128]{2,1,0:T(8,128)}), f32[8,24,128]{2,1,0:T(8,128)S(1)}, u32[]{:S(2)}, u32[]{:S(2)}) async-start(f32[8,24,128]{2,1,0:T(8,128)} %get-tuple-element.33), calls=%async_computation.1 | async-start | bytes 196608 | tf_op jit(solution)/shard_map/all_to_all | solution.py:932

commit v11 on v10

--- a/solution.py
+++ b/solution.py
@@ -905,6 +905,9 @@
         return lax.ppermute(value, "line", [(s, (s + shift) % peers) for s in range(peers)])
 
     tiles = [own] + [shifted(own, m) for m in range(1, peers)]
+    k_couple, _ = lax.optimization_barrier((couple, outgoing))
+    k_tile, k_map, k_rows, k_carry = prepare_k(k_couple, k_factors[0])
+    counts, _ = lax.optimization_barrier((counts, k_tile))
     begun = scatter_own(
         counts,
         tables,
@@ -924,8 +927,6 @@
         base,
     )
     got = [ends[0]] + [shifted(ends[m], m) for m in range(1, peers)]
-    couple, _ = lax.optimization_barrier((couple, ends[0]))
-    k_tile, k_map, k_rows, k_carry = prepare_k(couple, k_factors[0])
     start, message = middle(
         start, k_rows, k_tile, tiles, got, base, owners, fields, cells_i
     )

time: 59.2 us -> 59.7 us (level)
  waiting for transfers between devices: 10.8 us -> 12.1 us
  Pallas kernels: 30.4 us -> 29.5 us
  starting transfers between devices: 16 us -> 16.9 us
    ppermute x6, waiting for transfers between devices: 1.04 us -> 3.26 us  [shifted(): lax.ppermute(value, 'line', [(s, (s + shift) % peers) for s in range(peer...]
    all_to_all x1, waiting for transfers between devices: 3.48 us -> 2.17 us  [per_device(): lax.all_to_all(outgoing, 'block', split_axis=0, concat_axis=0, tiled=True)]
    pallas_call x1, Pallas kernels: 7.68 us -> 6.71 us  [gather(): pl.pallas_call(functools.partial(gather_kernel, chunk=chunk, group=group,...]
    all_to_all x1, starting transfers between devices: 6.55 us -> 7.42 us  [per_device(): lax.all_to_all(outgoing, 'block', split_axis=0, concat_axis=0, tiled=True)]
  transfers between devices with their start and end apart: 8 -> 8, of which waited for: 4 -> 5; matrix products, arithmetic and copies ran while one was open for 0% -> 0% of each run, Pallas kernels for 14% -> 13%
where the time goes in v11:
time: 59.7 us; the launch traced here: 59.4 us
  Pallas kernels  29.5 us (49%)
  starting transfers between devices  16.9 us (28%)
  waiting for transfers between devices  12.1 us (20%)
  local copies, waits for them, and re-layouts  0.79 us (1%)
    pallas_call x1, Pallas kernels, scatter(): pl.pallas_call(functools.partial(scatter_kernel, peers=peers, chunk=chunk...  11.6 us
    all_to_all x1, starting transfers between devices, per_device(): lax.all_to_all(outgoing, 'block', split_axis=0, concat_axis=0, tiled=True)  7.42 us
    pallas_call x1, Pallas kernels, gather(): pl.pallas_call(functools.partial(gather_kernel, chunk=chunk, group=group,...  6.71 us
    all_to_all x1, waiting for transfers between devices, per_device(): lax.all_to_all(message, 'block', split_axis=0, concat_axis=0, tiled=True)  6.66 us
    ppermute x6, starting transfers between devices, shifted(): lax.ppermute(value, 'line', [(s, (s + shift) % peers) for s in range(peer...  5.71 us
    pallas_call x1, Pallas kernels, scatter_own(): pl.pallas_call(functools.partial(scatter_own_kernel, sizes=sizes, gather_...  3.8 us
    all_to_all x1, starting transfers between devices, per_device(): lax.all_to_all(message, 'block', split_axis=0, concat_axis=0, tiled=True)  3.76 us
    ppermute x6, waiting for transfers between devices, shifted(): lax.ppermute(value, 'line', [(s, (s + shift) % peers) for s in range(peer...  3.26 us
  transfers between devices with their start and end apart: 8, of which 5 were waited for; matrix products, arithmetic and copies ran while one was open for 0% of the time, Pallas kernels for 13%

profile of v11, /device:TPU:0, one launch (start us, length us, event | category | flops | bytes accessed | tf_op | source)
XLA Modules:
  0.0 59.4 jit_solution(536887334380577991)
XLA Ops:
  0.0 6.7 %gather.1 = (f32[8,96,128]{2,1,0:T(8,128)}, bf16[360,256]{1,0:T(8,128)(2,1)S(1)}, bf16[360,256]{1,0:T(8,128)(2,1)S(1)}) custom-call(s32[8]{0:T(128)} %bitcast.28, s32[8,2048]{1,0:T(8,128)} %bitcast.23, f32[720,128]{1,0:T(8,128)} %bitcast.27), custom_call_target="tpu_custom_call" | custom-call | tf_op jit(solution)/shard_map/gather/pallas_call | solution.py:273
  6.7 0.0 copy-start.6
  6.7 7.4 %all-to-all-start = ((f32[8,96,128]{2,1,0:T(8,128)}), f32[8,96,128]{2,1,0:T(8,128)S(1)}, u32[]{:S(2)}, u32[]{:S(2)}) async-start(f32[8,96,128]{2,1,0:T(8,128)} %get-tuple-element.21), calls=%async_computation | async-start | bytes 786432 | tf_op jit(solution)/shard_map/all_to_all | solution.py:897
  14.2 0.0 copy-done.6
  14.2 0.1 reshape.12
  14.2 0.0 copy-start.5
  14.3 0.7 %copy-done.5 = f32[1,1,4,3,6]{4,2,3,1,0:T(4,128)S(1)} copy-done((f32[1,1,4,3,6]{4,2,3,1,0:T(4,128)S(1)}, f32[1,1,4,3,6]{4,2,3,1,0:T(4,128)}, u32[]{:S(2)}) %copy-start.5) | copy-done | bytes 312
  14.9 0.8 %prepare_i.1.refs_6_.refs_3_ = f32[8,128]{1,0:T(8,128)S(1)} custom-call(f32[3,4,6]{2,1,0:T(4,128)S(1)} %bitcast.25, f32[2,8,128]{2,1,0:T(8,128)S(1)} %pad.4.i_ref.refs_0_), custom_call_target="tpu_custom_call" | custom-call | tf_op jit(solution)/shard_map/prepare_i/pallas_call | solution.py:355
  15.8 1.6 %collective-permute-start.2 = (f32[8,128]{1,0:T(8,128)S(1)}, f32[8,128]{1,0:T(8,128)S(1)}, u32[]{:S(2)}, u32[]{:S(2)}) collective-permute-start(f32[8,128]{1,0:T(8,128)S(1)} %prepare_i.1.refs_6_.refs_3_), channel_id=1, source_target_pairs={{0,24},{8,0},{16,8},{24,16},{1,25},{9,1},{17,9},{25,17},{2,26},{10... | collective-permute-start | bytes 12296 | tf_op jit(solution)/shard_map/ppermute | solution.py:905
  17.4 0.9 %collective-permute-start.1 = (f32[8,128]{1,0:T(8,128)S(1)}, f32[8,128]{1,0:T(8,128)S(1)}, u32[]{:S(2)}, u32[]{:S(2)}) collective-permute-start(f32[8,128]{1,0:T(8,128)S(1)} %prepare_i.1.refs_6_.refs_3_), channel_id=1, source_target_pairs={{0,16},{8,24},{16,0},{24,8},{1,17},{9,25},{17,1},{25,9},{2,18},{10... | collective-permute-start | bytes 12296 | tf_op jit(solution)/shard_map/ppermute | solution.py:905
  18.3 0.2 collective-permute-start
  18.4 2.2 %prepare_k.1 = (f32[8,128]{1,0:T(8,128)S(1)}, f32[6,128,128]{2,1,0:T(8,128)S(1)}, f32[6,8,128]{2,1,0:T(8,128)S(1)}, f32[4,8,128]{2,1,0:T(8,128)S(1)}) custom-call(f32[3,4,6]{2,1,0:T(4,128)S(1)} %bitcast.26, f32[2,6,128,128]{3,2,1,0:T(8,128)S(1)} %bitcast.17), custom_call_target="tpu_custom_call" | custom-call | tf_op jit(solution)/shard_map/prepare_k/pallas_call | solution.py:408
  20.7 0.0 copy-done.3
  20.7 0.0 copy-done.4
  20.7 0.0 copy-start.2
  20.7 3.8 %scatter_own.1.refs_1_ = f32[720,256]{1,0:T(8,128)S(1)} custom-call(s32[8]{0:T(128)} %bitcast.29, bf16[360,256]{1,0:T(8,128)(2,1)S(1)} %get-tuple-element.25.high_ref, bf16[360,256]{1,0:T(8,128)(2,1)S(1)} %get-tuple-element.26.low_ref, s32[8,2048]{1,0:T(8,128)S(1)} %bitcast.24, s32[8,2048]{1,0:T(8,128)S(1)} %bitcast.21, f32[3,8,2048]{2,1,0:T(8,128)S(1)} %bitcast.18), custom_call_target="tpu_custom_call" | custom-call | tf_op jit(solution)/shard_map/scatter_own/pallas_call | solution.py:547
  24.5 0.0 collective-permute-done.2.refs_9_.refs_6_
  24.5 0.0 collective-permute-done.1.refs_8_.refs_5_
  24.5 0.0 collective-permute-done.refs_7_.refs_4_
  24.5 2.2 %all-to-all-done.refs_2_ = f32[8,96,128]{2,1,0:T(8,128)S(1)} async-done(((f32[8,96,128]{2,1,0:T(8,128)}), f32[8,96,128]{2,1,0:T(8,128)S(1)}, u32[]{:S(2)}, u32[]{:S(2)}) %all-to-all-start) | async-done | bytes 393248 | tf_op jit(solution)/shard_map/all_to_all | solution.py:897
  26.7 11.6 %scatter.1 = (f32[768,128]{1,0:T(8,128)S(1)}, f32[192,128]{1,0:T(8,128)S(1)}, f32[192,128]{1,0:T(8,128)S(1)}, f32[192,128]{1,0:T(8,128)S(1)}, f32[192,128]{1,0:T(8,128)S(1)}) custom-call(f32[2,8,128]{2,1,0:T(8,128)S(1)} %pad.4.i_ref.refs_0_, f32[720,256]{1,0:T(8,128)S(1)} %scatter_own.1.refs_1_, f32[8,96,128]{2,1,0:T(8,128)S(1)} %all-to-all-done.refs_2_, ...), custom_call_target="tpu_custom_call" | custom-call | tf_op jit(solution)/shard_map/scatter/pallas_call | solution.py:652
  38.3 0.1 collective-permute-start.3
  38.4 1.6 %collective-permute-start.4 = (f32[192,128]{1,0:T(8,128)S(1)}, f32[192,128]{1,0:T(8,128)S(1)}, u32[]{:S(2)}, u32[]{:S(2)}) collective-permute-start(f32[192,128]{1,0:T(8,128)S(1)} %get-tuple-element.31), channel_id=1, source_target_pairs={{0,16},{8,24},{16,0},{24,8},{1,17},{9,25},{17,1},{25,9},{2,18},{10... | collective-permute-start | bytes 294920 | tf_op jit(solution)/shard_map/ppermute | solution.py:905
  39.9 1.4 %collective-permute-start.5 = (f32[192,128]{1,0:T(8,128)S(1)}, f32[192,128]{1,0:T(8,128)S(1)}, u32[]{:S(2)}, u32[]{:S(2)}) collective-permute-start(f32[192,128]{1,0:T(8,128)S(1)} %get-tuple-element.32), channel_id=1, source_target_pairs={{0,24},{8,0},{16,8},{24,16},{1,25},{9,1},{17,9},{25,17},{2,26},{10... | collective-permute-start | bytes 294920 | tf_op jit(solution)/shard_map/ppermute | solution.py:905
  41.3 1.4 %collective-permute-done.3.refs_8_ = f32[192,128]{1,0:T(8,128)S(1)} collective-permute-done((f32[192,128]{1,0:T(8,128)S(1)}, f32[192,128]{1,0:T(8,128)S(1)}, u32[]{:S(2)}, u32[]{:S(2)}) %collective-permute-start.3) | collective-permute-done | bytes 98336 | tf_op jit(solution)/shard_map/ppermute | solution.py:905
  42.8 1.3 %collective-permute-done.4.refs_9_ = f32[192,128]{1,0:T(8,128)S(1)} collective-permute-done((f32[192,128]{1,0:T(8,128)S(1)}, f32[192,128]{1,0:T(8,128)S(1)}, u32[]{:S(2)}, u32[]{:S(2)}) %collective-permute-start.4) | collective-permute-done | bytes 98336 | tf_op jit(solution)/shard_map/ppermute | solution.py:905
  44.1 0.5 collective-permute-done.5.refs_10_
  44.6 1.9 %middle.1 = (f32[768,128]{1,0:T(8,128)S(1)}, f32[8,24,128]{2,1,0:T(8,128)}) custom-call(f32[768,128]{1,0:T(8,128)S(1)} %get-tuple-element.27.refs_0_, f32[6,8,128]{2,1,0:T(8,128)S(1)} %get-tuple-element.28.refs_1_, f32[8,128]{1,0:T(8,128)S(1)} %get-tuple-element.23.refs_2_, f32[8,128]{1,0:T(8,128)S(1)} %prepare_i.1.refs_6_.refs_3_, ...), custom_call_target="tpu_custom_call" | custom-call | tf_op jit(solution)/shard_map/middle/pallas_call | solution.py:759
  46.5 3.8 %all-to-all-start.1 = ((f32[8,24,128]{2,1,0:T(8,128)}), f32[8,24,128]{2,1,0:T(8,128)S(1)}, u32[]{:S(2)}, u32[]{:S(2)}) async-start(f32[8,24,128]{2,1,0:T(8,128)} %get-tuple-element.35), calls=%async_computation.1 | async-start | bytes 196608 | tf_op jit(solution)/shard_map/all_to_all | solution.py:933
  50.2 1.1 %apply_k.1.start_ref = f32[768,128]{1,0:T(8,128)S(1)} custom-call(f32[768,128]{1,0:T(8,128)S(1)} %get-tuple-element.33.field_ref, f32[6,128,128]{2,1,0:T(8,128)S(1)} %get-tuple-element.34.map_ref), custom_call_target="tpu_custom_call" | custom-call | tf_op jit(solution)/shard_map/apply_k/pallas_call | solution.py:792
  51.3 6.7 %all-to-all-done.1.got_ref = f32[8,24,128]{2,1,0:T(8,128)S(1)} async-done(((f32[8,24,128]{2,1,0:T(8,128)}), f32[8,24,128]{2,1,0:T(8,128)S(1)}, u32[]{:S(2)}, u32[]{:S(2)}) %all-to-all-start.1) | async-done | bytes 98336 | tf_op jit(solution)/shard_map/all_to_all | solution.py:933
  58.0 1.4 %finish.1 = f32[6,15,8,128]{3,2,1,0:T(8,128)} custom-call(f32[768,128]{1,0:T(8,128)S(1)} %apply_k.1.start_ref, f32[8,24,128]{2,1,0:T(8,128)S(1)} %all-to-all-done.1.got_ref, f32[4,8,128]{2,1,0:T(8,128)S(1)} %get-tuple-element.36.carry_ref), custom_call_target="tpu_custom_call" | custom-call | tf_op jit(solution)/shard_map/finish/pallas_call | solution.py:864
  (8 shorter events, 0.0 us)
Async XLA Ops:
  0.0 18.4 %copy-start = (f32[1,2,6,128,128]{4,3,2,1,0:T(8,128)S(1)}, f32[1,2,6,128,128]{4,3,2,1,0:T(8,128)}, u32[]{:S(2)}) copy-start(f32[1,2,6,128,128]{4,3,2,1,0:T(8,128)} %param.12) | copy-start | bytes 2359300
  6.7 7.4 %copy-start.6 = (f32[1,2,6,8,8]{4,3,2,1,0:T(8,128)S(1)}, f32[1,2,6,8,8]{4,3,2,1,0:T(8,128)}, u32[]{:S(2)}) copy-start(f32[1,2,6,8,8]{4,3,2,1,0:T(8,128)} %param.11) | copy-start | bytes 9220
  6.7 20.0 %all-to-all-start = ((f32[8,96,128]{2,1,0:T(8,128)}), f32[8,96,128]{2,1,0:T(8,128)S(1)}, u32[]{:S(2)}, u32[]{:S(2)}) async-start(f32[8,96,128]{2,1,0:T(8,128)} %get-tuple-element.21), calls=%async_computation | async-start | bytes 786432 | tf_op jit(solution)/shard_map/all_to_all | solution.py:897
  14.2 0.7 %copy-start.5 = (f32[1,1,4,3,6]{4,2,3,1,0:T(4,128)S(1)}, f32[1,1,4,3,6]{4,2,3,1,0:T(4,128)}, u32[]{:S(2)}) copy-start(f32[1,1,4,3,6]{4,2,3,1,0:T(4,128)} %param.13) | copy-start | bytes 868
  15.8 8.7 %collective-permute-start.2 = (f32[8,128]{1,0:T(8,128)S(1)}, f32[8,128]{1,0:T(8,128)S(1)}, u32[]{:S(2)}, u32[]{:S(2)}) collective-permute-start(f32[8,128]{1,0:T(8,128)S(1)} %prepare_i.1.refs_6_.refs_3_), channel_id=1, source_target_pairs={{0,24},{8,0},{16,8},{24,16},{1,25},{9,1},{17,9},{25,17},{2,26},{10... | collective-permute-start | bytes 12296 | tf_op jit(solution)/shard_map/ppermute | solution.py:905
  17.4 7.2 %collective-permute-start.1 = (f32[8,128]{1,0:T(8,128)S(1)}, f32[8,128]{1,0:T(8,128)S(1)}, u32[]{:S(2)}, u32[]{:S(2)}) collective-permute-start(f32[8,128]{1,0:T(8,128)S(1)} %prepare_i.1.refs_6_.refs_3_), channel_id=1, source_target_pairs={{0,16},{8,24},{16,0},{24,8},{1,17},{9,25},{17,1},{25,9},{2,18},{10... | collective-permute-start | bytes 12296 | tf_op jit(solution)/shard_map/ppermute | solution.py:905
  18.3 6.2 %collective-permute-start = (f32[8,128]{1,0:T(8,128)S(1)}, f32[8,128]{1,0:T(8,128)S(1)}, u32[]{:S(2)}, u32[]{:S(2)}) collective-permute-start(f32[8,128]{1,0:T(8,128)S(1)} %prepare_i.1.refs_6_.refs_3_), channel_id=1, source_target_pairs={{0,8},{8,16},{16,24},{24,0},{1,9},{9,17},{17,25},{25,1},{2,10},{10... | collective-permute-start | bytes 12296 | tf_op jit(solution)/shard_map/ppermute | solution.py:905
  18.4 2.2 %copy-start.1 = (f32[1,1,3,8,2048]{4,3,2,1,0:T(8,128)S(1)}, f32[1,1,3,8,2048]{4,3,2,1,0:T(8,128)}, u32[]{:S(2)}) copy-start(f32[1,1,3,8,2048]{4,3,2,1,0:T(8,128)} %param.17) | copy-start | bytes 589828
  18.4 2.2 %copy-start.3 = (s32[1,1,8,2048]{3,2,1,0:T(8,128)S(1)}, s32[1,1,8,2048]{3,2,1,0:T(8,128)}, u32[]{:S(2)}) copy-start(s32[1,1,8,2048]{3,2,1,0:T(8,128)} %param.16) | copy-start | bytes 196612
  18.4 2.2 %copy-start.4 = (s32[1,1,8,2048]{3,2,1,0:T(8,128)S(1)}, s32[1,1,8,2048]{3,2,1,0:T(8,128)}, u32[]{:S(2)}) copy-start(s32[1,1,8,2048]{3,2,1,0:T(8,128)} %param.14) | copy-start | bytes 196612
  20.7 6.0 %copy-start.2 = (f32[6,8,15,128]{3,1,2,0:T(8,128)S(1)}, f32[6,8,15,128]{3,1,2,0:T(8,128)}, u32[]{:S(2)}) copy-start(f32[6,8,15,128]{3,1,2,0:T(8,128)} %param.9) | copy-start | bytes 1105924
  38.3 4.5 %collective-permute-start.3 = (f32[192,128]{1,0:T(8,128)S(1)}, f32[192,128]{1,0:T(8,128)S(1)}, u32[]{:S(2)}, u32[]{:S(2)}) collective-permute-start(f32[192,128]{1,0:T(8,128)S(1)} %get-tuple-element.30), channel_id=1, source_target_pairs={{0,8},{8,16},{16,24},{24,0},{1,9},{9,17},{17,25},{25,1},{2,10},{10... | collective-permute-start | bytes 294920 | tf_op jit(solution)/shard_map/ppermute | solution.py:905
  38.4 5.7 %collective-permute-start.4 = (f32[192,128]{1,0:T(8,128)S(1)}, f32[192,128]{1,0:T(8,128)S(1)}, u32[]{:S(2)}, u32[]{:S(2)}) collective-permute-start(f32[192,128]{1,0:T(8,128)S(1)} %get-tuple-element.31), channel_id=1, source_target_pairs={{0,16},{8,24},{16,0},{24,8},{1,17},{9,25},{17,1},{25,9},{2,18},{10... | collective-permute-start | bytes 294920 | tf_op jit(solution)/shard_map/ppermute | solution.py:905
  39.9 4.6 %collective-permute-start.5 = (f32[192,128]{1,0:T(8,128)S(1)}, f32[192,128]{1,0:T(8,128)S(1)}, u32[]{:S(2)}, u32[]{:S(2)}) collective-permute-start(f32[192,128]{1,0:T(8,128)S(1)} %get-tuple-element.32), channel_id=1, source_target_pairs={{0,24},{8,0},{16,8},{24,16},{1,25},{9,1},{17,9},{25,17},{2,26},{10... | collective-permute-start | bytes 294920 | tf_op jit(solution)/shard_map/ppermute | solution.py:905
  46.5 11.5 %all-to-all-start.1 = ((f32[8,24,128]{2,1,0:T(8,128)}), f32[8,24,128]{2,1,0:T(8,128)S(1)}, u32[]{:S(2)}, u32[]{:S(2)}) async-start(f32[8,24,128]{2,1,0:T(8,128)} %get-tuple-element.35), calls=%async_computation.1 | async-start | bytes 196608 | tf_op jit(solution)/shard_map/all_to_all | solution.py:933
